TPU v7x, 32 devices: a whole 2x2x4 slice. The times are simulated.
32 devices in a mesh: dp: 8 (over y, x, core), tensor: 4 (over z).
Axes of the slice: x: 2, y: 2, z: 4, core: 2. Of those that a mesh axis runs over, the one named last changes fastest.
Arguments:
- tokens: bfloat16 [8192, 1024], P(('dp', 'tensor')), may hold values from -6 to 6
- time_embed: bfloat16 [8192, 256], P(('dp', 'tensor')), may hold values from -6 to 6
- segment_ids: int32 [8, 1024], P('dp'), may hold values from 0 to 3, as said below
- positions: int32 [8, 1024], P('dp'), may hold values from 0 to 2047, as said below
- first_gain: float32 [1024], replicated, may hold values from 0.1 to 1.9
- first_bias: float32 [1024], replicated, may hold values from -4 to 4
- second_gain: float32 [1024], replicated, may hold values from 0.1 to 1.9
- second_bias: float32 [1024], replicated, may hold values from -4 to 4
- time_weight: bfloat16 [256, 4, 1024], replicated, may hold values from -0.1875 to 0.1875
- time_bias: float32 [4, 1024], replicated, may hold values from -4 to 4
- qkv_weight: bfloat16 [1024, 3, 1024], P(None, None, 'tensor'), may hold values from -0.1875 to 0.1875
- out_weight: bfloat16 [1024, 1024], P('tensor'), may hold values from -0.75 to 0.75
- up_weight: bfloat16 [1024, 4096], P(None, 'tensor'), may hold values from -0.1875 to 0.1875
- down_weight: bfloat16 [4096, 1024], P('tensor'), may hold values from -0.09375 to 0.09375
- cotangent: bfloat16 [8192, 1024], P(('dp', 'tensor')), may hold values from -6 to 6
Outputs:
- result: bfloat16 [8192, 1024], P(('dp', 'tensor'))
- input_grad: float32 [8192, 1024], P(('dp', 'tensor'))
- first_gain_grad: float32 [1024], replicated
- first_bias_grad: float32 [1024], replicated
- second_gain_grad: float32 [1024], replicated
- second_bias_grad: float32 [1024], replicated
- time_weight_grad: float32 [256, 4, 1024], replicated
- time_bias_grad: float32 [4, 1024], replicated
- qkv_grad: float32 [1024, 3, 1024], P(None, None, 'tensor')
- out_weight_grad: float32 [1024, 1024], P('tensor')
- up_grad: float32 [1024, 4096], P(None, 'tensor')
- down_grad: float32 [4096, 1024], P('tensor')
Inputs may be any that keep to these rules, and one draw needn't show every extreme that they name: `segment_ids`: in each row of 1024 positions the ids never fall; they are 0 at the first position and 3 at the last. Within a segment the positions rise by one from each place to the next; each row's first segment starts at 0 and its last segment ends at 2047.
All inputs are finite; a program needn't handle non-finite values.
Results may differ from a plain program's by a relative error of at most 0.014.
The roundings to bfloat16 on the way count: a program that leaves them out, or rounds other values in their place, can miss the bound.
Values may be sent and summed in bfloat16 or wider, within the bound.
No kernel may reach another device: no remote copies, remote signals or barrier semaphores. Data moves between devices by JAX's collectives and lax.ppermute only.
A program may use at most 128 MiB of HBM per device.

v0:
```python
import math

import jax
import jax.numpy as jnp
from jax import lax
from jax.sharding import PartitionSpec as P

HEAD = 64


def modulated_norm(values, norm_gain, norm_bias, mod_scale, mod_shift):
    centre = values - jnp.mean(values, axis=-1, keepdims=True)
    spread = jnp.mean(centre * centre, axis=-1, keepdims=True)
    normed = centre * lax.rsqrt(spread + 1e-05)
    return (normed * norm_gain + norm_bias) * (1.0 + mod_scale) + mod_shift


def rotary_tables(position_list):
    half_size = HEAD // 2
    frequency = jnp.exp(jnp.arange(half_size, dtype=jnp.float32) * (-math.log(10000.0) / half_size))
    angles = position_list.astype(jnp.float32)[:, None] * frequency[None, :]
    return (jnp.cos(angles)[:, None, :], jnp.sin(angles)[:, None, :])


def rotate(values, cosine_table, sine_table):
    first_half = values[..., : HEAD // 2]
    second_half = values[..., HEAD // 2 :]
    return jnp.concatenate(
        [
            first_half * cosine_table - second_half * sine_table,
            second_half * cosine_table + first_half * sine_table,
        ],
        axis=-1,
    )


def unrotate(grads_in, cosine_table, sine_table):
    first_half = grads_in[..., : HEAD // 2]
    second_half = grads_in[..., HEAD // 2 :]
    return jnp.concatenate(
        [
            first_half * cosine_table + second_half * sine_table,
            second_half * cosine_table - first_half * sine_table,
        ],
        axis=-1,
    )


def gelu_exact(values):
    return jax.nn.gelu(values, approximate=False)


def masked_scores(query_block, key_rows, segment_block, segments, score_scale):
    scores = (
        jnp.einsum("qhd,khd->hqk", query_block, key_rows, preferred_element_type=jnp.float32)
        * score_scale
    )
    allowed = segment_block[:, None] == segments[None, :]
    return jnp.where(allowed[None], scores, -1e30)


def attend_row(inputs):
    query_rows, key_rows, value_rows, segments = inputs
    seq_len = query_rows.shape[0]
    block_len = min(512, seq_len)
    score_scale = 1.0 / math.sqrt(HEAD)
    outputs = []
    logsums = []
    for offset in range(0, seq_len, block_len):
        scores = masked_scores(
            query_rows[offset : offset + block_len],
            key_rows,
            segments[offset : offset + block_len],
            segments,
            score_scale,
        )
        row_peak = jnp.max(scores, axis=-1, keepdims=True)
        raised = jnp.exp(scores - row_peak)
        row_total = jnp.sum(raised, axis=-1, keepdims=True)
        attention = (raised / row_total).astype(jnp.bfloat16)
        mixed_block = jnp.einsum(
            "hqk,khd->qhd", attention, value_rows, preferred_element_type=jnp.float32
        )
        outputs.append(mixed_block.astype(jnp.bfloat16))
        logsums.append((row_peak + jnp.log(row_total))[..., 0])
    return (jnp.concatenate(outputs, axis=0), jnp.concatenate(logsums, axis=1))


def attend_back(inputs):
    query_rows, key_rows, value_rows, segments, logsum, mixed_grad = inputs
    seq_len = query_rows.shape[0]
    block_len = min(512, seq_len)
    score_scale = 1.0 / math.sqrt(HEAD)
    key_total = jnp.zeros(key_rows.shape, jnp.float32)
    value_total = jnp.zeros(value_rows.shape, jnp.float32)
    query_parts = []
    for offset in range(0, seq_len, block_len):
        query_block = query_rows[offset : offset + block_len]
        grad_block = mixed_grad[offset : offset + block_len]
        scores = masked_scores(
            query_block, key_rows, segments[offset : offset + block_len], segments, score_scale
        )
        probability = jnp.exp(scores - logsum[:, offset : offset + block_len, None])
        attention = probability.astype(jnp.bfloat16)
        value_total = value_total + jnp.einsum(
            "hqk,qhd->khd", attention, grad_block, preferred_element_type=jnp.float32
        )
        prob_grad = jnp.einsum(
            "qhd,khd->hqk", grad_block, value_rows, preferred_element_type=jnp.float32
        )
        row_dot = jnp.sum(probability * prob_grad, axis=-1, keepdims=True)
        score_grad = (probability * (prob_grad - row_dot)).astype(jnp.bfloat16)
        query_parts.append(
            jnp.einsum("hqk,khd->qhd", score_grad, key_rows, preferred_element_type=jnp.float32)
            * score_scale
        )
        key_total = (
            key_total
            + jnp.einsum(
                "hqk,qhd->khd", score_grad, query_block, preferred_element_type=jnp.float32
            )
            * score_scale
        )
    return (jnp.concatenate(query_parts, axis=0), key_total, value_total)


def local(
    tokens,
    time_embed,
    segment_ids,
    positions,
    first_gain,
    first_bias,
    second_gain,
    second_bias,
    time_weight,
    time_bias,
    qkv_weight,
    out_weight,
    up_weight,
    down_weight,
    cotangent,
):
    local_rows = tokens.shape[0]
    model_width = tokens.shape[1]
    embed_width = time_embed.shape[1]
    row_count, seq_len = segment_ids.shape
    group_rows = row_count * seq_len
    local_width = qkv_weight.shape[2]
    head_local = local_width // HEAD
    lead_pair = (((0,), (0,)), ((), ()))
    trail_pair = (((1,), (1,)), ((), ()))
    tokens_float = tokens.astype(jnp.float32)
    modulation = (
        jnp.dot(
            time_embed,
            time_weight.reshape(embed_width, 4 * model_width),
            preferred_element_type=jnp.float32,
        ).reshape(local_rows, 4, model_width)
        + time_bias
    )
    first_normed = modulated_norm(
        tokens_float, first_gain, first_bias, modulation[:, 0], modulation[:, 1]
    ).astype(jnp.bfloat16)
    first_all = lax.all_gather(first_normed, "tensor", axis=0, tiled=True)
    qkv_flat = qkv_weight.reshape(model_width, 3 * local_width)
    projected = jnp.dot(first_all, qkv_flat, preferred_element_type=jnp.float32)
    projected = projected.reshape(group_rows, 3, head_local, HEAD)
    cosine_table, sine_table = rotary_tables(positions.reshape(-1))
    row_shape = (row_count, seq_len, head_local, HEAD)
    queries = (
        rotate(projected[:, 0], cosine_table, sine_table).astype(jnp.bfloat16).reshape(row_shape)
    )
    keys_all = (
        rotate(projected[:, 1], cosine_table, sine_table).astype(jnp.bfloat16).reshape(row_shape)
    )
    values_all = projected[:, 2].astype(jnp.bfloat16).reshape(row_shape)
    mixed_heads, logsum = lax.map(attend_row, (queries, keys_all, values_all, segment_ids))
    mixed_flat = mixed_heads.reshape(group_rows, local_width)
    picked = lax.slice_in_dim(mixed_flat, 0, lax.axis_size("tensor") * local_rows, axis=0)
    attended = lax.psum_scatter(
        jnp.dot(picked, out_weight, preferred_element_type=jnp.float32),
        "tensor",
        scatter_dimension=0,
        tiled=True,
    )
    residual = tokens_float + attended
    second_normed = modulated_norm(
        residual, second_gain, second_bias, modulation[:, 2], modulation[:, 3]
    ).astype(jnp.bfloat16)
    second_all = lax.all_gather(second_normed, "tensor", axis=0, tiled=True)
    hidden = jnp.dot(second_all, up_weight, preferred_element_type=jnp.float32)
    active = gelu_exact(hidden).astype(jnp.bfloat16)
    picked = lax.slice_in_dim(active, 0, local_rows * lax.axis_size("tensor"), axis=0)
    branch = lax.psum_scatter(
        jnp.dot(picked, down_weight, preferred_element_type=jnp.float32).astype(jnp.bfloat16),
        "tensor",
        scatter_dimension=0,
        tiled=True,
    ).astype(jnp.float32)
    result = (residual + branch).astype(jnp.bfloat16)
    grad_float = cotangent.astype(jnp.float32)
    branch_all = lax.all_gather(cotangent, "tensor", axis=0, tiled=True)
    down_grad = lax.dot_general(active, branch_all, lead_pair, preferred_element_type=jnp.float32)
    active_grad = lax.dot_general(
        branch_all, down_weight, trail_pair, preferred_element_type=jnp.float32
    )
    gelu_value, gelu_pull = jax.vjp(gelu_exact, hidden)
    hidden_grad = gelu_pull(active_grad)[0].astype(jnp.bfloat16)
    up_grad = lax.dot_general(
        second_all, hidden_grad, lead_pair, preferred_element_type=jnp.float32
    )
    picked = lax.slice_in_dim(hidden_grad, 0, lax.axis_size("tensor") * local_rows, axis=0)
    second_grad = lax.psum_scatter(
        lax.dot_general(picked, up_weight, trail_pair, preferred_element_type=jnp.float32),
        "tensor",
        scatter_dimension=0,
        tiled=True,
    )
    norm_value, second_pull = jax.vjp(
        modulated_norm, residual, second_gain, second_bias, modulation[:, 2], modulation[:, 3]
    )
    residual_back, second_gain_grad, second_bias_grad, scale_two_grad, shift_two_grad = second_pull(
        second_grad
    )
    residual_grad = grad_float + residual_back
    attended_all = lax.all_gather(residual_grad.astype(jnp.bfloat16), "tensor", axis=0, tiled=True)
    out_weight_grad = lax.dot_general(
        mixed_flat, attended_all, lead_pair, preferred_element_type=jnp.float32
    )
    mixed_grad = lax.dot_general(
        attended_all, out_weight, trail_pair, preferred_element_type=jnp.float32
    ).astype(jnp.bfloat16)
    query_grad, key_grad, value_grad = lax.map(
        attend_back,
        (queries, keys_all, values_all, segment_ids, logsum, mixed_grad.reshape(row_shape)),
    )
    flat_shape = (group_rows, head_local, HEAD)
    query_pre = unrotate(query_grad.reshape(flat_shape), cosine_table, sine_table)
    key_pre = unrotate(key_grad.reshape(flat_shape), cosine_table, sine_table)
    projected_grad = jnp.stack([query_pre, key_pre, value_grad.reshape(flat_shape)], axis=1)
    projected_grad = projected_grad.astype(jnp.bfloat16).reshape(group_rows, 3 * local_width)
    qkv_grad = lax.dot_general(
        first_all, projected_grad, lead_pair, preferred_element_type=jnp.float32
    )
    qkv_grad = qkv_grad.reshape(model_width, 3, local_width)
    picked = projected_grad
    first_grad = lax.psum_scatter(
        lax.dot_general(picked, qkv_flat, trail_pair, preferred_element_type=jnp.float32),
        "tensor",
        scatter_dimension=0,
        tiled=True,
    )
    first_value, first_pull = jax.vjp(
        modulated_norm, tokens_float, first_gain, first_bias, modulation[:, 0], modulation[:, 1]
    )
    input_back, first_gain_grad, first_bias_grad, scale_one_grad, shift_one_grad = first_pull(
        first_grad
    )
    input_grad = residual_grad + input_back
    modulation_grad = jnp.stack(
        [scale_one_grad, shift_one_grad, scale_two_grad, shift_two_grad], axis=1
    )
    time_bias_grad = jnp.sum(modulation_grad, axis=0)
    time_weight_grad = lax.dot_general(
        time_embed,
        modulation_grad.astype(jnp.bfloat16).reshape(local_rows, 4 * model_width),
        lead_pair,
        preferred_element_type=jnp.float32,
    ).reshape(embed_width, 4, model_width)
    shared = lax.psum(
        (
            first_gain_grad,
            first_bias_grad,
            second_gain_grad,
            second_bias_grad,
            time_weight_grad,
            time_bias_grad,
        ),
        ("dp", "tensor"),
    )
    qkv_summed, out_summed, up_summed, down_summed = lax.psum(
        (qkv_grad, out_weight_grad, up_grad, down_grad), "dp"
    )
    return (
        result,
        input_grad,
        shared[0],
        shared[1],
        shared[2],
        shared[3],
        shared[4],
        shared[5],
        qkv_summed,
        out_summed,
        up_summed,
        down_summed,
    )


def solution(mesh):
    return jax.shard_map(
        local,
        mesh=mesh,
        in_specs=(
            P(("dp", "tensor"), None),
            P(("dp", "tensor"), None),
            P("dp", None),
            P("dp", None),
            P(),
            P(),
            P(),
            P(),
            P(),
            P(),
            P(None, None, "tensor"),
            P("tensor", None),
            P(None, "tensor"),
            P("tensor", None),
            P(("dp", "tensor"), None),
        ),
        out_specs=(
            P(("dp", "tensor"), None),
            P(("dp", "tensor"), None),
            P(),
            P(),
            P(),
            P(),
            P(),
            P(),
            P(None, None, "tensor"),
            P("tensor", None),
            P(None, "tensor"),
            P("tensor", None),
        ),
        check_vma=False,
    )
```

profile of v0, /device:TPU:21, one launch (start us, length us, event | category | flops | bytes accessed | tf_op | source)
XLA Modules:
  0.0 918.6 jit_solution(1928452809448740917)
XLA Ops:
  10.5 3.8 copy.38
  14.3 4.1 copy.30
  18.4 2.4 convolution_add_fusion
  20.8 2.0 copy-done.4
  24.6 2.6 copy.31
  28.5 41.3 %all-gather.5.cloned.1.call-done = bf16[1024,1024]{1,0:T(8,128)(2,1)} async-done(((bf16[256,1024]{1,0:T(8,128)(2,1)}), bf16[1024,1024]{1,0:T(8,128)(2,1)}) %all-gather.5.cloned.1.call-update) | async-done | bytes 2097168 | tf_op jit(solution)/shard_map/all_gather | solution.py:165
  69.8 3.9 fusion.20
  76.1 1.9 fusion.1
  79.4 2.1 fusion.43
  83.4 1.9 fusion
  86.7 2.1 fusion.42
  89.7 2.8 fusion.86
  92.5 77.5 %reduce-scatter.5.cloned.1.call-done = f32[256,1024]{1,0:T(8,128)} async-done(((f32[1024,1024]{1,0:T(8,128)}), f32[256,1024]{1,0:T(8,128)}) %reduce-scatter.5.cloned.1.call-update) | async-done | bytes 1048592 | tf_op jit(solution)/shard_map/reduce_scatter | solution.py:181
  171.9 2.7 fusion.54
  175.4 43.9 %all-gather.7.cloned.1.call-done = bf16[1024,1024]{1,0:T(8,128)(2,1)} async-done(((bf16[256,1024]{1,0:T(8,128)(2,1)}), bf16[1024,1024]{1,0:T(8,128)(2,1)}) %all-gather.7.cloned.1.call-update) | async-done | bytes 2097168 | tf_op jit(solution)/shard_map/all_gather | solution.py:191
  219.2 6.6 fusion.87
  225.8 39.6 %all-gather.9.cloned.1.call-done = bf16[1024,1024]{1,0:T(8,128)(2,1)} async-done(((bf16[256,1024]{1,0:T(8,128)(2,1)}), bf16[1024,1024]{1,0:T(8,128)(2,1)}) %all-gather.9.cloned.1.call-update) | async-done | bytes 2097168 | tf_op jit(solution)/shard_map/all_gather | solution.py:203
  265.4 14.5 %add_convert_fusion = (bf16[1024,1024]{1,0:T(8,128)(2,1)S(1)}, f32[1024,1024]{1,0:T(8,128)}) fusion(f32[1024,1024]{1,0:T(8,128)} %fusion.87, bf16[1024,1024]{1,0:T(8,128)(2,1)} %all-gather.9.cloned.1.call-done, bf16[1024,1024]{1,0:T(8,128)(2,1)S(1)} %copy-done), kind=kOutput, calls=%fused_computation.23 | convolution fusion | flops 2222981120 | bytes 14680064 | tf_op jit(solution)/shard_map/dot_general | solution.py:205
  281.2 4.3 fusion.88
  285.7 4.6 multiply_convert_fusion.2
  291.6 3.7 convolution_convert_fusion
  295.3 67.9 %reduce-scatter.9.cloned.1.call-done = f32[256,1024]{1,0:T(8,128)} async-done(((f32[1024,1024]{1,0:T(8,128)}), f32[256,1024]{1,0:T(8,128)}) %reduce-scatter.9.cloned.1.call-update) | async-done | bytes 1048592 | tf_op jit(solution)/shard_map/reduce_scatter | solution.py:214
  363.2 3.3 multiply_reduce_fusion.2
  366.5 42.6 %reduce-scatter.7.cloned.1.call-done = bf16[256,1024]{1,0:T(8,128)(2,1)} async-done(((bf16[1024,1024]{1,0:T(8,128)(2,1)}), bf16[256,1024]{1,0:T(8,128)(2,1)}) %reduce-scatter.7.cloned.1.call-update) | async-done | bytes 524304 | tf_op jit(solution)/shard_map/reduce_scatter | solution.py:195
  409.1 2.5 fusion.74
  413.1 44.4 %all-gather.11.cloned.1.call-done = bf16[1024,1024]{1,0:T(8,128)(2,1)} async-done(((bf16[256,1024]{1,0:T(8,128)(2,1)}), bf16[1024,1024]{1,0:T(8,128)(2,1)}) %all-gather.11.cloned.1.call-update) | async-done | bytes 2097168 | tf_op jit(solution)/shard_map/all_gather | solution.py:227
  457.5 2.5 convolution_convert_fusion.1
  460.1 7.9 multiply_reduce_fusion.1
  468.5 4.6 multiply_convert_fusion.1
  473.1 2.2 fusion.36
  477.9 3.3 multiply_reduce_fusion
  489.0 3.9 fusion.89
  494.5 6.3 fusion.93
  500.8 4.4 fusion.92
  507.0 3.5 fusion.22
  510.7 59.9 %reduce-scatter.11.cloned.1.call-done = f32[256,1024]{1,0:T(8,128)} async-done(((f32[1024,1024]{1,0:T(8,128)}), f32[256,1024]{1,0:T(8,128)}) %reduce-scatter.11.cloned.1.call-update) | async-done | bytes 1048592 | tf_op jit(solution)/shard_map/reduce_scatter | solution.py:248
  570.6 2.1 fusion.72
  573.7 3.0 fusion.19
  576.7 3.9 copy.32
  580.6 4.7 fusion.90
  585.3 5.5 copy.33
  590.9 2.6 fusion.18
  594.1 40.6 %all-reduce = (f32[1024]{0:T(1024)}, f32[1024]{0:T(1024)}, f32[1024]{0:T(1024)}, f32[1024]{0:T(1024)}, f32[4,1024]{1,0:T(4,128)}) all-reduce(f32[1024]{0:T(1024)S(1)} %get-tuple-element.55, f32[1024]{0:T(1024)S(1)} %get-tuple-element.68, f32[1024]{0:T(1024)S(1)} %get-tuple-element.53, ...), channel_id=1, replica_groups=mesh['dp'=8,'tensor'=4] {'dp','tensor'}, use_global_device_ids=true, to_apply=%region_19.20 | all-reduce | flops 8192 | bytes 65536 | tf_op jit(solution)/shard_map/psum | solution.py:271
  636.1 113.8 %all-reduce.7.cloned.1.call-done = (f32[1024,3,256]{2,0,1:T(8,128)}, f32[256,1024]{1,0:T(8,128)}, f32[1024,1024]{1,0:T(8,128)}, f32[1024,1024]{1,0:T(8,128)}) async-done(((f32[1024,3,256]{2,0,1:T(8,128)}, f32[256,1024]{1,0:T(8,128)}, f32[1024,1024]{1,0:T(8,128)}, f32[1024,1024]{1,0:T(8,128)}), (f32[1024,3,256]{2,0,1:T(8,128)}, f32[256,1024]{1,0:T(8,128)}, f32[1024,1024]{1,0:T(8,128)}, ...) | async-done | bytes 12582928 | tf_op jit(solution)/shard_map/psum | solution.py:282
  749.9 146.2 %all-reduce.5.cloned.1.call-done = f32[256,4,1024]{2,1,0:T(4,128)} async-done(((f32[256,4,1024]{2,1,0:T(4,128)}), f32[256,4,1024]{2,1,0:T(4,128)}) %all-reduce.5.cloned.1.call-update) | async-done | bytes 4194320 | tf_op jit(solution)/shard_map/psum | solution.py:271
  896.2 5.3 copy.44
  905.5 2.1 copy.47
  909.2 2.0 copy.48
  (214 shorter events, 43.8 us)
Async XLA Ops:
  7.2 258.2 %copy-start = (bf16[1024,1024]{1,0:T(8,128)(2,1)S(1)}, bf16[1024,1024]{1,0:T(8,128)(2,1)}, u32[]{:S(2)}) copy-start(bf16[1024,1024]{1,0:T(8,128)(2,1)} %param.28) | copy-start | bytes 6291460
  7.2 62.6 %all-gather.5.cloned.1.call-start = ((), (), s32[]{:S(2)}) async-start(), calls=%async_computation.4 | async-start | bytes 2621440 | tf_op jit(solution)/shard_map/all_gather | solution.py:165
  8.6 12.2 %copy-start.55 = (f32[256]{0:T(256)}, f32[256]{0:T(256)S(1)}, u32[]{:S(2)}) copy-start(f32[256]{0:T(256)S(1)} %broadcast_multiply_fusion.1) | copy-start | bytes 3076
  10.5 10.3 %copy-start.57 = (f32[256]{0:T(256)}, f32[256]{0:T(256)S(1)}, u32[]{:S(2)}) copy-start(f32[256]{0:T(256)S(1)} %fusion.64) | copy-start | bytes 3076
  10.5 7.9 copy-start.48
  10.5 7.9 copy-start.59
  18.4 6.2 copy-start.66
  24.0 146.0 %reduce-scatter.5.cloned.1.call-start = ((), (), s32[]{:S(2)}) async-start(), calls=%async_computation.5 | async-start | bytes 5242880 | tf_op jit(solution)/shard_map/reduce_scatter | solution.py:181
  27.8 46.1 %copy-start.43 = (f32[1024,32]{0,1:T(8,128)}, f32[1024,32]{0,1:T(8,128)S(1)}, u32[]{:S(2)}) copy-start(f32[1024,32]{0,1:T(8,128)S(1)} %get-tuple-element.106) | copy-start | bytes 393220
  27.8 46.1 %copy-start.45 = (f32[1024,32]{0,1:T(8,128)}, f32[1024,32]{0,1:T(8,128)S(1)}, u32[]{:S(2)}) copy-start(f32[1024,32]{0,1:T(8,128)S(1)} %get-tuple-element.107) | copy-start | bytes 393220
  73.7 11.6 %copy-start.14 = (f32[1024,3,4,64]{0,3,2,1:T(8,128)}, f32[1024,3,4,64]{0,3,2,1:T(8,128)S(1)}, u32[]{:S(2)}) copy-start(f32[1024,3,4,64]{0,3,2,1:T(8,128)S(1)} %fusion.20) | copy-start | bytes 9437188
  74.3 7.3 copy-start.24
  74.3 7.3 copy-start.27
  74.3 7.3 copy-start.30
  74.3 7.3 copy-start.33
  92.4 79.4 %copy-start.54 = (f32[1024]{0:T(1024)S(1)}, f32[1024]{0:T(1024)}, u32[]{:S(2)}) copy-start(f32[1024]{0:T(1024)} %param.21) | copy-start | bytes 12292
  92.4 79.4 %copy-start.61 = (f32[1024]{0:T(1024)S(1)}, f32[1024]{0:T(1024)}, u32[]{:S(2)}) copy-start(f32[1024]{0:T(1024)} %param.22) | copy-start | bytes 12292
  92.5 126.8 %all-gather.7.cloned.1.call-start = ((), (), s32[]{:S(2)}) async-start(), calls=%async_computation.6 | async-start | bytes 2621440 | tf_op jit(solution)/shard_map/all_gather | solution.py:191
  174.6 90.9 %all-gather.9.cloned.1.call-start = ((), (), s32[]{:S(2)}) async-start(), calls=%async_computation.8 | async-start | bytes 2621440 | tf_op jit(solution)/shard_map/all_gather | solution.py:203
  175.1 188.1 %reduce-scatter.9.cloned.1.call-start = ((), (), s32[]{:S(2)}) async-start(), calls=%async_computation.9 | async-start | bytes 5242880 | tf_op jit(solution)/shard_map/reduce_scatter | solution.py:214
  265.4 15.8 %copy-start.67 = (bf16[1024,1024]{1,0:T(8,128)(2,1)S(1)}, bf16[1024,1024]{1,0:T(8,128)(2,1)}, u32[]{:S(2)}) copy-start(bf16[1024,1024]{1,0:T(8,128)(2,1)} %param.27) | copy-start | bytes 6291460
  285.6 123.5 %reduce-scatter.7.cloned.1.call-start = ((), (), s32[]{:S(2)}) async-start(), calls=%async_computation.7 | async-start | bytes 2621440 | tf_op jit(solution)/shard_map/reduce_scatter | solution.py:195
  295.3 116.4 %copy-start.16 = (bf16[256,1024]{1,0:T(8,128)(2,1)S(1)}, bf16[256,1024]{1,0:T(8,128)(2,1)}, u32[]{:S(2)}) copy-start(bf16[256,1024]{1,0:T(8,128)(2,1)} %param.29) | copy-start | bytes 1572868
  295.3 162.2 %all-gather.11.cloned.1.call-start = ((), (), s32[]{:S(2)}) async-start(), calls=%async_computation.10 | async-start | bytes 2621440 | tf_op jit(solution)/shard_map/all_gather | solution.py:227
  366.5 91.0 %copy-start.51 = (bf16[256,1024]{1,0:T(8,128)(2,1)S(1)}, bf16[256,1024]{1,0:T(8,128)(2,1)}, u32[]{:S(2)}) copy-start(bf16[256,1024]{1,0:T(8,128)(2,1)} %param.26) | copy-start | bytes 1572868
  411.6 48.3 %copy-start.7 = (f32[256,1024]{1,0:T(8,128)}, f32[256,1024]{1,0:T(8,128)S(1)}, u32[]{:S(2)}) copy-start(f32[256,1024]{1,0:T(8,128)S(1)} %get-tuple-element.81) | copy-start | bytes 3145732
  412.8 157.7 %reduce-scatter.11.cloned.1.call-start = ((), (), s32[]{:S(2)}) async-start(), calls=%async_computation.11 | async-start | bytes 5242880 | tf_op jit(solution)/shard_map/reduce_scatter | solution.py:248
  460.0 8.0 copy-start.21
  460.0 16.1 %copy-start.23 = (bf16[512,256]{0,1:T(8,128)(2,1)}, bf16[512,256]{0,1:T(8,128)(2,1)S(1)}, u32[]{:S(2)}) copy-start(bf16[512,256]{0,1:T(8,128)(2,1)S(1)} %get-tuple-element.101) | copy-start | bytes 786436
  460.0 8.0 slice-start.2
  460.1 8.4 slice-start.3
  468.0 8.1 slice-start
  468.5 7.7 slice-start.1
  492.9 257.0 %all-reduce.7.cloned.1.call-start = ((), (), s32[]{:S(2)}) async-start(), calls=%async_computation.13 | async-start | bytes 25165824 | tf_op jit(solution)/shard_map/psum | solution.py:282
  494.5 6.3 copy-start.69
  494.5 6.3 copy-start.71
  500.8 6.2 copy-start.42
  500.8 6.2 copy-start.68
  510.5 60.0 %copy-start.6 = (bf16[256,1024]{1,0:T(8,128)(2,1)S(1)}, bf16[256,1024]{1,0:T(8,128)(2,1)}, u32[]{:S(2)}) copy-start(bf16[256,1024]{1,0:T(8,128)(2,1)} %param.15) | copy-start | bytes 1572868
  510.5 60.0 %copy-start.53 = (f32[1024]{0:T(1024)S(1)}, f32[1024]{0:T(1024)}, u32[]{:S(2)}) copy-start(f32[1024]{0:T(1024)} %param.19) | copy-start | bytes 12292
  510.6 60.0 %copy-start.56 = (f32[256]{0:T(256)S(1)}, f32[256]{0:T(256)}, u32[]{:S(2)}) copy-start(f32[256]{0:T(256)} %copy-done.55) | copy-start | bytes 3076
  510.6 60.0 %copy-start.58 = (f32[256]{0:T(256)S(1)}, f32[256]{0:T(256)}, u32[]{:S(2)}) copy-start(f32[256]{0:T(256)} %copy-done.57) | copy-start | bytes 3076
  510.6 60.0 %copy-start.63 = (f32[1024]{0:T(1024)S(1)}, f32[1024]{0:T(1024)}, u32[]{:S(2)}) copy-start(f32[1024]{0:T(1024)} %param.20) | copy-start | bytes 12292
  510.6 63.1 %copy-start.9 = (f32[256,1024]{1,0:T(8,128)S(1)}, f32[256,1024]{1,0:T(8,128)}, u32[]{:S(2)}) copy-start(f32[256,1024]{1,0:T(8,128)} %reduce-scatter.9.cloned.1.call-done) | copy-start | bytes 3145732
  510.6 385.6 %all-reduce.5.cloned.1.call-start = ((), (), s32[]{:S(2)}) async-start(), calls=%async_computation.12 | async-start | bytes 8388608 | tf_op jit(solution)/shard_map/psum | solution.py:271
  573.7 6.9 copy-start.49
  590.9 43.8 %copy-start.8 = (f32[256,1024]{1,0:T(8,128)S(1)}, f32[256,1024]{1,0:T(8,128)}, u32[]{:S(2)}) copy-start(f32[256,1024]{1,0:T(8,128)} %copy-done.7) | copy-start | bytes 3145732
  590.9 43.8 %copy-start.17 = (bf16[256,1024]{1,0:T(8,128)(2,1)S(1)}, bf16[256,1024]{1,0:T(8,128)(2,1)}, u32[]{:S(2)}) copy-start(bf16[256,1024]{1,0:T(8,128)(2,1)} %param.29) | copy-start | bytes 1572868
  (38 other events, 103.3 us)
Sparse Core Ops, SparseCore 0:
  24.1 45.5 all-gather.4
  92.6 77.3 reduce-scatter.4
  174.7 44.4 all-gather.6
  220.7 44.6 all-gather.8
  285.7 77.4 reduce-scatter.8
  365.9 43.1 reduce-scatter.6
  412.9 44.5 all-gather.10
  493.0 77.4 reduce-scatter.10
  575.7 174.2 all-reduce.6
  756.8 139.3 all-reduce.4
where the time goes:
time: 926 us; the launch traced here: 919 us
  waiting for transfers between devices  678 us (73%)
  matrix products  93 us (10%)
  local copies, waits for them, and re-layouts  48.3 us (5%)
  other arithmetic  41.8 us (5%)
  blocking collectives  40.6 us (4%)
  between operations  15.5 us (2%)
    psum x1, waiting for transfers between devices, local(): lax.psum((first_gain_grad, first_bias_grad, second_gain_grad, second_bias...  146 us
    psum x1, waiting for transfers between devices, local(): lax.psum((qkv_grad, out_weight_grad, up_grad, down_grad), 'dp')  114 us
    reduce_scatter x1, waiting for transfers between devices, local(): lax.psum_scatter(jnp.dot(picked, out_weight, preferred_element_type=jnp.f...  77.5 us
    reduce_scatter x1, waiting for transfers between devices, local(): lax.psum_scatter(lax.dot_general(picked, up_weight, trail_pair, preferred...  67.9 us
    reduce_scatter x1, waiting for transfers between devices, local(): lax.psum_scatter(lax.dot_general(picked, qkv_flat, trail_pair, preferred_...  59.9 us
    all_gather x1, waiting for transfers between devices, local(): lax.all_gather(residual_grad.astype(jnp.bfloat16), 'tensor', axis=0, tile...  44.4 us
    all_gather x1, waiting for transfers between devices, local(): second_all = lax.all_gather(second_normed, 'tensor', axis=0, tiled=True)  43.9 us
    reduce_scatter x1, waiting for transfers between devices, local(): lax.psum_scatter(jnp.dot(picked, down_weight, preferred_element_type=jnp....  42.6 us
  transfers between devices with their start and end apart: 10, of which 10 were waited for; matrix products, arithmetic and copies ran while one was open for 7% of the time, Pallas kernels for 0%

commit v1 on v0

--- a/solution.py
+++ b/solution.py
@@ -179,11 +179,11 @@
     mixed_flat = mixed_heads.reshape(group_rows, local_width)
     picked = lax.slice_in_dim(mixed_flat, 0, lax.axis_size("tensor") * local_rows, axis=0)
     attended = lax.psum_scatter(
-        jnp.dot(picked, out_weight, preferred_element_type=jnp.float32),
+        jnp.dot(picked, out_weight, preferred_element_type=jnp.float32).astype(jnp.bfloat16),
         "tensor",
         scatter_dimension=0,
         tiled=True,
-    )
+    ).astype(jnp.float32)
     residual = tokens_float + attended
     second_normed = modulated_norm(
         residual, second_gain, second_bias, modulation[:, 2], modulation[:, 3]
@@ -212,11 +212,13 @@
     )
     picked = lax.slice_in_dim(hidden_grad, 0, lax.axis_size("tensor") * local_rows, axis=0)
     second_grad = lax.psum_scatter(
-        lax.dot_general(picked, up_weight, trail_pair, preferred_element_type=jnp.float32),
+        lax.dot_general(picked, up_weight, trail_pair, preferred_element_type=jnp.float32).astype(
+            jnp.bfloat16
+        ),
         "tensor",
         scatter_dimension=0,
         tiled=True,
-    )
+    ).astype(jnp.float32)
     norm_value, second_pull = jax.vjp(
         modulated_norm, residual, second_gain, second_bias, modulation[:, 2], modulation[:, 3]
     )
@@ -246,11 +248,13 @@
     qkv_grad = qkv_grad.reshape(model_width, 3, local_width)
     picked = projected_grad
     first_grad = lax.psum_scatter(
-        lax.dot_general(picked, qkv_flat, trail_pair, preferred_element_type=jnp.float32),
+        lax.dot_general(picked, qkv_flat, trail_pair, preferred_element_type=jnp.float32).astype(
+            jnp.bfloat16
+        ),
         "tensor",
         scatter_dimension=0,
         tiled=True,
-    )
+    ).astype(jnp.float32)
     first_value, first_pull = jax.vjp(
         modulated_norm, tokens_float, first_gain, first_bias, modulation[:, 0], modulation[:, 1]
     )
@@ -274,14 +278,18 @@
             first_bias_grad,
             second_gain_grad,
             second_bias_grad,
-            time_weight_grad,
+            time_weight_grad.astype(jnp.bfloat16),
             time_bias_grad,
         ),
         ("dp", "tensor"),
     )
-    qkv_summed, out_summed, up_summed, down_summed = lax.psum(
-        (qkv_grad, out_weight_grad, up_grad, down_grad), "dp"
-    )
+    halves = lax.psum(
+        tuple(
+            part.astype(jnp.bfloat16) for part in (qkv_grad, out_weight_grad, up_grad, down_grad)
+        ),
+        "dp",
+    )
+    qkv_summed, out_summed, up_summed, down_summed = (part.astype(jnp.float32) for part in halves)
     return (
         result,
         input_grad,
@@ -289,7 +297,7 @@
         shared[1],
         shared[2],
         shared[3],
-        shared[4],
+        shared[4].astype(jnp.float32),
         shared[5],
         qkv_summed,
         out_summed,

time: 926 us -> 744 us (0.80)
  waiting for transfers between devices: 678 us -> 489 us
  other arithmetic: 41.8 us -> 61.1 us
  local copies, waits for them, and re-layouts: 48.3 us -> 30.5 us
  starting transfers between devices: 1.57 us -> 13.2 us
    psum x1, waiting for transfers between devices: 146 us -> 88.1 us  [local(): lax.psum((first_gain_grad, first_bias_grad, second_gain_grad, second_bias...]
    reduce_scatter x1, waiting for transfers between devices: 67.9 us -> 33.8 us  [local(): lax.psum_scatter(lax.dot_general(picked, up_weight, trail_pair, preferred...]
    reduce_scatter x1, waiting for transfers between devices: 77.5 us -> 43.4 us  [local(): lax.psum_scatter(jnp.dot(picked, out_weight, preferred_element_type=jnp.f...]
    reduce_scatter x1, waiting for transfers between devices: 59.9 us -> 35.4 us  [local(): lax.psum_scatter(lax.dot_general(picked, qkv_flat, trail_pair, preferred_...]
    unnamed x159 -> x152, local copies, waits for them, and re-layouts: 34.6 us -> 18.6 us
    convert_element_type x0 -> x5, other arithmetic: none -> 15.4 us  [the longest x4 10.6 us: local(): part.astype(jnp.float32)]
    psum x1, waiting for transfers between devices: 114 us -> 98.5 us  [local(): lax.psum(tuple((part.astype(jnp.bfloat16) for part in (qkv_grad, out_weig...]
    reduce_scatter x1, starting transfers between devices: 0.21 us -> 12.3 us  [local(): lax.psum_scatter(lax.dot_general(picked, up_weight, trail_pair, preferred...]
where the time goes in v1:
time: 744 us; the launch traced here: 737 us
  waiting for transfers between devices  489 us (66%)
  matrix products  88.5 us (12%)
  other arithmetic  61.1 us (8%)
  blocking collectives  39.5 us (5%)
  local copies, waits for them, and re-layouts  30.5 us (4%)
  between operations  15.3 us (2%)
  starting transfers between devices  13.2 us (2%)
    psum x1, waiting for transfers between devices, local(): lax.psum(tuple((part.astype(jnp.bfloat16) for part in (qkv_grad, out_weig...  98.5 us
    psum x1, waiting for transfers between devices, local(): lax.psum((first_gain_grad, first_bias_grad, second_gain_grad, second_bias...  88.1 us
    reduce_scatter x1, waiting for transfers between devices, local(): lax.psum_scatter(jnp.dot(picked, out_weight, preferred_element_type=jnp.f...  43.4 us
    reduce_scatter x1, waiting for transfers between devices, local(): lax.psum_scatter(jnp.dot(picked, down_weight, preferred_element_type=jnp....  42.3 us
    all_gather x1, waiting for transfers between devices, local(): first_all = lax.all_gather(first_normed, 'tensor', axis=0, tiled=True)  40.5 us
    all_gather x1, waiting for transfers between devices, local(): branch_all = lax.all_gather(cotangent, 'tensor', axis=0, tiled=True)  39.6 us
    psum x1, blocking collectives, local(): lax.psum((first_gain_grad, first_bias_grad, second_gain_grad, second_bias...  39.5 us
    reduce_scatter x1, waiting for transfers between devices, local(): lax.psum_scatter(lax.dot_general(picked, qkv_flat, trail_pair, preferred_...  35.4 us
  transfers between devices with their start and end apart: 10, of which 10 were waited for; matrix products, arithmetic and copies ran while one was open for 7% of the time, Pallas kernels for 0%

profile of v1, /device:TPU:21, one launch (start us, length us, event | category | flops | bytes accessed | tf_op | source)
XLA Modules:
  0.0 736.5 jit_solution(4456388751135296459)
XLA Ops:
  10.0 3.8 copy.38
  13.8 4.1 copy.30
  17.9 2.4 convolution_add_fusion
  20.3 2.0 copy-done.5
  24.0 2.6 copy.31
  28.8 40.5 %all-gather.5.cloned.1.call-done = bf16[1024,1024]{1,0:T(8,128)(2,1)} async-done(((bf16[256,1024]{1,0:T(8,128)(2,1)}), bf16[1024,1024]{1,0:T(8,128)(2,1)}) %all-gather.5.cloned.1.call-update) | async-done | bytes 2097168 | tf_op jit(solution)/shard_map/all_gather | solution.py:165
  69.3 3.9 fusion.20
  79.7 2.1 fusion.46
  87.0 2.1 fusion.45
  90.0 2.1 convolution_convert_fusion.5
  92.1 43.4 %reduce-scatter.5.cloned.1.call-done = bf16[256,1024]{1,0:T(8,128)(2,1)} async-done(((bf16[1024,1024]{1,0:T(8,128)(2,1)}), bf16[256,1024]{1,0:T(8,128)(2,1)}) %reduce-scatter.5.cloned.1.call-update) | async-done | bytes 524304 | tf_op jit(solution)/shard_map/reduce_scatter | solution.py:181
  138.2 2.9 fusion.57
  141.7 12.3 %reduce-scatter.9.cloned.1.call-start = ((), (), s32[]{:S(2)}) async-start(), calls=%async_computation.9 | async-start | bytes 2621440 | tf_op jit(solution)/shard_map/reduce_scatter | solution.py:214
  154.0 31.8 %all-gather.7.cloned.1.call-done = bf16[1024,1024]{1,0:T(8,128)(2,1)} async-done(((bf16[256,1024]{1,0:T(8,128)(2,1)}), bf16[1024,1024]{1,0:T(8,128)(2,1)}) %all-gather.7.cloned.1.call-update) | async-done | bytes 2097168 | tf_op jit(solution)/shard_map/all_gather | solution.py:191
  185.8 6.6 fusion.87
  192.3 39.6 %all-gather.9.cloned.1.call-done = bf16[1024,1024]{1,0:T(8,128)(2,1)} async-done(((bf16[256,1024]{1,0:T(8,128)(2,1)}), bf16[1024,1024]{1,0:T(8,128)(2,1)}) %all-gather.9.cloned.1.call-update) | async-done | bytes 2097168 | tf_op jit(solution)/shard_map/all_gather | solution.py:203
  232.0 14.5 %add_convert_fusion = (bf16[1024,1024]{1,0:T(8,128)(2,1)S(1)}, f32[1024,1024]{1,0:T(8,128)}) fusion(f32[1024,1024]{1,0:T(8,128)} %fusion.87, bf16[1024,1024]{1,0:T(8,128)(2,1)} %all-gather.9.cloned.1.call-done, bf16[1024,1024]{1,0:T(8,128)(2,1)S(1)} %copy-done), kind=kOutput, calls=%fused_computation.24 | convolution fusion | flops 2222981120 | bytes 14680064 | tf_op jit(solution)/shard_map/dot_general | solution.py:205
  247.8 3.8 convolution_convert_fusion.3
  251.7 4.6 multiply_convert_fusion.2
  257.6 3.7 convolution_convert_fusion.4
  261.3 33.8 %reduce-scatter.9.cloned.1.call-done = bf16[256,1024]{1,0:T(8,128)(2,1)} async-done(((bf16[1024,1024]{1,0:T(8,128)(2,1)}), bf16[256,1024]{1,0:T(8,128)(2,1)}) %reduce-scatter.9.cloned.1.call-update) | async-done | bytes 524304 | tf_op jit(solution)/shard_map/reduce_scatter | solution.py:214
  295.1 3.7 multiply_reduce_fusion.2
  298.8 42.3 %reduce-scatter.7.cloned.1.call-done = bf16[256,1024]{1,0:T(8,128)(2,1)} async-done(((bf16[1024,1024]{1,0:T(8,128)(2,1)}), bf16[256,1024]{1,0:T(8,128)(2,1)}) %reduce-scatter.7.cloned.1.call-update) | async-done | bytes 524304 | tf_op jit(solution)/shard_map/reduce_scatter | solution.py:195
  341.0 2.8 fusion.77
  345.2 6.2 convolution_convert_fusion.1
  351.4 3.8 convolution_convert_fusion.2
  355.2 34.6 %all-gather.11.cloned.1.call-done = bf16[1024,1024]{1,0:T(8,128)(2,1)} async-done(((bf16[256,1024]{1,0:T(8,128)(2,1)}), bf16[1024,1024]{1,0:T(8,128)(2,1)}) %all-gather.11.cloned.1.call-update) | async-done | bytes 2097168 | tf_op jit(solution)/shard_map/all_gather | solution.py:229
  389.7 2.3 convolution_convert_fusion.8
  392.1 8.1 %multiply_reduce_fusion.1 = (f32[4,512]{1,0:T(4,128)S(1)}, f32[4,512,1024]{2,1,0:T(8,128)}) fusion(f32[4,512,1024]{2,1,0:T(8,128)} %copy-done.3, f32[4,512]{1,0:T(4,128)S(1)} %log_add_fusion.1, bf16[512,4,64]{0,2,1:T(8,128)(2,1)S(1)} %bitcast.156, f32[1024,3,4,64]{0,3,2,1:T(8,128)} %copy-done.9), kind=kOutput, calls=%fused_computation.4 | convolution fusion | flops 274724864 | bytes 17580032 | tf_op jit(solution)/shard_map/while/body/eval_jaxpr/qhd,khd->hqk/dot_general | solution.py:108
  400.6 4.5 multiply_convert_fusion.1
  405.2 2.2 fusion.39
  410.0 3.4 multiply_reduce_fusion
  422.7 3.0 fusion.24
  427.1 4.7 convolution_convert_fusion.6
  432.0 98.5 %all-reduce.7.cloned.1.call-done = (bf16[1024,3,256]{2,0,1:T(8,128)(2,1)}, bf16[256,1024]{1,0:T(8,128)(2,1)}, bf16[1024,1024]{1,0:T(8,128)(2,1)}, bf16[1024,1024]{1,0:T(8,128)(2,1)}) async-done(((bf16[1024,3,256]{2,0,1:T(8,128)(2,1)}, bf16[256,1024]{1,0:T(8,128)(2,1)}, bf16[1024,1024]{1,0:T(8,128)(2,1)}, bf16[1024,1024]{1,0:T(8,128)(2,1)}), (bf16[1024,3,256]{2,0,1:T(8,128)(2,1)}, ...) | async-done | bytes 6291472 | tf_op jit(solution)/shard_map/psum | solution.py:286
  530.4 2.3 convert_element_type.203
  532.7 3.3 convert_element_type.201
  536.0 2.5 convert_element_type.205
  538.5 2.5 convert_element_type.207
  541.0 35.4 %reduce-scatter.11.cloned.1.call-done = bf16[256,1024]{1,0:T(8,128)(2,1)} async-done(((bf16[1024,1024]{1,0:T(8,128)(2,1)}), bf16[256,1024]{1,0:T(8,128)(2,1)}) %reduce-scatter.11.cloned.1.call-update) | async-done | bytes 524304 | tf_op jit(solution)/shard_map/reduce_scatter | solution.py:250
  577.7 2.0 fusion.51
  583.0 2.8 copy.32
  585.9 2.1 convolution_convert_fusion
  588.0 4.7 copy.33
  592.7 39.5 %all-reduce = (f32[1024]{0:T(1024)}, f32[1024]{0:T(1024)}, f32[1024]{0:T(1024)}, f32[1024]{0:T(1024)}, f32[4,1024]{1,0:T(4,128)}) all-reduce(f32[1024]{0:T(1024)S(1)} %get-tuple-element.55, f32[1024]{0:T(1024)S(1)} %get-tuple-element.68, f32[1024]{0:T(1024)S(1)} %copy-done.54, ...), channel_id=1, replica_groups=mesh['dp'=8,'tensor'=4] {'dp','tensor'}, use_global_device_ids=true, to_apply=%region_19.20 | all-reduce | flops 8192 | bytes 65536 | tf_op jit(solution)/shard_map/psum | solution.py:275
  634.0 2.6 add_add_fusion.2
  636.6 88.1 %all-reduce.5.cloned.1.call-done = bf16[256,4,1024]{2,1,0:T(4,128)(2,1)} async-done(((bf16[256,4,1024]{2,1,0:T(4,128)(2,1)}), bf16[256,4,1024]{2,1,0:T(4,128)(2,1)}) %all-reduce.5.cloned.1.call-update) | async-done | bytes 2097168 | tf_op jit(solution)/shard_map/psum | solution.py:275
  724.6 4.8 convert_element_type.199
  (214 shorter events, 46.4 us)
Async XLA Ops:
  7.2 224.8 %copy-start = (bf16[1024,1024]{1,0:T(8,128)(2,1)S(1)}, bf16[1024,1024]{1,0:T(8,128)(2,1)}, u32[]{:S(2)}) copy-start(bf16[1024,1024]{1,0:T(8,128)(2,1)} %param.28) | copy-start | bytes 6291460
  7.2 62.1 %all-gather.5.cloned.1.call-start = ((), (), s32[]{:S(2)}) async-start(), calls=%async_computation.4 | async-start | bytes 2621440 | tf_op jit(solution)/shard_map/all_gather | solution.py:165
  8.6 11.7 %copy-start.45 = (f32[256]{0:T(256)}, f32[256]{0:T(256)S(1)}, u32[]{:S(2)}) copy-start(f32[256]{0:T(256)S(1)} %broadcast_multiply_fusion.1) | copy-start | bytes 3076
  9.9 10.3 %copy-start.47 = (f32[256]{0:T(256)}, f32[256]{0:T(256)S(1)}, u32[]{:S(2)}) copy-start(f32[256]{0:T(256)S(1)} %fusion.67) | copy-start | bytes 3076
  9.9 7.9 %copy-start.30 = (bf16[256,256]{1,0:T(8,128)(2,1)S(1)}, bf16[256,256]{1,0:T(8,128)(2,1)}, u32[]{:S(2)}) copy-start(bf16[256,256]{1,0:T(8,128)(2,1)} %param.16) | copy-start | bytes 393220
  10.0 7.9 %copy-start.49 = (f32[4,1024]{1,0:T(4,128)S(1)}, f32[4,1024]{1,0:T(4,128)}, u32[]{:S(2)}) copy-start(f32[4,1024]{1,0:T(4,128)} %param.24) | copy-start | bytes 49156
  23.5 112.0 %reduce-scatter.5.cloned.1.call-start = ((), (), s32[]{:S(2)}) async-start(), calls=%async_computation.5 | async-start | bytes 2621440 | tf_op jit(solution)/shard_map/reduce_scatter | solution.py:181
  27.1 46.3 %copy-start.28 = (f32[1024,32]{0,1:T(8,128)}, f32[1024,32]{0,1:T(8,128)S(1)}, u32[]{:S(2)}) copy-start(f32[1024,32]{0,1:T(8,128)S(1)} %get-tuple-element.104) | copy-start | bytes 393220
  73.2 12.4 %copy-start.9 = (f32[1024,3,4,64]{0,3,2,1:T(8,128)}, f32[1024,3,4,64]{0,3,2,1:T(8,128)S(1)}, u32[]{:S(2)}) copy-start(f32[1024,3,4,64]{0,3,2,1:T(8,128)S(1)} %fusion.20) | copy-start | bytes 9437188
  73.8 8.1 %copy-start.14 = (bf16[1024,4,32]{0,2,1:T(8,128)(2,1)}, bf16[1024,4,32]{0,2,1:T(8,128)(2,1)S(1)}, u32[]{:S(2)}) copy-start(bf16[1024,4,32]{0,2,1:T(8,128)(2,1)S(1)} %get-tuple-element.102) | copy-start | bytes 786436
  73.8 8.1 %copy-start.16 = (bf16[1024,4,32]{0,2,1:T(8,128)(2,1)}, bf16[1024,4,32]{0,2,1:T(8,128)(2,1)S(1)}, u32[]{:S(2)}) copy-start(bf16[1024,4,32]{0,2,1:T(8,128)(2,1)S(1)} %get-tuple-element.91) | copy-start | bytes 786436
  73.8 8.1 %copy-start.18 = (bf16[1024,4,32]{0,2,1:T(8,128)(2,1)}, bf16[1024,4,32]{0,2,1:T(8,128)(2,1)S(1)}, u32[]{:S(2)}) copy-start(bf16[1024,4,32]{0,2,1:T(8,128)(2,1)S(1)} %get-tuple-element.92) | copy-start | bytes 786436
  89.1 49.1 %copy-start.38 = (f32[1024]{0:T(1024)S(1)}, f32[1024]{0:T(1024)}, u32[]{:S(2)}) copy-start(f32[1024]{0:T(1024)} %param.21) | copy-start | bytes 12292
  89.1 49.1 %copy-start.53 = (f32[1024]{0:T(1024)S(1)}, f32[1024]{0:T(1024)}, u32[]{:S(2)}) copy-start(f32[1024]{0:T(1024)} %param.22) | copy-start | bytes 12292
  92.1 93.7 %all-gather.7.cloned.1.call-start = ((), (), s32[]{:S(2)}) async-start(), calls=%async_computation.6 | async-start | bytes 2621440 | tf_op jit(solution)/shard_map/all_gather | solution.py:191
  138.2 54.2 %copy-start.62 = (f32[256]{0:T(256)}, f32[256]{0:T(256)S(1)}, u32[]{:S(2)}) copy-start(f32[256]{0:T(256)S(1)} %multiply_reduce_fusion.4) | copy-start | bytes 3076
  138.2 54.1 %copy-start.56 = (f32[256]{0:T(256)}, f32[256]{0:T(256)S(1)}, u32[]{:S(2)}) copy-start(f32[256]{0:T(256)S(1)} %fusion.68) | copy-start | bytes 3076
  141.1 90.9 %all-gather.9.cloned.1.call-start = ((), (), s32[]{:S(2)}) async-start(), calls=%async_computation.8 | async-start | bytes 2621440 | tf_op jit(solution)/shard_map/all_gather | solution.py:203
  141.7 153.4 %reduce-scatter.9.cloned.1.call-start = ((), (), s32[]{:S(2)}) async-start(), calls=%async_computation.9 | async-start | bytes 2621440 | tf_op jit(solution)/shard_map/reduce_scatter | solution.py:214
  232.0 15.9 %copy-start.65 = (bf16[1024,1024]{1,0:T(8,128)(2,1)S(1)}, bf16[1024,1024]{1,0:T(8,128)(2,1)}, u32[]{:S(2)}) copy-start(bf16[1024,1024]{1,0:T(8,128)(2,1)} %param.27) | copy-start | bytes 6291460
  251.6 89.4 %reduce-scatter.7.cloned.1.call-start = ((), (), s32[]{:S(2)}) async-start(), calls=%async_computation.7 | async-start | bytes 2621440 | tf_op jit(solution)/shard_map/reduce_scatter | solution.py:195
  257.6 37.5 %copy-start.6 = (bf16[256,1024]{1,0:T(8,128)(2,1)S(1)}, bf16[256,1024]{1,0:T(8,128)(2,1)}, u32[]{:S(2)}) copy-start(bf16[256,1024]{1,0:T(8,128)(2,1)} %reduce-scatter.5.cloned.1.call-done) | copy-start | bytes 1572868
  261.2 37.5 %copy-start.63 = (f32[256]{0:T(256)S(1)}, f32[256]{0:T(256)}, u32[]{:S(2)}) copy-start(f32[256]{0:T(256)} %copy-done.62) | copy-start | bytes 3076
  261.2 79.8 %copy-start.57 = (f32[256]{0:T(256)S(1)}, f32[256]{0:T(256)}, u32[]{:S(2)}) copy-start(f32[256]{0:T(256)} %copy-done.56) | copy-start | bytes 3076
  261.3 82.6 %copy-start.11 = (bf16[256,1024]{1,0:T(8,128)(2,1)S(1)}, bf16[256,1024]{1,0:T(8,128)(2,1)}, u32[]{:S(2)}) copy-start(bf16[256,1024]{1,0:T(8,128)(2,1)} %param.29) | copy-start | bytes 1572868
  261.3 128.4 %all-gather.11.cloned.1.call-start = ((), (), s32[]{:S(2)}) async-start(), calls=%async_computation.10 | async-start | bytes 2621440 | tf_op jit(solution)/shard_map/all_gather | solution.py:229
  298.8 46.4 %copy-start.40 = (f32[4,512]{1,0:T(4,128)S(1)}, f32[4,512]{1,0:T(4,128)}, u32[]{:S(2)}) copy-start(f32[4,512]{1,0:T(4,128)} %copy-done.39) | copy-start | bytes 24580
  298.8 46.4 %copy-start.42 = (f32[4,512]{1,0:T(4,128)S(1)}, f32[4,512]{1,0:T(4,128)}, u32[]{:S(2)}) copy-start(f32[4,512]{1,0:T(4,128)} %copy-done.41) | copy-start | bytes 24580
  298.8 46.4 %copy-start.44 = (f32[4,512]{1,0:T(4,128)S(1)}, f32[4,512]{1,0:T(4,128)}, u32[]{:S(2)}) copy-start(f32[4,512]{1,0:T(4,128)} %copy-done.43) | copy-start | bytes 24580
  343.9 7.5 %copy-start.7 = (f32[256,1024]{1,0:T(8,128)}, f32[256,1024]{1,0:T(8,128)S(1)}, u32[]{:S(2)}) copy-start(f32[256,1024]{1,0:T(8,128)S(1)} %get-tuple-element.81) | copy-start | bytes 3145732
  345.1 185.4 %all-reduce.7.cloned.1.call-start = ((), (), s32[]{:S(2)}) async-start(), calls=%async_computation.13 | async-start | bytes 12582912 | tf_op jit(solution)/shard_map/psum | solution.py:286
  345.2 6.2 copy-start.67
  351.4 38.3 %copy-start.35 = (bf16[256,1024]{1,0:T(8,128)(2,1)S(1)}, bf16[256,1024]{1,0:T(8,128)(2,1)}, u32[]{:S(2)}) copy-start(bf16[256,1024]{1,0:T(8,128)(2,1)} %param.26) | copy-start | bytes 1572868
  392.1 8.1 %slice-start.2 = ((s8[8388608]{0:T(1024)(128)(4,1)}), s8[4194304]{0:T(1024)(128)(4,1)S(1)}, s32[]{:S(2)}) async-start(s8[8388608]{0:T(1024)(128)(4,1)} %bitcast.150), calls=%async_computation.16 | async-start | bytes 8388608
  392.1 8.5 %slice-start.3 = ((s8[8388608]{0:T(1024)(128)(4,1)}), s8[4194304]{0:T(1024)(128)(4,1)S(1)}, s32[]{:S(2)}) async-start(s8[8388608]{0:T(1024)(128)(4,1)} %bitcast.150), calls=%async_computation.17 | async-start | bytes 8388608
  400.2 8.1 %slice-start = ((s8[8388608]{0:T(1024)(128)(4,1)}), s8[4194304]{0:T(1024)(128)(4,1)S(1)}, s32[]{:S(2)}) async-start(s8[8388608]{0:T(1024)(128)(4,1)} %bitcast.148), calls=%async_computation.14 | async-start | bytes 8388608
  400.6 7.6 %slice-start.1 = ((s8[8388608]{0:T(1024)(128)(4,1)}), s8[4194304]{0:T(1024)(128)(4,1)S(1)}, s32[]{:S(2)}) async-start(s8[8388608]{0:T(1024)(128)(4,1)} %bitcast.148), calls=%async_computation.15 | async-start | bytes 8388608
  425.7 150.7 %reduce-scatter.11.cloned.1.call-start = ((), (), s32[]{:S(2)}) async-start(), calls=%async_computation.11 | async-start | bytes 2621440 | tf_op jit(solution)/shard_map/reduce_scatter | solution.py:250
  431.8 292.9 %all-reduce.5.cloned.1.call-start = ((), (), s32[]{:S(2)}) async-start(), calls=%async_computation.12 | async-start | bytes 4194304 | tf_op jit(solution)/shard_map/psum | solution.py:275
  538.5 39.1 %copy-start.37 = (f32[1024]{0:T(1024)S(1)}, f32[1024]{0:T(1024)}, u32[]{:S(2)}) copy-start(f32[1024]{0:T(1024)} %param.19) | copy-start | bytes 12292
  538.5 39.1 %copy-start.46 = (f32[256]{0:T(256)S(1)}, f32[256]{0:T(256)}, u32[]{:S(2)}) copy-start(f32[256]{0:T(256)} %copy-done.45) | copy-start | bytes 3076
  538.5 39.2 %copy-start.48 = (f32[256]{0:T(256)S(1)}, f32[256]{0:T(256)}, u32[]{:S(2)}) copy-start(f32[256]{0:T(256)} %copy-done.47) | copy-start | bytes 3076
  538.5 39.2 %copy-start.51 = (f32[1024]{0:T(1024)S(1)}, f32[1024]{0:T(1024)}, u32[]{:S(2)}) copy-start(f32[1024]{0:T(1024)} %param.20) | copy-start | bytes 12292
  588.0 44.2 %copy-start.61 = (f32[256]{0:T(256)S(1)}, f32[256]{0:T(256)}, u32[]{:S(2)}) copy-start(f32[256]{0:T(256)} %copy-done.60) | copy-start | bytes 3076
  588.0 44.2 %copy-start.10 = (bf16[256,1024]{1,0:T(8,128)(2,1)S(1)}, bf16[256,1024]{1,0:T(8,128)(2,1)}, u32[]{:S(2)}) copy-start(bf16[256,1024]{1,0:T(8,128)(2,1)} %reduce-scatter.11.cloned.1.call-done) | copy-start | bytes 1572868
  588.0 46.0 %copy-start.12 = (bf16[256,1024]{1,0:T(8,128)(2,1)S(1)}, bf16[256,1024]{1,0:T(8,128)(2,1)}, u32[]{:S(2)}) copy-start(bf16[256,1024]{1,0:T(8,128)(2,1)} %param.29) | copy-start | bytes 1572868
  588.0 46.0 %copy-start.59 = (f32[256]{0:T(256)S(1)}, f32[256]{0:T(256)}, u32[]{:S(2)}) copy-start(f32[256]{0:T(256)} %copy-done.58) | copy-start | bytes 3076
  633.9 95.6 %copy-start.1 = (bf16[1024,1024]{1,0:T(8,128)(2,1)S(1)}, bf16[1024,1024]{1,0:T(8,128)(2,1)}, u32[]{:S(2)}) copy-start(bf16[1024,1024]{1,0:T(8,128)(2,1)} %param.28) | copy-start | bytes 6291460
  (37 other events, 115.1 us)
Sparse Core Ops, SparseCore 0:
  23.6 45.5 all-gather.4
  92.2 43.3 reduce-scatter.4
  141.2 44.5 all-gather.6
  187.3 44.6 all-gather.8
  251.7 43.3 reduce-scatter.8
  297.8 43.1 reduce-scatter.6
  345.2 44.4 all-gather.10
  425.8 104.5 all-reduce.6
  532.7 43.6 reduce-scatter.10
  592.8 131.8 all-reduce.4

commit v2 on v0

v2 whole, which is shorter than its diff:
```python
import math

import jax
import jax.numpy as jnp
from jax import lax
from jax.sharding import Mesh
from jax.sharding import PartitionSpec as P

HEAD = 64
F32 = jnp.float32
BF16 = jnp.bfloat16
LEAD = (((0,), (0,)), ((), ()))
TRAIL = (((1,), (1,)), ((), ()))


def product(left, right, dims=(((1,), (0,)), ((), ()))):
    return lax.dot_general(left, right, dims, preferred_element_type=F32)


def norm_parts(values):
    centre = values - jnp.mean(values, axis=-1, keepdims=True)
    spread = jnp.mean(centre * centre, axis=-1, keepdims=True)
    scale = lax.rsqrt(spread + 1e-05)
    return (centre * scale, scale)


def norm_input_back(grads, normed, scale, gain, mod_scale):
    inner = grads * (1.0 + mod_scale) * gain
    return scale * (
        inner
        - jnp.mean(inner, axis=-1, keepdims=True)
        - normed * jnp.mean(inner * normed, axis=-1, keepdims=True)
    )


def rotary_tables(position_list):
    half_size = HEAD // 2
    frequency = jnp.exp(jnp.arange(half_size, dtype=F32) * (-math.log(10000.0) / half_size))
    angles = position_list.astype(F32)[:, None] * frequency[None, :]
    return (jnp.cos(angles)[:, None, :], jnp.sin(angles)[:, None, :])


def rotate(values, cosine_table, sine_table):
    first_half = values[..., : HEAD // 2]
    second_half = values[..., HEAD // 2 :]
    return jnp.concatenate(
        [
            first_half * cosine_table - second_half * sine_table,
            second_half * cosine_table + first_half * sine_table,
        ],
        axis=-1,
    )


def unrotate(grads_in, cosine_table, sine_table):
    return rotate(grads_in, cosine_table, -sine_table)


def masked_scores(query_block, key_rows, segment_block, segments, score_scale):
    scores = (
        jnp.einsum("qhd,khd->hqk", query_block, key_rows, preferred_element_type=F32) * score_scale
    )
    allowed = segment_block[:, None] == segments[None, :]
    return jnp.where(allowed[None], scores, -1e30)


def attend_block(query_block, key_rows, value_rows, segment_block, segments):
    scores = masked_scores(query_block, key_rows, segment_block, segments, 1.0 / math.sqrt(HEAD))
    row_peak = jnp.max(scores, axis=-1, keepdims=True)
    raised = jnp.exp(scores - row_peak)
    row_total = jnp.sum(raised, axis=-1, keepdims=True)
    attention = (raised / row_total).astype(BF16)
    mixed = jnp.einsum("hqk,khd->qhd", attention, value_rows, preferred_element_type=F32)
    return (mixed.astype(BF16), row_peak + jnp.log(row_total))


def attend_back_block(query_block, key_rows, value_rows, segment_block, segments, logsum, grad_block):
    score_scale = 1.0 / math.sqrt(HEAD)
    scores = masked_scores(query_block, key_rows, segment_block, segments, score_scale)
    probability = jnp.exp(scores - logsum)
    attention = probability.astype(BF16)
    value_part = jnp.einsum("hqk,qhd->khd", attention, grad_block, preferred_element_type=F32)
    prob_grad = jnp.einsum("qhd,khd->hqk", grad_block, value_rows, preferred_element_type=F32)
    row_dot = jnp.sum(probability * prob_grad, axis=-1, keepdims=True)
    score_grad = (probability * (prob_grad - row_dot)).astype(BF16)
    query_part = (
        jnp.einsum("hqk,khd->qhd", score_grad, key_rows, preferred_element_type=F32) * score_scale
    )
    key_part = (
        jnp.einsum("hqk,qhd->khd", score_grad, query_block, preferred_element_type=F32)
        * score_scale
    )
    return (query_part, key_part, value_part)


def swap(values, axis_name, bit):
    size = lax.axis_size(axis_name)
    return lax.ppermute(values, axis_name, [(at, at ^ (1 << bit)) for at in range(size)])


def bit_of(axis_name, bit):
    return (lax.axis_index(axis_name) >> bit) & 1


def halve(values, axis_name, bit, dim):
    own = bit_of(axis_name, bit)
    kept = lax.dynamic_index_in_dim(values, own, dim, keepdims=False)
    sent = lax.dynamic_index_in_dim(values, 1 - own, dim, keepdims=False)
    got = swap(sent, axis_name, bit)
    return (kept.astype(F32) + got.astype(F32)).astype(BF16)


def double(values, axis_name, bit, dim):
    own = bit_of(axis_name, bit) == 0
    got = swap(values, axis_name, bit)
    return jnp.stack([jnp.where(own, values, got), jnp.where(own, got, values)], axis=dim)


def plane_scatter(values, order, dim):
    bits = len(order)
    shape = values.shape
    values = values.reshape(shape[:dim] + (2,) * bits + shape[dim + 1 :])
    left = list(range(bits - 1, -1, -1))
    for bit in order:
        values = halve(values, "plane", bit, dim + left.index(bit))
        left.remove(bit)
    return values


def plane_gather(values, order, dim):
    bits = len(order)
    left = []
    for bit in reversed(order):
        left = sorted(left + [bit], reverse=True)
        values = double(values, "plane", bit, dim + left.index(bit))
    shape = values.shape
    return values.reshape(shape[:dim] + (1 << bits,) + shape[dim + bits :])


def tensor_scatter(values):
    size = lax.axis_size("tensor")
    own = lax.axis_index("tensor")
    total = lax.dynamic_index_in_dim(values, own, 0, keepdims=False).astype(F32)
    for hop in range(1, size):
        sent = lax.dynamic_index_in_dim(values, (own + hop) % size, 0, keepdims=False)
        got = lax.ppermute(sent, "tensor", [(at, (at + hop) % size) for at in range(size)])
        total = total + got.astype(F32)
    return total.astype(BF16)


def ring_gather(shard):
    size = lax.axis_size("tensor")
    half = shard.shape[0] // 2
    right, left = [shard[:half]], [shard[half:]]
    for _ in range(size - 1):
        right.append(lax.ppermute(right[-1], "tensor", [(at, (at + 1) % size) for at in range(size)]))
        left.append(lax.ppermute(left[-1], "tensor", [(at, (at - 1) % size) for at in range(size)]))
    return [(right[(size - at) % size], left[at]) for at in range(size)]


def ring_scatter(chunks):
    size = len(chunks)
    half = chunks[0].shape[0] // 2
    right = chunks[size - 1][:half]
    left = chunks[1 % size][half:]
    for step in range(1, size):
        right = lax.ppermute(right, "tensor", [(at, (at + 1) % size) for at in range(size)])
        left = lax.ppermute(left, "tensor", [(at, (at - 1) % size) for at in range(size)])
        right = right.astype(F32) + chunks[size - 1 - step][:half].astype(F32)
        left = left.astype(F32) + chunks[(step + 1) % size][half:].astype(F32)
        if step < size - 1:
            right, left = right.astype(BF16), left.astype(BF16)
    return jnp.concatenate([right, left], axis=0)


def after(values, *others):
    return lax.optimization_barrier((values, others))[0]


def own_first(values, dim):
    size = lax.axis_size("tensor")
    stretch = values.shape[dim] // size
    doubled = jnp.concatenate([values, values], axis=dim)
    return lax.dynamic_slice_in_dim(
        doubled, lax.axis_index("tensor") * stretch, values.shape[dim], dim
    )


def tensor_sum(values):
    size = lax.axis_size("tensor")
    for bit in range(size.bit_length() - 1):
        values = (values.astype(F32) + swap(values, "tensor", bit).astype(F32)).astype(BF16)
    return values


def local(
    tokens,
    time_embed,
    segment_ids,
    positions,
    first_gain,
    first_bias,
    second_gain,
    second_bias,
    time_weight,
    time_bias,
    qkv_weight,
    out_weight,
    up_weight,
    down_weight,
    cotangent,
):
    local_rows, width = tokens.shape
    embed_width = time_embed.shape[1]
    group_rows = segment_ids.shape[1]
    local_width = qkv_weight.shape[2]
    head_local = local_width // HEAD
    hidden_local = up_weight.shape[1]
    half_hidden = hidden_local // 2
    planes = lax.axis_size("plane")
    groups = lax.axis_size("tensor")
    plane_at = lax.axis_index("plane")
    core_at = lax.axis_index("core")
    rising = list(range(planes.bit_length() - 1))
    falling = rising[::-1]

    up_rows = width // planes
    up_piece = lax.dynamic_slice(
        up_weight, (plane_at * up_rows, core_at * half_hidden), (up_rows, half_hidden)
    )
    down_rows = half_hidden // planes
    down_piece = lax.dynamic_slice(
        down_weight, (core_at * half_hidden + plane_at * down_rows, 0), (down_rows, width)
    )
    gathered = ring_gather(jnp.concatenate([tokens, time_embed], axis=1))
    gathered = jnp.concatenate([half for pair in gathered for half in pair], axis=0)
    tokens_all = gathered[:, :width]
    embed_all = gathered[:, width:]
    segments = own_first(segment_ids, 1)[0]
    places = own_first(positions, 1)[0]
    up_all = lax.all_gather(up_piece, ("tensor", "plane"), axis=0, tiled=True)
    up_all = up_all.reshape(groups, width, half_hidden)
    down_all = lax.all_gather(down_piece, ("tensor", "plane"), axis=0, tiled=True)
    down_all = down_all.reshape(groups, half_hidden, width)

    time_flat = time_weight.reshape(embed_width, 4 * width)
    bias_flat = time_bias.reshape(4 * width)

    tokens_float = tokens_all.astype(F32)
    normed_all, _ = norm_parts(tokens_float)
    mod_all = product(embed_all, time_flat[:, : 2 * width]) + bias_flat[: 2 * width]
    base_all = normed_all * first_gain + first_bias
    scale_all = 1.0 + mod_all[:, :width]
    first_all = (base_all * scale_all + mod_all[:, width:]).astype(BF16)

    qkv_flat = qkv_weight.reshape(width, 3 * local_width)
    projected = product(first_all, qkv_flat).reshape(group_rows, 3, head_local, HEAD)
    cosine_table, sine_table = rotary_tables(places)
    queries = rotate(projected[:, 0], cosine_table, sine_table).astype(BF16)
    keys_all = rotate(projected[:, 1], cosine_table, sine_table).astype(BF16)
    values_all = projected[:, 2].astype(BF16)
    spans = [slice(at * local_rows, (at + 1) * local_rows) for at in range(groups)]
    forward_blocks = [
        attend_block(queries[span], keys_all, values_all, segments[span], segments)
        for span in spans
    ]
    mixed_blocks = [pair[0].reshape(local_rows, local_width) for pair in forward_blocks]
    attended = ring_scatter([product(block, out_weight).astype(BF16) for block in mixed_blocks])
    own_tokens = tokens.astype(F32)
    residual = own_tokens + attended

    mod_own = product(time_embed, time_flat) + bias_flat
    second_base_normed, second_scale = norm_parts(residual)
    second_base = second_base_normed * second_gain + second_bias
    mod_two = mod_own[:, 2 * width : 3 * width]
    second_normed = (second_base * (1.0 + mod_two) + mod_own[:, 3 * width :]).astype(BF16)
    second_both = jnp.concatenate([second_normed, swap(second_normed, "core", 0)], axis=0)
    grad_both = jnp.concatenate([cotangent, swap(cotangent, "core", 0)], axis=0)

    branch_part = 0.0
    second_part = 0.0
    up_parts = []
    down_parts = []
    for at in range(groups):
        hidden = product(second_both, up_all[at])
        tail = 0.5 * (1.0 + lax.erf(hidden * math.sqrt(0.5)))
        slope = tail + hidden * jnp.exp(hidden * hidden * -0.5) * (1.0 / math.sqrt(2.0 * math.pi))
        active = (hidden * tail).astype(BF16)
        branch_part = branch_part + product(active, down_all[at])
        down_parts.append(product(active, grad_both, LEAD).astype(BF16))
        hidden_grad = (product(grad_both, down_all[at], TRAIL) * slope).astype(BF16)
        second_part = second_part + product(hidden_grad, up_all[at], TRAIL)
        up_parts.append(product(second_both, hidden_grad, LEAD).astype(BF16))
    second_grad = second_part[:local_rows] + swap(second_part[local_rows:], "core", 0)
    branch = branch_part[:local_rows] + swap(branch_part[local_rows:], "core", 0)
    result = (residual + branch).astype(BF16)

    residual_grad = cotangent.astype(F32) + norm_input_back(
        second_grad, second_base_normed, second_scale, second_gain, mod_two
    )
    second_weighted = second_grad * (1.0 + mod_two)
    scale_two_grad = second_grad * second_base

    down_stack = jnp.stack(down_parts).reshape(groups, planes, down_rows, width)
    up_stack = jnp.stack(up_parts).reshape(groups, planes, up_rows, half_hidden)
    down_sum = plane_scatter(down_stack, rising, 1)
    up_sum = plane_scatter(up_stack, falling, 1)

    attended_halves = ring_gather(residual_grad.astype(BF16))
    attended_blocks = [jnp.concatenate(pair, axis=0) for pair in attended_halves]
    attended_all = jnp.concatenate(attended_blocks, axis=0)
    out_weight_grad = product(jnp.concatenate(mixed_blocks, axis=0), attended_all, LEAD).astype(BF16)
    back_blocks = [
        attend_back_block(
            queries[span],
            keys_all,
            values_all,
            segments[span],
            segments,
            pair[1],
            product(block, out_weight, TRAIL).astype(BF16).reshape(local_rows, head_local, HEAD),
        )
        for span, pair, block in zip(spans, forward_blocks, attended_blocks)
    ]
    query_grad = jnp.concatenate([triple[0] for triple in back_blocks], axis=0)
    key_grad = sum(triple[1] for triple in back_blocks)
    value_grad = sum(triple[2] for triple in back_blocks)
    query_pre = unrotate(query_grad, cosine_table, sine_table)
    key_pre = unrotate(key_grad, cosine_table, sine_table)
    projected_grad = jnp.stack([query_pre, key_pre, value_grad], axis=1)
    projected_grad = projected_grad.astype(BF16).reshape(group_rows, 3 * local_width)
    projected_grad = after(projected_grad, down_sum, up_sum)
    first_part = product(projected_grad, qkv_flat, TRAIL)
    first_half = first_part.astype(BF16)
    first_grad = ring_scatter([first_half[span] for span in spans])
    qkv_grad = product(first_all, projected_grad, LEAD).astype(BF16)

    down_own = tensor_scatter(down_sum)
    up_own = tensor_scatter(up_sum)
    down_half = plane_gather(down_own, rising, 0).reshape(half_hidden, width)
    up_half = plane_gather(up_own, falling, 0).reshape(width, half_hidden)
    down_summed = double(down_half, "core", 0, 0).reshape(hidden_local, width).astype(F32)
    up_summed = double(up_half, "core", 0, 1).reshape(width, hidden_local).astype(F32)

    scale_one_part = first_part * base_all
    weighted = first_part * scale_all
    small = jnp.stack(
        [
            jnp.sum(weighted * normed_all, axis=0),
            jnp.sum(weighted, axis=0),
            jnp.sum(second_weighted * second_base_normed, axis=0),
            jnp.sum(second_weighted, axis=0),
            jnp.sum(scale_one_part, axis=0),
            jnp.sum(first_part, axis=0),
            jnp.sum(scale_two_grad, axis=0),
            jnp.sum(second_grad, axis=0),
        ]
    )
    time_parts = [
        product(embed_all, scale_one_part.astype(BF16), LEAD).astype(BF16),
        product(embed_all, first_half, LEAD).astype(BF16),
        product(time_embed, scale_two_grad.astype(BF16), LEAD).astype(BF16),
        product(time_embed, second_grad.astype(BF16), LEAD).astype(BF16),
    ]
    lanes = 8 * width // embed_width
    small_rows = jnp.pad(small.reshape(embed_width, lanes), ((0, 0), (0, -lanes % 128))).astype(BF16)
    blocks = width // embed_width
    qkv_blocks = [qkv_grad[at * embed_width : (at + 1) * embed_width] for at in range(blocks)]
    shared_pack = jnp.concatenate(time_parts + [small_rows], axis=1)
    share_width = shared_pack.shape[1]
    pack = jnp.concatenate([shared_pack, out_weight_grad] + qkv_blocks, axis=1)
    pack = halve(pack.reshape(2, embed_width // 2, -1), "core", 0, 0)
    pack = pack.reshape(planes, embed_width // (2 * planes), -1)
    pack = plane_scatter(pack, rising, 0)
    pack = jnp.concatenate([tensor_sum(pack[:, :share_width]), pack[:, share_width:]], axis=1)
    pack = plane_gather(pack, rising, 0).reshape(embed_width // 2, -1)
    pack = double(pack, "core", 0, 0).reshape(embed_width, -1)
    time_weight_grad = pack[:, : 4 * width].astype(F32).reshape(embed_width, 4, width)
    small = pack[:, 4 * width : 4 * width + lanes].astype(F32).reshape(8, width)
    at = share_width
    out_summed = pack[:, at : at + width].astype(F32)
    at += width
    qkv_summed = jnp.concatenate(
        [
            pack[:, at + 3 * local_width * block : at + 3 * local_width * (block + 1)]
            for block in range(blocks)
        ],
        axis=0,
    )
    qkv_summed = qkv_summed.astype(F32).reshape(width, 3, local_width)

    own_normed, own_scale = norm_parts(own_tokens)
    input_grad = residual_grad + norm_input_back(
        first_grad, own_normed, own_scale, first_gain, mod_own[:, :width]
    )
    return (
        result,
        input_grad,
        small[0],
        small[1],
        small[2],
        small[3],
        time_weight_grad,
        small[4:],
        qkv_summed,
        out_summed,
        up_summed,
        down_summed,
    )


def solution(mesh):
    whole, tensor = mesh.devices.shape
    finer = Mesh(mesh.devices.reshape(whole // 2, 2, tensor), ("plane", "core", "tensor"))
    rows = P(("plane", "core", "tensor"), None)
    group = P(("plane", "core"), None)
    return jax.shard_map(
        local,
        mesh=finer,
        in_specs=(
            rows,
            rows,
            group,
            group,
            P(),
            P(),
            P(),
            P(),
            P(),
            P(),
            P(None, None, "tensor"),
            P("tensor", None),
            P(None, "tensor"),
            P("tensor", None),
            rows,
        ),
        out_specs=(
            rows,
            rows,
            P(),
            P(),
            P(),
            P(),
            P(),
            P(),
            P(None, None, "tensor"),
            P("tensor", None),
            P(None, "tensor"),
            P("tensor", None),
        ),
        check_vma=False,
    )
```

time: 926 us -> 574 us (0.62)
  waiting for transfers between devices: 678 us -> 239 us
  starting transfers between devices: 1.57 us -> 77.7 us
  blocking collectives: 40.6 us -> 0 us
  local copies, waits for them, and re-layouts: 48.3 us -> 78.3 us
  other arithmetic: 41.8 us -> 61.4 us
    psum x2 -> x0, waiting for transfers between devices: 260 us -> none  [the longest x1 146 us: local(): lax.psum((first_gain_grad, first_bias_grad, second_gain_grad, second_bias...]
    reduce_scatter x4 -> x0, waiting for transfers between devices: 248 us -> none  [the longest x1 77.5 us: local(): lax.psum_scatter(jnp.dot(picked, out_weight, preferred_element_type=jnp.f...]
    ppermute x0 -> x52, waiting for transfers between devices: none -> 221 us  [the longest x22 82.6 us: swap(): lax.ppermute(values, axis_name, [(at, at ^ 1 << bit) for at in range(size)])]
    all_gather x4 -> x2, waiting for transfers between devices: 169 us -> 18.2 us  [the longest x1 18.2 us: local(): lax.all_gather(down_piece, ('tensor', 'plane'), axis=0, tiled=True)]
    ppermute x0 -> x52, starting transfers between devices: none -> 77.6 us  [the longest x22 36 us: swap(): lax.ppermute(values, axis_name, [(at, at ^ 1 << bit) for at in range(size)])]
    psum x1 -> x0, blocking collectives: 40.6 us -> none  [local(): lax.psum((first_gain_grad, first_bias_grad, second_gain_grad, second_bias...]
    convert_element_type x9 -> x27, other arithmetic: 19 us -> 29.1 us  [the longest x7 12.1 us: halve(): return (kept.astype(F32) + got.astype(F32)).astype(BF16)]
    unnamed x159 -> x222, local copies, waits for them, and re-layouts: 34.6 us -> 44.3 us
  transfers between devices with their start and end apart: 10 -> 54, of which waited for: 10 -> 32; matrix products, arithmetic and copies ran while one was open for 7% -> 27% of each run, Pallas kernels for 0% -> 0%
where the time goes in v2:
time: 574 us; the launch traced here: 563 us
  waiting for transfers between devices  239 us (42%)
  matrix products  91 us (16%)
  local copies, waits for them, and re-layouts  78.3 us (14%)
  starting transfers between devices  77.7 us (14%)
  other arithmetic  61.4 us (11%)
  between operations  16.1 us (3%)
    ppermute x22, waiting for transfers between devices, swap(): lax.ppermute(values, axis_name, [(at, at ^ 1 << bit) for at in range(size)])  82.6 us
    dot_general x42, matrix products, product(): return lax.dot_general(left, right, dims, preferred_element_type=F32)  63.6 us
    unnamed x222, local copies, waits for them, and re-layouts  44.3 us
    ppermute x6, waiting for transfers between devices, tensor_scatter(): lax.ppermute(sent, 'tensor', [(at, (at + hop) % size) for at in range(siz...  43.7 us
    ppermute x22, starting transfers between devices, swap(): lax.ppermute(values, axis_name, [(at, at ^ 1 << bit) for at in range(size)])  36 us
    ppermute x6, waiting for transfers between devices, ring_scatter(): lax.ppermute(right, 'tensor', [(at, (at + 1) % size) for at in range(size)])  33.9 us
    ppermute x6, waiting for transfers between devices, ring_gather(): lax.ppermute(left[-1], 'tensor', [(at, (at - 1) % size) for at in range(s...  27.6 us
    ppermute x6, waiting for transfers between devices, ring_gather(): lax.ppermute(right[-1], 'tensor', [(at, (at + 1) % size) for at in range(...  23.6 us
  transfers between devices with their start and end apart: 54, of which 32 were waited for; matrix products, arithmetic and copies ran while one was open for 27% of the time, Pallas kernels for 0%

profile of v2, /device:TPU:21, one launch (start us, length us, event | category | flops | bytes accessed | tf_op | source)
XLA Modules:
  0.0 563.3 jit_solution(12663478947984656495)
XLA Ops:
  29.3 6.4 %collective-permute-done.3 = bf16[128,1280]{1,0:T(8,128)(2,1)} collective-permute-done((bf16[128,1280]{1,0:T(8,128)(2,1)}, bf16[128,1280]{1,0:T(8,128)(2,1)}, u32[]{:S(2)}, u32[]{:S(2)}) %collective-permute-start.3) | collective-permute-done | bytes 327712 | tf_op jit(solution)/shard_map/ppermute | solution.py:157
  35.6 3.4 collective-permute-start.4
  39.1 4.5 collective-permute-done.1
  46.3 12.6 %collective-permute-done.4 = bf16[128,1280]{1,0:T(8,128)(2,1)S(1)} collective-permute-done((bf16[128,1280]{1,0:T(8,128)(2,1)}, bf16[128,1280]{1,0:T(8,128)(2,1)S(1)}, u32[]{:S(2)}, u32[]{:S(2)}) %collective-permute-start.4) | collective-permute-done | bytes 327712 | tf_op jit(solution)/shard_map/ppermute | solution.py:157
  58.9 5.7 %collective-permute-start.5 = (bf16[128,1280]{1,0:T(8,128)(2,1)S(1)}, bf16[128,1280]{1,0:T(8,128)(2,1)S(1)}, u32[]{:S(2)}, u32[]{:S(2)}) collective-permute-start(bf16[128,1280]{1,0:T(8,128)(2,1)S(1)} %collective-permute-done.4), channel_id=1, source_target_pairs={{0,3},{1,0},{2,1},{3,2},{4,7},{5,4},{6,5},{7,6},{8,11},{9,8},{10,9... | collective-permute-start | bytes 983048 | tf_op jit(solution)/shard_map/ppermute | solution.py:157
  64.7 3.6 collective-permute-done.2
  79.7 3.9 fusion.11
  108.0 4.9 collective-permute-start.7
  114.0 13.6 %collective-permute-done.7 = bf16[128,1024]{1,0:T(8,128)(2,1)S(1)} collective-permute-done((bf16[128,1024]{1,0:T(8,128)(2,1)S(1)}, bf16[128,1024]{1,0:T(8,128)(2,1)S(1)}, u32[]{:S(2)}, u32[]{:S(2)}) %collective-permute-start.7) | collective-permute-done | bytes 262176 | tf_op jit(solution)/shard_map/ppermute | solution.py:167
  130.6 16.3 %collective-permute-done.8 = bf16[128,1024]{1,0:T(8,128)(2,1)S(1)} collective-permute-done((bf16[128,1024]{1,0:T(8,128)(2,1)S(1)}, bf16[128,1024]{1,0:T(8,128)(2,1)S(1)}, u32[]{:S(2)}, u32[]{:S(2)}) %collective-permute-start.8) | collective-permute-done | bytes 262176 | tf_op jit(solution)/shard_map/ppermute | solution.py:167
  148.9 8.4 %collective-permute-start.12 = (bf16[256,1024]{1,0:T(8,128)(2,1)S(1)}, bf16[256,1024]{1,0:T(8,128)(2,1)}, u32[]{:S(2)}, u32[]{:S(2)}) collective-permute-start(bf16[256,1024]{1,0:T(8,128)(2,1)S(1)} %fusion.102), channel_id=1, source_target_pairs={{0,4},{4,0},{1,5},{5,1},{2,6},{6,2},{3,7},{7,3},{8,12},{12,8},{9,1... | collective-permute-start | bytes 1572872 | tf_op jit(solution)/shard_map/ppermute | solution.py:98
  161.8 3.5 multiply_convert_fusion.5
  165.3 2.9 multiply_convert_fusion.7
  168.2 3.0 multiply_convert_fusion.6
  173.0 18.2 %all-gather.5.cloned.1.call-done = bf16[2048,1024]{1,0:T(8,128)(2,1)} async-done(((bf16[128,1024]{1,0:T(8,128)(2,1)}), bf16[2048,1024]{1,0:T(8,128)(2,1)}) %all-gather.5.cloned.1.call-update) | async-done | bytes 4194320 | tf_op jit(solution)/shard_map/all_gather | solution.py:243
  191.1 3.0 fusion.61
  224.8 3.5 multiply_reduce_fusion.4
  238.2 7.6 %collective-permute-done.16 = bf16[128,1024]{1,0:T(8,128)(2,1)S(1)} collective-permute-done((bf16[128,1024]{1,0:T(8,128)(2,1)S(1)}, bf16[128,1024]{1,0:T(8,128)(2,1)S(1)}, u32[]{:S(2)}, u32[]{:S(2)}) %collective-permute-start.16) | collective-permute-done | bytes 262176 | tf_op jit(solution)/shard_map/ppermute | solution.py:156
  248.9 7.5 %collective-permute-done.17 = bf16[128,1024]{1,0:T(8,128)(2,1)S(1)} collective-permute-done((bf16[128,1024]{1,0:T(8,128)(2,1)S(1)}, bf16[128,1024]{1,0:T(8,128)(2,1)S(1)}, u32[]{:S(2)}, u32[]{:S(2)}) %collective-permute-start.17) | collective-permute-done | bytes 262176 | tf_op jit(solution)/shard_map/ppermute | solution.py:156
  263.8 4.7 collective-permute-done.21
  296.0 16.9 %collective-permute-done.23 = bf16[4,128,1024]{2,1,0:T(8,128)(2,1)S(1)} collective-permute-done((bf16[4,128,1024]{2,1,0:T(8,128)(2,1)S(1)}, bf16[4,128,1024]{2,1,0:T(8,128)(2,1)S(1)}, u32[]{:S(2)}, u32[]{:S(2)}) %collective-permute-start.23) | collective-permute-done | bytes 1048608 | tf_op jit(solution)/shard_map/ppermute | solution.py:98
  316.6 3.5 convolution_convert_fusion
  320.1 4.6 fusion.57
  324.7 3.9 fusion.65
  334.3 3.2 fusion.69
  340.7 3.1 dynamic-slice_bitcast_fusion
  343.8 3.1 collective-permute-start.32
  346.9 4.2 collective-permute-done.32
  357.4 23.8 %collective-permute-done.33 = bf16[2,32,8320]{2,1,0:T(8,128)(2,1)} collective-permute-done((bf16[2,32,8320]{2,1,0:T(8,128)(2,1)}, bf16[2,32,8320]{2,1,0:T(8,128)(2,1)}, u32[]{:S(2)}, u32[]{:S(2)}) %collective-permute-start.33) | collective-permute-done | bytes 1064992 | tf_op jit(solution)/shard_map/ppermute | solution.py:98
  391.0 4.5 collective-permute-done.34
  400.3 4.0 collective-permute-done.42
  407.0 13.8 %collective-permute-done.41 = bf16[256,512]{1,0:T(8,128)(2,1)S(1)} collective-permute-done((bf16[256,512]{1,0:T(8,128)(2,1)S(1)}, bf16[256,512]{1,0:T(8,128)(2,1)S(1)}, u32[]{:S(2)}, u32[]{:S(2)}) %collective-permute-start.41) | collective-permute-done | bytes 262176 | tf_op jit(solution)/shard_map/ppermute | solution.py:146
  420.7 5.1 collective-permute-done.40
  428.0 20.8 %collective-permute-done.47 = bf16[128,1024]{1,0:T(8,128)(2,1)S(1)} collective-permute-done((bf16[128,1024]{1,0:T(8,128)(2,1)S(1)}, bf16[128,1024]{1,0:T(8,128)(2,1)S(1)}, u32[]{:S(2)}, u32[]{:S(2)}) %collective-permute-start.47) | collective-permute-done | bytes 262176 | tf_op jit(solution)/shard_map/ppermute | solution.py:146
  448.8 3.5 collective-permute-start.36
  452.8 4.0 collective-permute-done.27
  456.8 9.1 %collective-permute-done.30 = bf16[128,1024]{1,0:T(8,128)(2,1)S(1)} collective-permute-done((bf16[128,1024]{1,0:T(8,128)(2,1)S(1)}, bf16[128,1024]{1,0:T(8,128)(2,1)S(1)}, u32[]{:S(2)}, u32[]{:S(2)}) %collective-permute-start.30) | collective-permute-done | bytes 262176 | tf_op jit(solution)/shard_map/ppermute | solution.py:168
  468.6 3.1 collective-permute-done.36
  474.0 9.6 %collective-permute-done.37 = bf16[32,8320]{1,0:T(8,128)(2,1)S(1)} collective-permute-done((bf16[32,8320]{1,0:T(8,128)(2,1)S(1)}, bf16[32,8320]{1,0:T(8,128)(2,1)S(1)}, u32[]{:S(2)}, u32[]{:S(2)}) %collective-permute-start.37) | collective-permute-done | bytes 532512 | tf_op jit(solution)/shard_map/ppermute | solution.py:98
  486.1 8.7 %collective-permute-done.44 = bf16[2,256,512]{2,1,0:T(8,128)(2,1)S(1)} collective-permute-done((bf16[2,256,512]{2,1,0:T(8,128)(2,1)S(1)}, bf16[2,256,512]{2,1,0:T(8,128)(2,1)S(1)}, u32[]{:S(2)}, u32[]{:S(2)}) %collective-permute-start.44) | collective-permute-done | bytes 524320 | tf_op jit(solution)/shard_map/ppermute | solution.py:98
  495.0 2.9 collective-permute-start.45
  497.9 7.7 %collective-permute-done.38 = bf16[2,32,8320]{2,1,0:T(8,128)(2,1)S(1)} collective-permute-done((bf16[2,32,8320]{2,1,0:T(8,128)(2,1)S(1)}, bf16[2,32,8320]{2,1,0:T(8,128)(2,1)S(1)}, u32[]{:S(2)}, u32[]{:S(2)}) %collective-permute-start.38) | collective-permute-done | bytes 1064992 | tf_op jit(solution)/shard_map/ppermute | solution.py:98
  507.6 5.2 collective-permute-start.39
  516.9 5.3 copy.81
  522.3 5.3 copy.84
  541.3 6.0 %reshape.487 = f32[256,4,1024]{2,1,0:T(4,128)} reshape(f32[256,4096]{1,0:T(8,128)} %slice_convert_fusion) | data formatting | bytes 8388608 | tf_op jit(solution)/shard_map/reshape | solution.py:378
  549.5 3.2 maximum_convert_fusion.1
  552.7 3.5 copy.83
  (488 shorter events, 218.5 us)
Async XLA Ops:
  7.2 151.8 %all-gather.3.cloned.1.call-start = ((), (), s32[]{:S(2)}) async-start(), calls=%async_computation | async-start | bytes 4456448 | tf_op jit(solution)/shard_map/all_gather | solution.py:241
  9.2 182.0 %all-gather.5.cloned.1.call-start = ((), (), s32[]{:S(2)}) async-start(), calls=%async_computation.1 | async-start | bytes 4456448 | tf_op jit(solution)/shard_map/all_gather | solution.py:243
  15.0 20.6 %collective-permute-start.3 = (bf16[128,1280]{1,0:T(8,128)(2,1)}, bf16[128,1280]{1,0:T(8,128)(2,1)}, u32[]{:S(2)}, u32[]{:S(2)}) collective-permute-start(bf16[128,1280]{1,0:T(8,128)(2,1)} %get-tuple-element.116), channel_id=1, source_target_pairs={{0,3},{1,0},{2,1},{3,2},{4,7},{5,4},{6,5},{7,6},{8,11},{9,8},{10,9... | collective-permute-start | bytes 983048 | tf_op jit(solution)/shard_map/ppermute | solution.py:157
  15.2 29.2 %collective-permute-start.14 = (bf16[256,1024]{1,0:T(8,128)(2,1)S(1)}, bf16[256,1024]{1,0:T(8,128)(2,1)}, u32[]{:S(2)}, u32[]{:S(2)}) collective-permute-start(bf16[256,1024]{1,0:T(8,128)(2,1)S(1)} %copy-done.30), channel_id=1, source_target_pairs={{0,4},{4,0},{1,5},{5,1},{2,6},{6,2},{3,7},{7,3},{8,12},{12,8},{9,1... | collective-permute-start | bytes 1572872 | tf_op jit(solution)/shard_map/ppermute | solution.py:98
  23.9 19.7 %collective-permute-start.1 = (bf16[128,1280]{1,0:T(8,128)(2,1)}, bf16[128,1280]{1,0:T(8,128)(2,1)S(1)}, u32[]{:S(2)}, u32[]{:S(2)}) collective-permute-start(bf16[128,1280]{1,0:T(8,128)(2,1)} %collective-permute-done), channel_id=1, source_target_pairs={{0,1},{1,2},{2,3},{3,0},{4,5},{5,6},{6,7},{7,4},{8,9},{9,10},{10,1... | collective-permute-start | bytes 983048 | tf_op jit(solution)/shard_map/ppermute | solution.py:156
  35.6 23.3 %collective-permute-start.4 = (bf16[128,1280]{1,0:T(8,128)(2,1)}, bf16[128,1280]{1,0:T(8,128)(2,1)S(1)}, u32[]{:S(2)}, u32[]{:S(2)}) collective-permute-start(bf16[128,1280]{1,0:T(8,128)(2,1)} %collective-permute-done.3), channel_id=1, source_target_pairs={{0,3},{1,0},{2,1},{3,2},{4,7},{5,4},{6,5},{7,6},{8,11},{9,8},{10,9... | collective-permute-start | bytes 983048 | tf_op jit(solution)/shard_map/ppermute | solution.py:157
  43.5 24.7 %collective-permute-start.2 = (bf16[128,1280]{1,0:T(8,128)(2,1)S(1)}, bf16[128,1280]{1,0:T(8,128)(2,1)S(1)}, u32[]{:S(2)}, u32[]{:S(2)}) collective-permute-start(bf16[128,1280]{1,0:T(8,128)(2,1)S(1)} %collective-permute-done.1), channel_id=1, source_target_pairs={{0,1},{1,2},{2,3},{3,0},{4,5},{5,6},{6,7},{7,4},{8,9},{9,10},{10,1... | collective-permute-start | bytes 983048 | tf_op jit(solution)/shard_map/ppermute | solution.py:156
  58.9 15.4 %collective-permute-start.5 = (bf16[128,1280]{1,0:T(8,128)(2,1)S(1)}, bf16[128,1280]{1,0:T(8,128)(2,1)S(1)}, u32[]{:S(2)}, u32[]{:S(2)}) collective-permute-start(bf16[128,1280]{1,0:T(8,128)(2,1)S(1)} %collective-permute-done.4), channel_id=1, source_target_pairs={{0,3},{1,0},{2,1},{3,2},{4,7},{5,4},{6,5},{7,6},{8,11},{9,8},{10,9... | collective-permute-start | bytes 983048 | tf_op jit(solution)/shard_map/ppermute | solution.py:157
  95.1 12.7 %collective-permute-start.6 = (bf16[128,1024]{1,0:T(8,128)(2,1)S(1)}, bf16[128,1024]{1,0:T(8,128)(2,1)S(1)}, u32[]{:S(2)}, u32[]{:S(2)}) collective-permute-start(bf16[128,1024]{1,0:T(8,128)(2,1)S(1)} %slice.382), channel_id=1, source_target_pairs={{0,1},{1,2},{2,3},{3,0},{4,5},{5,6},{6,7},{7,4},{8,9},{9,10},{10,1... | collective-permute-start | bytes 786440 | tf_op jit(solution)/shard_map/ppermute | solution.py:167
  108.0 19.6 %collective-permute-start.7 = (bf16[128,1024]{1,0:T(8,128)(2,1)S(1)}, bf16[128,1024]{1,0:T(8,128)(2,1)S(1)}, u32[]{:S(2)}, u32[]{:S(2)}) collective-permute-start(bf16[128,1024]{1,0:T(8,128)(2,1)S(1)} %get-tuple-element.127), channel_id=1, source_target_pairs={{0,1},{1,2},{2,3},{3,0},{4,5},{5,6},{6,7},{7,4},{8,9},{9,10},{10,1... | collective-permute-start | bytes 786440 | tf_op jit(solution)/shard_map/ppermute | solution.py:167
  112.9 17.1 %collective-permute-start.10 = (bf16[128,1024]{1,0:T(8,128)(2,1)S(1)}, bf16[128,1024]{1,0:T(8,128)(2,1)S(1)}, u32[]{:S(2)}, u32[]{:S(2)}) collective-permute-start(bf16[128,1024]{1,0:T(8,128)(2,1)S(1)} %get-tuple-element.128), channel_id=1, source_target_pairs={{0,3},{1,0},{2,1},{3,2},{4,7},{5,4},{6,5},{7,6},{8,11},{9,8},{10,9... | collective-permute-start | bytes 786440 | tf_op jit(solution)/shard_map/ppermute | solution.py:168
  127.7 19.2 %collective-permute-start.8 = (bf16[128,1024]{1,0:T(8,128)(2,1)S(1)}, bf16[128,1024]{1,0:T(8,128)(2,1)S(1)}, u32[]{:S(2)}, u32[]{:S(2)}) collective-permute-start(bf16[128,1024]{1,0:T(8,128)(2,1)S(1)} %add_convert_fusion.10), channel_id=1, source_target_pairs={{0,1},{1,2},{2,3},{3,0},{4,5},{5,6},{6,7},{7,4},{8,9},{9,10},{10,1... | collective-permute-start | bytes 786440 | tf_op jit(solution)/shard_map/ppermute | solution.py:167
  130.1 16.8 %collective-permute-start.11 = (bf16[128,1024]{1,0:T(8,128)(2,1)S(1)}, bf16[128,1024]{1,0:T(8,128)(2,1)S(1)}, u32[]{:S(2)}, u32[]{:S(2)}) collective-permute-start(bf16[128,1024]{1,0:T(8,128)(2,1)S(1)} %add_convert_fusion.8), channel_id=1, source_target_pairs={{0,3},{1,0},{2,1},{3,2},{4,7},{5,4},{6,5},{7,6},{8,11},{9,8},{10,9... | collective-permute-start | bytes 786440 | tf_op jit(solution)/shard_map/ppermute | solution.py:168
  203.0 21.8 %collective-permute-start.15 = (f32[256,1024]{1,0:T(8,128)S(1)}, f32[256,1024]{1,0:T(8,128)S(1)}, u32[]{:S(2)}, u32[]{:S(2)}) collective-permute-start(f32[256,1024]{1,0:T(8,128)S(1)} %slice.410), channel_id=1, source_target_pairs={{0,4},{4,0},{1,5},{5,1},{2,6},{6,2},{3,7},{7,3},{8,12},{12,8},{9,1... | collective-permute-start | bytes 3145736 | tf_op jit(solution)/shard_map/ppermute | solution.py:98
  210.0 14.8 %collective-permute-start.13 = (f32[256,1024]{1,0:T(8,128)S(1)}, f32[256,1024]{1,0:T(8,128)S(1)}, u32[]{:S(2)}, u32[]{:S(2)}) collective-permute-start(f32[256,1024]{1,0:T(8,128)S(1)} %slice.408), channel_id=1, source_target_pairs={{0,4},{4,0},{1,5},{5,1},{2,6},{6,2},{3,7},{7,3},{8,12},{12,8},{9,1... | collective-permute-start | bytes 3145736 | tf_op jit(solution)/shard_map/ppermute | solution.py:98
  214.2 72.5 %collective-permute-start.22 = (bf16[4,2,128,1024]{3,2,0,1:T(8,128)(2,1)}, bf16[4,2,128,1024]{3,2,0,1:T(8,128)(2,1)}, u32[]{:S(2)}, u32[]{:S(2)}) collective-permute-start(bf16[4,2,128,1024]{3,2,0,1:T(8,128)(2,1)} %bitcast.267), channel_id=1, source_target_pairs={{0,8},{8,0},{16,24},{24,16},{1,9},{9,1},{17,25},{25,17},{2,10},{10... | collective-permute-start | bytes 6291464 | tf_op jit(solution)/shard_map/ppermute | solution.py:98
  223.7 66.7 %collective-permute-start.24 = (bf16[4,2,256,512]{3,2,1,0:T(8,128)(2,1)}, bf16[4,2,256,512]{3,2,1,0:T(8,128)(2,1)}, u32[]{:S(2)}, u32[]{:S(2)}) collective-permute-start(bf16[4,2,256,512]{3,2,1,0:T(8,128)(2,1)} %dynamic-slice_bitcast_fusion.1), channel_id=1, source_target_pairs={{0,16},{8,24},{16,0},{24,8},{1,17},{9,25},{17,1},{25,9},{2,18},{10... | collective-permute-start | bytes 6291464 | tf_op jit(solution)/shard_map/ppermute | solution.py:98
  231.1 14.7 %collective-permute-start.16 = (bf16[128,1024]{1,0:T(8,128)(2,1)S(1)}, bf16[128,1024]{1,0:T(8,128)(2,1)S(1)}, u32[]{:S(2)}, u32[]{:S(2)}) collective-permute-start(bf16[128,1024]{1,0:T(8,128)(2,1)S(1)} %get-tuple-element.122), channel_id=1, source_target_pairs={{0,1},{1,2},{2,3},{3,0},{4,5},{5,6},{6,7},{7,4},{8,9},{9,10},{10,1... | collective-permute-start | bytes 786440 | tf_op jit(solution)/shard_map/ppermute | solution.py:156
  237.5 11.5 %collective-permute-start.20 = (bf16[128,1024]{1,0:T(8,128)(2,1)S(1)}, bf16[128,1024]{1,0:T(8,128)(2,1)S(1)}, u32[]{:S(2)}, u32[]{:S(2)}) collective-permute-start(bf16[128,1024]{1,0:T(8,128)(2,1)S(1)} %collective-permute-done.19), channel_id=1, source_target_pairs={{0,3},{1,0},{2,1},{3,2},{4,7},{5,4},{6,5},{7,6},{8,11},{9,8},{10,9... | collective-permute-start | bytes 786440 | tf_op jit(solution)/shard_map/ppermute | solution.py:157
  245.8 10.7 %collective-permute-start.17 = (bf16[128,1024]{1,0:T(8,128)(2,1)S(1)}, bf16[128,1024]{1,0:T(8,128)(2,1)S(1)}, u32[]{:S(2)}, u32[]{:S(2)}) collective-permute-start(bf16[128,1024]{1,0:T(8,128)(2,1)S(1)} %collective-permute-done.16), channel_id=1, source_target_pairs={{0,1},{1,2},{2,3},{3,0},{4,5},{5,6},{6,7},{7,4},{8,9},{9,10},{10,1... | collective-permute-start | bytes 786440 | tf_op jit(solution)/shard_map/ppermute | solution.py:156
  260.9 12.6 %collective-permute-start.18 = (bf16[128,1024]{1,0:T(8,128)(2,1)S(1)}, bf16[128,1024]{1,0:T(8,128)(2,1)S(1)}, u32[]{:S(2)}, u32[]{:S(2)}) collective-permute-start(bf16[128,1024]{1,0:T(8,128)(2,1)S(1)} %collective-permute-done.17), channel_id=1, source_target_pairs={{0,1},{1,2},{2,3},{3,0},{4,5},{5,6},{6,7},{7,4},{8,9},{9,10},{10,1... | collective-permute-start | bytes 786440 | tf_op jit(solution)/shard_map/ppermute | solution.py:156
  290.0 22.8 %collective-permute-start.23 = (bf16[4,128,1024]{2,1,0:T(8,128)(2,1)S(1)}, bf16[4,128,1024]{2,1,0:T(8,128)(2,1)S(1)}, u32[]{:S(2)}, u32[]{:S(2)}) collective-permute-start(bf16[4,128,1024]{2,1,0:T(8,128)(2,1)S(1)} %dynamic-slice_bitcast_fusion.4), channel_id=1, source_target_pairs={{0,16},{8,24},{16,0},{24,8},{1,17},{9,25},{17,1},{25,9},{2,18},{10... | collective-permute-start | bytes 3145736 | tf_op jit(solution)/shard_map/ppermute | solution.py:98
  292.8 22.6 %collective-permute-start.25 = (bf16[4,256,512]{2,1,0:T(8,128)(2,1)S(1)}, bf16[4,256,512]{2,1,0:T(8,128)(2,1)S(1)}, u32[]{:S(2)}, u32[]{:S(2)}) collective-permute-start(bf16[4,256,512]{2,1,0:T(8,128)(2,1)S(1)} %dynamic-slice_bitcast_fusion.3), channel_id=1, source_target_pairs={{0,8},{8,0},{16,24},{24,16},{1,9},{9,1},{17,25},{25,17},{2,10},{10... | collective-permute-start | bytes 3145736 | tf_op jit(solution)/shard_map/ppermute | solution.py:98
  356.2 25.0 %collective-permute-start.33 = (bf16[2,32,8320]{2,1,0:T(8,128)(2,1)}, bf16[2,32,8320]{2,1,0:T(8,128)(2,1)}, u32[]{:S(2)}, u32[]{:S(2)}) collective-permute-start(bf16[2,32,8320]{2,1,0:T(8,128)(2,1)} %dynamic-slice_bitcast_fusion.2), channel_id=1, source_target_pairs={{0,8},{8,0},{16,24},{24,16},{1,9},{9,1},{17,25},{25,17},{2,10},{10... | collective-permute-start | bytes 3194888 | tf_op jit(solution)/shard_map/ppermute | solution.py:98
  383.0 12.5 %collective-permute-start.34 = (bf16[32,8320]{1,0:T(8,128)(2,1)S(1)}, bf16[32,8320]{1,0:T(8,128)(2,1)S(1)}, u32[]{:S(2)}, u32[]{:S(2)}) collective-permute-start(bf16[32,8320]{1,0:T(8,128)(2,1)S(1)} %dynamic-slice_bitcast_fusion.5), channel_id=1, source_target_pairs={{0,16},{8,24},{16,0},{24,8},{1,17},{9,25},{17,1},{25,9},{2,18},{10... | collective-permute-start | bytes 1597448 | tf_op jit(solution)/shard_map/ppermute | solution.py:98
  384.3 14.2 %collective-permute-start.26 = (bf16[128,1024]{1,0:T(8,128)(2,1)S(1)}, bf16[128,1024]{1,0:T(8,128)(2,1)S(1)}, u32[]{:S(2)}, u32[]{:S(2)}) collective-permute-start(bf16[128,1024]{1,0:T(8,128)(2,1)S(1)} %get-tuple-element.93), channel_id=1, source_target_pairs={{0,1},{1,2},{2,3},{3,0},{4,5},{5,6},{6,7},{7,4},{8,9},{9,10},{10,1... | collective-permute-start | bytes 786440 | tf_op jit(solution)/shard_map/ppermute | solution.py:167
  387.2 11.5 %collective-permute-start.29 = (bf16[128,1024]{1,0:T(8,128)(2,1)S(1)}, bf16[128,1024]{1,0:T(8,128)(2,1)S(1)}, u32[]{:S(2)}, u32[]{:S(2)}) collective-permute-start(bf16[128,1024]{1,0:T(8,128)(2,1)S(1)} %get-tuple-element.94), channel_id=1, source_target_pairs={{0,3},{1,0},{2,1},{3,2},{4,7},{5,4},{6,5},{7,6},{8,11},{9,8},{10,9... | collective-permute-start | bytes 786440 | tf_op jit(solution)/shard_map/ppermute | solution.py:168
  387.3 17.0 %collective-permute-start.42 = (bf16[256,512]{1,0:T(8,128)(2,1)S(1)}, bf16[256,512]{1,0:T(8,128)(2,1)S(1)}, u32[]{:S(2)}, u32[]{:S(2)}) collective-permute-start(bf16[256,512]{1,0:T(8,128)(2,1)S(1)} %get-tuple-element.113), channel_id=1, source_target_pairs={{0,3},{1,0},{2,1},{3,2},{4,7},{5,4},{6,5},{7,6},{8,11},{9,8},{10,9... | collective-permute-start | bytes 786440 | tf_op jit(solution)/shard_map/ppermute | solution.py:146
  388.6 32.1 %collective-permute-start.41 = (bf16[256,512]{1,0:T(8,128)(2,1)S(1)}, bf16[256,512]{1,0:T(8,128)(2,1)S(1)}, u32[]{:S(2)}, u32[]{:S(2)}) collective-permute-start(bf16[256,512]{1,0:T(8,128)(2,1)S(1)} %get-tuple-element.114), channel_id=1, source_target_pairs={{0,2},{1,3},{2,0},{3,1},{4,6},{5,7},{6,4},{7,5},{8,10},{9,11},{10,... | collective-permute-start | bytes 786440 | tf_op jit(solution)/shard_map/ppermute | solution.py:146
  395.5 30.3 %collective-permute-start.40 = (bf16[256,512]{1,0:T(8,128)(2,1)S(1)}, bf16[256,512]{1,0:T(8,128)(2,1)S(1)}, u32[]{:S(2)}, u32[]{:S(2)}) collective-permute-start(bf16[256,512]{1,0:T(8,128)(2,1)S(1)} %get-tuple-element.112), channel_id=1, source_target_pairs={{0,1},{1,2},{2,3},{3,0},{4,5},{5,6},{6,7},{7,4},{8,9},{9,10},{10,1... | collective-permute-start | bytes 786440 | tf_op jit(solution)/shard_map/ppermute | solution.py:146
  398.5 29.0 %collective-permute-start.48 = (bf16[128,1024]{1,0:T(8,128)(2,1)S(1)}, bf16[128,1024]{1,0:T(8,128)(2,1)S(1)}, u32[]{:S(2)}, u32[]{:S(2)}) collective-permute-start(bf16[128,1024]{1,0:T(8,128)(2,1)S(1)} %get-tuple-element.108), channel_id=1, source_target_pairs={{0,3},{1,0},{2,1},{3,2},{4,7},{5,4},{6,5},{7,6},{8,11},{9,8},{10,9... | collective-permute-start | bytes 786440 | tf_op jit(solution)/shard_map/ppermute | solution.py:146
  398.7 28.7 %collective-permute-start.35 = (bf16[32,4224]{1,0:T(8,128)(2,1)S(1)}, bf16[32,4224]{1,0:T(8,128)(2,1)S(1)}, u32[]{:S(2)}, u32[]{:S(2)}) collective-permute-start(bf16[32,4224]{1,0:T(8,128)(2,1)S(1)} %slice.430), channel_id=1, source_target_pairs={{0,1},{1,0},{2,3},{3,2},{4,5},{5,4},{6,7},{7,6},{8,9},{9,8},{10,11... | collective-permute-start | bytes 811016 | tf_op jit(solution)/shard_map/ppermute | solution.py:98
  404.3 44.4 %collective-permute-start.47 = (bf16[128,1024]{1,0:T(8,128)(2,1)S(1)}, bf16[128,1024]{1,0:T(8,128)(2,1)S(1)}, u32[]{:S(2)}, u32[]{:S(2)}) collective-permute-start(bf16[128,1024]{1,0:T(8,128)(2,1)S(1)} %get-tuple-element.109), channel_id=1, source_target_pairs={{0,2},{1,3},{2,0},{3,1},{4,6},{5,7},{6,4},{7,5},{8,10},{9,11},{10,... | collective-permute-start | bytes 786440 | tf_op jit(solution)/shard_map/ppermute | solution.py:146
  420.7 31.5 %collective-permute-start.46 = (bf16[128,1024]{1,0:T(8,128)(2,1)S(1)}, bf16[128,1024]{1,0:T(8,128)(2,1)S(1)}, u32[]{:S(2)}, u32[]{:S(2)}) collective-permute-start(bf16[128,1024]{1,0:T(8,128)(2,1)S(1)} %get-tuple-element.107), channel_id=1, source_target_pairs={{0,1},{1,2},{2,3},{3,0},{4,5},{5,6},{6,7},{7,4},{8,9},{9,10},{10,1... | collective-permute-start | bytes 786440 | tf_op jit(solution)/shard_map/ppermute | solution.py:146
  425.8 31.0 %collective-permute-start.27 = (bf16[128,1024]{1,0:T(8,128)(2,1)S(1)}, bf16[128,1024]{1,0:T(8,128)(2,1)S(1)}, u32[]{:S(2)}, u32[]{:S(2)}) collective-permute-start(bf16[128,1024]{1,0:T(8,128)(2,1)S(1)} %get-tuple-element.91), channel_id=1, source_target_pairs={{0,1},{1,2},{2,3},{3,0},{4,5},{5,6},{6,7},{7,4},{8,9},{9,10},{10,1... | collective-permute-start | bytes 786440 | tf_op jit(solution)/shard_map/ppermute | solution.py:167
  427.3 38.5 %collective-permute-start.30 = (bf16[128,1024]{1,0:T(8,128)(2,1)S(1)}, bf16[128,1024]{1,0:T(8,128)(2,1)S(1)}, u32[]{:S(2)}, u32[]{:S(2)}) collective-permute-start(bf16[128,1024]{1,0:T(8,128)(2,1)S(1)} %get-tuple-element.92), channel_id=1, source_target_pairs={{0,3},{1,0},{2,1},{3,2},{4,7},{5,4},{6,5},{7,6},{8,11},{9,8},{10,9... | collective-permute-start | bytes 786440 | tf_op jit(solution)/shard_map/ppermute | solution.py:168
  427.6 44.6 %collective-permute-start.43 = (bf16[256,512]{1,0:T(8,128)(2,1)S(1)}, bf16[256,512]{1,0:T(8,128)(2,1)S(1)}, u32[]{:S(2)}, u32[]{:S(2)}) collective-permute-start(bf16[256,512]{1,0:T(8,128)(2,1)S(1)} %fusion.154), channel_id=1, source_target_pairs={{0,8},{8,0},{16,24},{24,16},{1,9},{9,1},{17,25},{25,17},{2,10},{10... | collective-permute-start | bytes 786440 | tf_op jit(solution)/shard_map/ppermute | solution.py:98
  448.8 23.0 %collective-permute-start.36 = (bf16[32,4224]{1,0:T(8,128)(2,1)S(1)}, bf16[32,4224]{1,0:T(8,128)(2,1)S(1)}, u32[]{:S(2)}, u32[]{:S(2)}) collective-permute-start(bf16[32,4224]{1,0:T(8,128)(2,1)S(1)} %add_convert_fusion.1), channel_id=1, source_target_pairs={{0,2},{1,3},{2,0},{3,1},{4,6},{5,7},{6,4},{7,5},{8,10},{9,11},{10,... | collective-permute-start | bytes 811016 | tf_op jit(solution)/shard_map/ppermute | solution.py:98
  452.4 21.1 %collective-permute-start.49 = (bf16[128,1024]{1,0:T(8,128)(2,1)S(1)}, bf16[128,1024]{1,0:T(8,128)(2,1)S(1)}, u32[]{:S(2)}, u32[]{:S(2)}) collective-permute-start(bf16[128,1024]{1,0:T(8,128)(2,1)S(1)} %fusion.151), channel_id=1, source_target_pairs={{0,16},{8,24},{16,0},{24,8},{1,17},{9,25},{17,1},{25,9},{2,18},{10... | collective-permute-start | bytes 786440 | tf_op jit(solution)/shard_map/ppermute | solution.py:98
  466.1 18.1 %collective-permute-start.28 = (bf16[128,1024]{1,0:T(8,128)(2,1)S(1)}, bf16[128,1024]{1,0:T(8,128)(2,1)S(1)}, u32[]{:S(2)}, u32[]{:S(2)}) collective-permute-start(bf16[128,1024]{1,0:T(8,128)(2,1)S(1)} %get-tuple-element.89), channel_id=1, source_target_pairs={{0,1},{1,2},{2,3},{3,0},{4,5},{5,6},{6,7},{7,4},{8,9},{9,10},{10,1... | collective-permute-start | bytes 786440 | tf_op jit(solution)/shard_map/ppermute | solution.py:167
  466.1 18.1 %collective-permute-start.31 = (bf16[128,1024]{1,0:T(8,128)(2,1)S(1)}, bf16[128,1024]{1,0:T(8,128)(2,1)S(1)}, u32[]{:S(2)}, u32[]{:S(2)}) collective-permute-start(bf16[128,1024]{1,0:T(8,128)(2,1)S(1)} %get-tuple-element.90), channel_id=1, source_target_pairs={{0,3},{1,0},{2,1},{3,2},{4,7},{5,4},{6,5},{7,6},{8,11},{9,8},{10,9... | collective-permute-start | bytes 786440 | tf_op jit(solution)/shard_map/ppermute | solution.py:168
  471.8 11.7 %collective-permute-start.37 = (bf16[32,8320]{1,0:T(8,128)(2,1)S(1)}, bf16[32,8320]{1,0:T(8,128)(2,1)S(1)}, u32[]{:S(2)}, u32[]{:S(2)}) collective-permute-start(bf16[32,8320]{1,0:T(8,128)(2,1)S(1)} %pad_maximum_fusion.11), channel_id=1, source_target_pairs={{0,16},{8,24},{16,0},{24,8},{1,17},{9,25},{17,1},{25,9},{2,18},{10... | collective-permute-start | bytes 1597448 | tf_op jit(solution)/shard_map/ppermute | solution.py:98
  472.3 22.5 %collective-permute-start.44 = (bf16[2,256,512]{2,1,0:T(8,128)(2,1)S(1)}, bf16[2,256,512]{2,1,0:T(8,128)(2,1)S(1)}, u32[]{:S(2)}, u32[]{:S(2)}) collective-permute-start(bf16[2,256,512]{2,1,0:T(8,128)(2,1)S(1)} %pad_maximum_fusion.13), channel_id=1, source_target_pairs={{0,16},{8,24},{16,0},{24,8},{1,17},{9,25},{17,1},{25,9},{2,18},{10... | collective-permute-start | bytes 1572872 | tf_op jit(solution)/shard_map/ppermute | solution.py:98
  473.6 39.2 %collective-permute-start.50 = (bf16[2,128,1024]{2,1,0:T(8,128)(2,1)S(1)}, bf16[2,128,1024]{2,1,0:T(8,128)(2,1)S(1)}, u32[]{:S(2)}, u32[]{:S(2)}) collective-permute-start(bf16[2,128,1024]{2,1,0:T(8,128)(2,1)S(1)} %pad_maximum_fusion.14), channel_id=1, source_target_pairs={{0,8},{8,0},{16,24},{24,16},{1,9},{9,1},{17,25},{25,17},{2,10},{10... | collective-permute-start | bytes 1572872 | tf_op jit(solution)/shard_map/ppermute | solution.py:98
  483.9 21.8 %collective-permute-start.38 = (bf16[2,32,8320]{2,1,0:T(8,128)(2,1)S(1)}, bf16[2,32,8320]{2,1,0:T(8,128)(2,1)S(1)}, u32[]{:S(2)}, u32[]{:S(2)}) collective-permute-start(bf16[2,32,8320]{2,1,0:T(8,128)(2,1)S(1)} %pad_maximum_fusion.6), channel_id=1, source_target_pairs={{0,8},{8,0},{16,24},{24,16},{1,9},{9,1},{17,25},{25,17},{2,10},{10... | collective-permute-start | bytes 3194888 | tf_op jit(solution)/shard_map/ppermute | solution.py:98
  495.0 19.5 %collective-permute-start.45 = (bf16[1024,512]{1,0:T(8,128)(2,1)S(1)}, bf16[1024,512]{1,0:T(8,128)(2,1)S(1)}, u32[]{:S(2)}, u32[]{:S(2)}) collective-permute-start(bf16[1024,512]{1,0:T(8,128)(2,1)S(1)} %bitcast.283), channel_id=1, source_target_pairs={{0,4},{4,0},{1,5},{5,1},{2,6},{6,2},{3,7},{7,3},{8,12},{12,8},{9,1... | collective-permute-start | bytes 3145736 | tf_op jit(solution)/shard_map/ppermute | solution.py:98
  507.6 24.2 %collective-permute-start.39 = (bf16[128,8320]{1,0:T(8,128)(2,1)}, bf16[128,8320]{1,0:T(8,128)(2,1)}, u32[]{:S(2)}, u32[]{:S(2)}) collective-permute-start(bf16[128,8320]{1,0:T(8,128)(2,1)} %bitcast.70), channel_id=1, source_target_pairs={{0,4},{4,0},{1,5},{5,1},{2,6},{6,2},{3,7},{7,3},{8,12},{12,8},{9,1... | collective-permute-start | bytes 6389768 | tf_op jit(solution)/shard_map/ppermute | solution.py:98
  513.0 14.6 %collective-permute-start.51 = (bf16[512,1024]{1,0:T(8,128)(2,1)S(1)}, bf16[512,1024]{1,0:T(8,128)(2,1)}, u32[]{:S(2)}, u32[]{:S(2)}) collective-permute-start(bf16[512,1024]{1,0:T(8,128)(2,1)S(1)} %bitcast.284), channel_id=1, source_target_pairs={{0,4},{4,0},{1,5},{5,1},{2,6},{6,2},{3,7},{7,3},{8,12},{12,8},{9,1... | collective-permute-start | bytes 3145736 | tf_op jit(solution)/shard_map/ppermute | solution.py:98
  (104 other events, 640.7 us)
Sparse Core Ops, SparseCore 0:
  11.4 91.1 all-gather.2
  105.4 85.7 all-gather.4

commit v3 on v2

v3 whole, which is shorter than its diff:
```python
import functools
import math

import jax
import jax.numpy as jnp
from jax import lax
from jax.experimental import pallas as pl
from jax.experimental.pallas import tpu as pltpu
from jax.sharding import Mesh
from jax.sharding import PartitionSpec as P

HEAD = 64
F32 = jnp.float32
BF16 = jnp.bfloat16
LEAD = (((0,), (0,)), ((), ()))
TRAIL = (((1,), (1,)), ((), ()))


def product(left, right, dims=(((1,), (0,)), ((), ()))):
    return lax.dot_general(left, right, dims, preferred_element_type=F32)


def norm_parts(values):
    centre = values - jnp.mean(values, axis=-1, keepdims=True)
    spread = jnp.mean(centre * centre, axis=-1, keepdims=True)
    scale = lax.rsqrt(spread + 1e-05)
    return (centre * scale, scale)


def norm_input_back(grads, normed, scale, gain, mod_scale):
    inner = grads * (1.0 + mod_scale) * gain
    return scale * (
        inner
        - jnp.mean(inner, axis=-1, keepdims=True)
        - normed * jnp.mean(inner * normed, axis=-1, keepdims=True)
    )


def rotary_tables(places, lanes):
    half_size = HEAD // 2
    lane = jnp.arange(lanes)
    frequency = jnp.exp((lane % half_size).astype(F32) * (-math.log(10000.0) / half_size))
    angles = places.astype(F32)[:, None] * frequency[None, :]
    sign = jnp.where(lane % HEAD < half_size, -1.0, 1.0)
    return (jnp.cos(angles), jnp.sin(angles) * sign[None, :])


def kept_out(*arrays):
    return tuple(pltpu.with_memory_space_constraint(each, pltpu.HBM) for each in arrays)


def block_of(shape, *place):
    return pl.BlockSpec(shape, lambda *_: place)


def whole(*shape):
    return pl.BlockSpec(shape, lambda *_: (0,) * len(shape))


def limits(megabytes):
    return pltpu.CompilerParams(vmem_limit_bytes=megabytes << 20)


def partner(values):
    lanes = values.shape[1]
    lane = lax.broadcasted_iota(jnp.int32, values.shape, 1)
    above = pltpu.roll(values, lanes - HEAD // 2, 1)
    below = pltpu.roll(values, HEAD // 2, 1)
    return jnp.where(lane % HEAD < HEAD // 2, above, below)


def widened(table, lanes):
    return jnp.concatenate([table] * (lanes // table.shape[1]), axis=1)


def turned(values, cosine, sine):
    return values * widened(cosine, values.shape[1]) + partner(values) * widened(sine, values.shape[1])


def entry_kernel(
    *refs, count
):
    halves, refs = refs[: 2 * count], refs[2 * count :]
    cosine_ref, sine_ref, time_ref, bias_ref, gain_ref, shift_ref, weight_ref = refs[:7]
    tokens_ref, first_ref, query_ref, key_ref, value_ref = refs[-5:]
    rows = jnp.concatenate([halves[0][...], halves[1][...]], axis=0)
    for at in range(1, count):
        other = jnp.concatenate([halves[2 * at][...], halves[2 * at + 1][...]], axis=0)
        rows = jnp.where(pl.program_id(0) == at, other, rows)
    tokens_ref[...] = rows
    width = gain_ref.shape[1]
    mod = product(rows[:, width:], time_ref[...]) + bias_ref[...]
    normed, _ = norm_parts(rows[:, :width].astype(F32))
    base = normed * gain_ref[...] + shift_ref[...]
    first = (base * (1.0 + mod[:, :width]) + mod[:, width:]).astype(BF16)
    first_ref[...] = first
    cosine, sine = cosine_ref[...], sine_ref[...]
    query_ref[...] = turned(product(first, weight_ref[0]), cosine, sine).astype(BF16)
    key_ref[...] = turned(product(first, weight_ref[1]), cosine, sine).astype(BF16)
    value_ref[...] = product(first, weight_ref[2]).astype(BF16)


def entry(halves, tables, time_flat, bias, gain, shift, weight, places, groups, before):
    half, both = halves[0].shape
    count = len(places)
    apart = places[-1] - places[0]
    rows = 2 * half
    width = gain.shape[1]
    part = weight.shape[2]
    lanes = tables[0].shape[1]
    widths = (both, width, part, part, part)
    table = pl.BlockSpec((rows, lanes), lambda i: (places[0] + i * apart, 0))
    inputs = (*halves, *kept_out(*tables, time_flat, bias, gain, shift, weight))
    return pl.pallas_call(
        functools.partial(entry_kernel, count=count),
        grid=(count,),
        in_specs=[whole(half, both)] * (2 * count)
        + [table, table]
        + [block_of((both - width, 2 * width), 0, 0), block_of((1, 2 * width), 0, 0)]
        + [whole(*each.shape) for each in (gain, shift, weight)]
        + [pl.BlockSpec(memory_space=pl.ANY)] * len(before),
        out_specs=[pl.BlockSpec((rows, each), lambda i: (places[0] + i * apart, 0)) for each in widths],
        out_shape=[pltpu.HBM((rows * groups, each), BF16) for each in widths],
        input_output_aliases={len(inputs) + at: at for at in range(len(before))},
        compiler_params=limits(16),
        cost_estimate=pl.CostEstimate(
            flops=2 * rows * width * 4 * part + 4 * rows * width * (both - width),
            bytes_accessed=8 * rows * width + 6 * width * part,
            transcendentals=rows,
        ),
    )(*inputs, *kept_out(*before))


def head_lanes(values, head):
    pair = values[:, head // 2 * 2 * HEAD : (head // 2 + 1) * 2 * HEAD]
    lane = lax.broadcasted_iota(jnp.int32, pair.shape, 1)
    return jnp.where(lane // HEAD == head % 2, pair, jnp.zeros_like(pair))


def pair_lanes(values, head):
    return values[:, head // 2 * 2 * HEAD : (head // 2 + 1) * 2 * HEAD]


def attend_kernel(query_ref, key_ref, value_ref, own_ref, all_ref, out_ref, mixed_ref, logsum_ref, part_ref):
    queries, keys, values = query_ref[...], key_ref[...], value_ref[...]
    allowed = all_ref[...] == own_ref[...]
    scale = 1.0 / math.sqrt(HEAD)
    pairs = []
    for head in range(queries.shape[1] // HEAD):
        scores = product(pair_lanes(keys, head), head_lanes(queries, head), TRAIL) * scale
        scores = jnp.where(allowed, scores, -1e30)
        peak = jnp.max(scores, axis=0, keepdims=True)
        raised = jnp.exp(scores - peak)
        total = jnp.sum(raised, axis=0, keepdims=True)
        attention = (raised / total).astype(BF16)
        logsum_ref[head : head + 1, :] = peak + jnp.log(total)
        mixed = product(attention, pair_lanes(values, head), LEAD)
        if head % 2 == 0:
            pairs.append(mixed)
        else:
            lane = lax.broadcasted_iota(jnp.int32, mixed.shape, 1)
            pairs[-1] = jnp.where(lane < HEAD, pairs[-1], mixed)
    mixed = jnp.concatenate(pairs, axis=1).astype(BF16)
    mixed_ref[...] = mixed
    part_ref[...] = product(mixed, out_ref[...]).astype(BF16)


def attend(queries, keys, values, own_segments, all_segments, out_weight, place, rows):
    seq, part = keys.shape
    width = out_weight.shape[1]
    heads = part // HEAD
    return pl.pallas_call(
        attend_kernel,
        grid=(1,),
        in_specs=[
            pl.BlockSpec((rows, part), lambda i: (place, 0)),
            whole(seq, part),
            whole(seq, part),
            pl.BlockSpec((1, rows), lambda i: (0, place)),
            whole(seq, 1),
            whole(part, width),
        ],
        out_specs=[whole(rows, part), whole(heads, rows), whole(rows, width)],
        out_shape=[
            pltpu.HBM((rows, part), BF16),
            pltpu.HBM((heads, rows), F32),
            jax.ShapeDtypeStruct((rows, width), BF16),
        ],
        compiler_params=limits(16),
        cost_estimate=pl.CostEstimate(
            flops=4 * rows * seq * part + 2 * rows * part * width,
            bytes_accessed=4 * seq * part + 4 * rows * width,
            transcendentals=rows * seq * heads,
        ),
    )(queries, keys, values, own_segments, all_segments, out_weight)


def attend_back_kernel(
    query_ref, key_ref, value_ref, own_ref, all_ref, out_ref, cosine_ref, sine_ref, *refs, count
):
    halves, logsum_refs, (grad_ref, key_grad_ref, value_grad_ref) = (
        refs[: 2 * count],
        refs[2 * count : 3 * count],
        refs[3 * count :],
    )
    step = pl.program_id(0)
    queries, keys, values = query_ref[...], key_ref[...], value_ref[...]
    incoming = jnp.concatenate([halves[0][...], halves[1][...]], axis=0)
    logsums = logsum_refs[0][...]
    for at in range(1, count):
        other = jnp.concatenate([halves[2 * at][...], halves[2 * at + 1][...]], axis=0)
        incoming = jnp.where(step == at, other, incoming)
        logsums = jnp.where(step == at, logsum_refs[at][...], logsums)
    mixed_grad = product(incoming, out_ref[...], TRAIL).astype(BF16)
    allowed = all_ref[...] == own_ref[...]
    scale = 1.0 / math.sqrt(HEAD)
    query_pairs, key_pairs, value_pairs = [], [], []
    for head in range(queries.shape[1] // HEAD):
        query, grad = head_lanes(queries, head), head_lanes(mixed_grad, head)
        scores = product(pair_lanes(keys, head), query, TRAIL) * scale
        scores = jnp.where(allowed, scores, -1e30)
        probability = jnp.exp(scores - logsums[head : head + 1, :])
        prob_grad = product(pair_lanes(values, head), grad, TRAIL)
        row_dot = jnp.sum(probability * prob_grad, axis=0, keepdims=True)
        score_grad = (probability * (prob_grad - row_dot)).astype(BF16)
        value_part = product(probability.astype(BF16), grad)
        key_part = product(score_grad, query)
        query_part = product(score_grad, head_lanes(keys, head), LEAD)
        if head % 2 == 0:
            query_pairs.append(query_part)
            key_pairs.append(key_part)
            value_pairs.append(value_part)
        else:
            query_pairs[-1] += query_part
            key_pairs[-1] += key_part
            value_pairs[-1] += value_part
    query_grad = jnp.concatenate(query_pairs, axis=1) * scale
    key_grad = jnp.concatenate(key_pairs, axis=1) * scale
    value_grad = jnp.concatenate(value_pairs, axis=1)
    grad_ref[...] = turned(query_grad, cosine_ref[...], -sine_ref[...]).astype(BF16)

    @pl.when(step == 0)
    def _():
        key_grad_ref[...] = key_grad
        value_grad_ref[...] = value_grad

    @pl.when(step > 0)
    def _():
        key_grad_ref[...] += key_grad
        value_grad_ref[...] += value_grad


def attend_back(halves, queries, keys, values, logsums, own_segments, all_segments, out_weight, tables, places):
    seq, part = keys.shape
    heads, rows = logsums[0].shape
    width = out_weight.shape[1]
    count = len(places)
    apart = places[-1] - places[0]
    shard = pl.BlockSpec((rows, part), lambda i: (places[0] + i * apart, 0))
    table = pl.BlockSpec((rows, tables[0].shape[1]), lambda i: (places[0] + i * apart, 0))
    constants = (own_segments, all_segments, out_weight, *tables)
    return pl.pallas_call(
        functools.partial(attend_back_kernel, count=count),
        grid=(count,),
        in_specs=[
            shard,
            whole(seq, part),
            whole(seq, part),
            pl.BlockSpec((1, rows), lambda i: (0, places[0] + i * apart)),
            whole(seq, 1),
            whole(part, width),
            table,
            table,
        ]
        + [whole(rows // 2, width)] * (2 * count)
        + [whole(heads, rows)] * count,
        out_specs=[
            pl.BlockSpec((rows, part), lambda i: (i, 0)),
            whole(seq, part),
            whole(seq, part),
        ],
        out_shape=[
            pltpu.HBM((count * rows, part), BF16),
            pltpu.HBM((seq, part), F32),
            pltpu.HBM((seq, part), F32),
        ],
        compiler_params=limits(32),
        cost_estimate=pl.CostEstimate(
            flops=10 * count * rows * seq * part + 2 * count * rows * part * width,
            bytes_accessed=16 * seq * part,
            transcendentals=count * rows * seq * heads,
        ),
    )(queries, keys, values, *kept_out(*constants), *halves, *kept_out(*logsums))


def exit_kernel(
    place_ref, cosine_ref, sine_ref, tokens_ref, first_ref, *refs, groups, calls
):
    shards = list(refs[:-18])
    lengths = (groups, calls, calls, groups, groups, groups)
    query_refs, key_refs, value_refs, mixed_refs, top_refs, bottom_refs = (
        [shards.pop(0) for _ in range(length)] for length in lengths
    )
    (
        scale_two_ref, shift_two_ref, small_two_ref, own_embed_ref, time_ref, bias_ref, gain_ref, shift_ref, weight_ref,
        first_grad_ref, time_kept_ref, time_sent_ref, weight_kept_ref, weight_sent_ref,
        weight_sum, time_sum, small_sum, out_sum,
    ) = refs[-18:]
    step = pl.program_id(0)
    width = gain_ref.shape[1]
    key_grad = sum(ref[...] for ref in key_refs)
    key_grad = turned(key_grad, cosine_ref[...], -sine_ref[...]).astype(BF16)

    def this(refs):
        values = refs[0][...]
        for at in range(1, len(refs)):
            values = jnp.where(step == at, refs[at][...], values)
        return values

    incoming = jnp.concatenate([this(top_refs), this(bottom_refs)], axis=0)
    out_part = product(this(mixed_refs), incoming, LEAD)
    grads = (this(query_refs), key_grad, sum(ref[...] for ref in value_refs).astype(BF16))
    first_grad = sum(product(grad, weight_ref[at], TRAIL) for at, grad in enumerate(grads))
    first_half = first_grad.astype(BF16)
    first_grad_ref[...] = first_half
    first = first_ref[...]
    weight_parts = [product(first, grad, LEAD) for grad in grads]
    rows = tokens_ref[...]
    embed = rows[:, width:]
    factor = 1.0 + product(embed, time_ref[...]) + bias_ref[...]
    normed, _ = norm_parts(rows[:, :width].astype(F32))
    base = normed * gain_ref[...] + shift_ref[...]
    scale_grad = first_grad * base
    weighted = first_grad * factor
    both = jnp.concatenate([scale_grad.astype(BF16), first_half], axis=1)
    time_part = product(embed, both, LEAD)
    small = jnp.concatenate(
        [
            jnp.sum(each, axis=0, keepdims=True)
            for each in (weighted * normed, weighted, scale_grad, first_grad)
        ],
        axis=0,
    )

    @pl.when(step == 0)
    def _():
        for at, part in enumerate(weight_parts):
            weight_sum[at] = part
        time_sum[...] = time_part
        out_sum[...] = out_part
        small_sum[:4] = small
        small_sum[4:] = small_two_ref[...]

    @pl.when(step > 0)
    def _():
        for at, part in enumerate(weight_parts):
            weight_sum[at] += part
        time_sum[...] += time_part
        out_sum[...] += out_part
        small_sum[:4] += small

    @pl.when(step == pl.num_programs(0) - 1)
    def _():
        one = place_ref[0] == 1
        half = time_kept_ref.shape[0]

        def put(kept_ref, sent_ref, at, values):
            values = values.astype(BF16)
            columns = slice(at, at + values.shape[1])
            kept_ref[:, columns] = jnp.where(one, values[half:], values[:half])
            sent_ref[:, columns] = jnp.where(one, values[:half], values[half:])

        put(time_kept_ref, time_sent_ref, 0, time_sum[...])
        own_embed = own_embed_ref[...]
        put(time_kept_ref, time_sent_ref, 2 * width, product(own_embed, scale_two_ref[...], LEAD))
        put(time_kept_ref, time_sent_ref, 3 * width, product(own_embed, shift_two_ref[...], LEAD))
        smalls = small_sum[...]
        smalls = jnp.concatenate(
            [smalls[:, at : at + 128] for at in range(0, width, 128)]
            + [jnp.zeros((2 * half - width // 16, 128), F32)],
            axis=0,
        )
        put(time_kept_ref, time_sent_ref, 4 * width, smalls)
        part = weight_sum.shape[2]
        for at in range(3):
            for row in range(0, width, 2 * half):
                column = (at * width + row) // (2 * half) * part
                put(weight_kept_ref, weight_sent_ref, column, weight_sum[at, row : row + 2 * half])
        put(weight_kept_ref, weight_sent_ref, 3 * part * width // (2 * half), out_sum[...])


def leave(
    core, queries, keys, values, mixed, halves, tables, tokens_all, first_all, second_grads, own_embed, time_flat, bias, gain, shift, weight, rows
):
    seq, both = tokens_all.shape
    part = weight.shape[2]
    width = gain.shape[1]
    embed = both - width
    half = embed // 2
    time_lanes = 4 * width + 128
    weight_lanes = 3 * part * width // embed + width

    def shard(lanes):
        return pl.BlockSpec((rows, lanes), lambda i, _: (i, 0))

    inputs = (*tables, tokens_all, first_all)
    extras = (*second_grads, own_embed)
    constants = (time_flat, bias, gain, shift, weight)
    groups = seq // rows
    picked = [pl.BlockSpec((rows, part), lambda i, _, at=at: (at, 0)) for _, at in queries]
    shards = [each for each, _ in queries] + [*keys, *values, *mixed]
    shards += [pair[0] for pair in halves] + [pair[1] for pair in halves]
    shard_specs = picked + [shard(part)] * (len(keys) + len(values)) + [whole(rows, part)] * groups
    shard_specs += [whole(rows // 2, width)] * (2 * groups)
    return pl.pallas_call(
        functools.partial(exit_kernel, groups=groups, calls=len(keys)),
        grid_spec=pltpu.PrefetchScalarGridSpec(
            num_scalar_prefetch=1,
            grid=(seq // rows,),
            in_specs=[shard(each.shape[1]) for each in inputs]
            + shard_specs
            + [whole(*each.shape) for each in extras]
            + [block_of((embed, width), 0, 0), block_of((1, width), 0, 0)]
            + [whole(*each.shape) for each in (gain, shift, weight)],
            out_specs=[shard(width)]
            + [whole(half, time_lanes)] * 2
            + [whole(half, weight_lanes)] * 2,
            scratch_shapes=[
                pltpu.VMEM((3, width, part), F32),
                pltpu.VMEM((embed, 2 * width), F32),
                pltpu.VMEM((8, width), F32),
                pltpu.VMEM((part, width), F32),
            ],
        ),
        out_shape=[jax.ShapeDtypeStruct((seq, width), BF16)]
        + [jax.ShapeDtypeStruct((half, time_lanes), BF16)] * 2
        + [jax.ShapeDtypeStruct((half, weight_lanes), BF16)] * 2,
        compiler_params=limits(48),
        cost_estimate=pl.CostEstimate(
            flops=seq * width,
            bytes_accessed=seq * width,
            transcendentals=seq,
        ),
    )(core, *kept_out(*inputs, *shards, *extras, *constants))


def middle_kernel(
    tokens_ref, top_ref, bottom_ref, embed_ref, time_ref, bias_ref, gain_ref, shift_ref, residual_ref, second_ref
):
    width = gain_ref.shape[1]
    attended = jnp.concatenate([top_ref[...], bottom_ref[...]], axis=0)
    residual = tokens_ref[...].astype(F32) + attended
    residual_ref[...] = residual
    mod = product(embed_ref[...], time_ref[...]) + bias_ref[...]
    normed, _ = norm_parts(residual)
    base = normed * gain_ref[...] + shift_ref[...]
    second_ref[...] = (base * (1.0 + mod[:, :width]) + mod[:, width:]).astype(BF16)


def middle(tokens, top, bottom, embed, time_flat, bias, gain, shift):
    rows, width = tokens.shape
    inputs = (tokens, top, bottom, embed, time_flat, bias, gain, shift)
    shard = whole(rows, width)
    return pl.pallas_call(
        middle_kernel,
        grid=(1,),
        in_specs=[whole(*each.shape) for each in inputs[:4]]
        + [block_of((embed.shape[1], 2 * width), 0, 1), block_of((1, 2 * width), 0, 1)]
        + [whole(*each.shape) for each in inputs[6:]],
        out_specs=[shard, shard],
        out_shape=[pltpu.HBM((rows, width), F32), pltpu.HBM((rows, width), BF16)],
        compiler_params=limits(16),
    )(*kept_out(tokens), top, bottom, *kept_out(*inputs[3:]))


def middle_back_kernel(
    part_ref, other_ref, cotangent_ref, residual_ref, embed_ref, time_ref, bias_ref, gain_ref, shift_ref,
    residual_grad_ref, half_ref, scale_grad_ref, shift_grad_ref, small_ref,
):
    grads = part_ref[...] + other_ref[...]
    factor = 1.0 + product(embed_ref[...], time_ref[...]) + bias_ref[...]
    normed, scale = norm_parts(residual_ref[...])
    gain = gain_ref[...]
    base = normed * gain + shift_ref[...]
    weighted = grads * factor
    inner = weighted * gain
    back = scale * (
        inner
        - jnp.mean(inner, axis=-1, keepdims=True)
        - normed * jnp.mean(inner * normed, axis=-1, keepdims=True)
    )
    residual_grad = cotangent_ref[...].astype(F32) + back
    residual_grad_ref[...] = residual_grad
    half_ref[...] = residual_grad.astype(BF16)
    scale_grad = grads * base
    scale_grad_ref[...] = scale_grad.astype(BF16)
    shift_grad_ref[...] = grads.astype(BF16)
    small_ref[...] = jnp.concatenate(
        [
            jnp.sum(each, axis=0, keepdims=True)
            for each in (weighted * normed, weighted, scale_grad, grads)
        ],
        axis=0,
    )


def middle_back(part, other, cotangent, residual, embed, time_flat, bias, gain, shift):
    rows, width = cotangent.shape
    shard = whole(rows, width)
    inputs = (part, other, cotangent, residual, embed, time_flat, bias, gain, shift)
    return pl.pallas_call(
        middle_back_kernel,
        grid=(1,),
        in_specs=[whole(*each.shape) for each in inputs[:5]]
        + [block_of((embed.shape[1], width), 0, 2), block_of((1, width), 0, 2)]
        + [whole(*each.shape) for each in inputs[7:]],
        out_specs=[shard] * 4 + [whole(4, width)],
        out_shape=[
            pltpu.HBM((rows, width), F32),
            jax.ShapeDtypeStruct((rows, width), BF16),
            pltpu.HBM((rows, width), BF16),
            pltpu.HBM((rows, width), BF16),
            pltpu.HBM((4, width), F32),
        ],
        compiler_params=limits(20),
    )(part, other, *kept_out(*inputs[2:]))


def forward_kernel(
    place_ref, rows_ref, rows_other_ref, grads_ref, grads_other_ref, up_own_ref, down_own_ref, up_ref, down_ref,
    branch_ref, branch_other_ref, second_ref, second_other_ref, *grad_refs, planes,
):
    step = pl.program_id(0)
    mine = step == 0
    rows = jnp.concatenate([rows_ref[...], rows_other_ref[...]], axis=0)
    grads = jnp.concatenate([grads_ref[...], grads_other_ref[...]], axis=0)
    count = branch_ref.shape[0]
    up = jnp.where(mine, up_own_ref[...], up_ref[...]).reshape(rows.shape[1], up_ref.shape[2])
    packed = jnp.where(mine, down_own_ref[...], down_ref[...])
    half = packed.shape[1] // 2
    down = jnp.concatenate(
        [packed[:, :half].reshape(-1, packed.shape[2]), packed[:, half:].reshape(-1, packed.shape[2])],
        axis=1,
    )
    hidden = product(rows, up)
    active_grad = product(grads, down, TRAIL)
    tail = 0.5 * (1.0 + lax.erf(hidden * math.sqrt(0.5)))
    slope = tail + hidden * jnp.exp(hidden * hidden * -0.5) * (1.0 / math.sqrt(2.0 * math.pi))
    active = (hidden * tail).astype(BF16)
    hidden_grad = (active_grad * slope).astype(BF16)
    branch = product(active, down)
    second = product(hidden_grad, up, TRAIL)

    @pl.when(mine)
    def _():
        branch_ref[...] = branch[:count]
        branch_other_ref[...] = branch[count:]
        second_ref[...] = second[:count]
        second_other_ref[...] = second[count:]

    @pl.when(step > 0)
    def _():
        branch_ref[...] += branch[:count]
        branch_other_ref[...] += branch[count:]
        second_ref[...] += second[:count]
        second_other_ref[...] += second[count:]

    bits = planes.bit_length() - 1
    down_grad = product(active, grads, LEAD)
    up_grad = product(rows, hidden_grad, LEAD)
    for bit, at, kept_ref, sent_ref in ((0, 0, *grad_refs[:2]), (bits - 1, 1, *grad_refs[2:])):
        one = (place_ref[0] >> bit) & 1 == 1
        for part, grad in enumerate((down_grad, up_grad)):
            middle = grad.shape[1] // 2
            columns = grad[:, at * middle : (at + 1) * middle].astype(BF16)
            low = columns.shape[0] // planes << bit
            split = columns.reshape(-1, 2, low, middle)
            each = columns.shape[0] // planes
            down_rows = kept_ref.shape[2] // 2
            for ref, chosen in (
                (kept_ref, jnp.where(one, split[:, 1], split[:, 0])),
                (sent_ref, jnp.where(one, split[:, 0], split[:, 1])),
            ):
                chosen = chosen.reshape(planes // 2, each, middle)
                if part == 0:
                    ref[:, 0, :down_rows] = chosen
                else:
                    ref[:, 0, down_rows:, :middle] = chosen[:, :down_rows]
                    ref[:, 0, down_rows:, middle:] = chosen[:, down_rows:]


def feed_forward(place, rows, rows_other, grads, grads_other, own_weights, weights, groups):
    tokens, width = rows.shape
    planes, piece_rows, hidden = own_weights.shape
    half = whole(tokens, width)
    block = (planes, piece_rows // 2, hidden)

    def other(i):
        return jnp.maximum(i - 1, 0)

    piece = (planes // 2, 1, 2 * hidden // planes, width // 2)
    grad_spec = pl.BlockSpec(piece, lambda i, at: (0, i, 0, 0))
    grad_shape = pltpu.HBM((piece[0], groups, *piece[2:]), BF16)
    return pl.pallas_call(
        functools.partial(forward_kernel, planes=planes),
        grid_spec=pltpu.PrefetchScalarGridSpec(
            num_scalar_prefetch=1,
            grid=(groups,),
            in_specs=[
                half,
                half,
                half,
                half,
                pl.BlockSpec(block, lambda i, _: (0, 0, 0)),
                pl.BlockSpec(block, lambda i, _: (0, 1, 0)),
                pl.BlockSpec(block, lambda i, _: (other(i), 0, 0)),
                pl.BlockSpec(block, lambda i, _: (other(i), 1, 0)),
            ],
            out_specs=[half] * 4 + [grad_spec] * 4,
        ),
        out_shape=[jax.ShapeDtypeStruct((tokens, width), F32)] * 4 + [grad_shape] * 4,
        compiler_params=limits(48),
        cost_estimate=pl.CostEstimate(
            flops=24 * tokens * width * groups * hidden,
            bytes_accessed=8 * width * groups * hidden,
            transcendentals=4 * tokens * groups * hidden,
        ),
    )(place, *kept_out(rows), rows_other, *kept_out(grads, grads_other, own_weights, own_weights, weights, weights))


def spread_kernel(packed_ref, spread_ref):
    width = spread_ref.shape[2]
    for at in range(spread_ref.shape[1]):
        spread_ref[:, at, :] = packed_ref[:, at * width : (at + 1) * width].astype(F32)


def spread(packed, shape, rows):
    blocks = packed.shape[0] // rows
    columns = shape[1] * shape[2]
    return pl.pallas_call(
        spread_kernel,
        grid=(shape[0] // rows,),
        in_specs=[pl.BlockSpec((rows, columns), lambda i: (i % blocks, i // blocks))],
        out_specs=pl.BlockSpec((rows, shape[1], shape[2]), lambda i: (i, 0, 0)),
        out_shape=jax.ShapeDtypeStruct(shape, F32),
        compiler_params=limits(16),
    )(packed)


def unfold_kernel(packed_ref, out_ref):
    rows, width = packed_ref.shape[0], out_ref.shape[2]
    for at in range(packed_ref.shape[1] // width):
        out_ref[0, at * rows : (at + 1) * rows] = packed_ref[:, at * width : (at + 1) * width].astype(F32)


def unfold(packed, shape):
    rows = packed.shape[0]
    blocks = shape[1] // rows
    return pl.pallas_call(
        unfold_kernel,
        grid=(shape[0],),
        in_specs=[pl.BlockSpec((rows, blocks * shape[2]), lambda i: (0, i))],
        out_specs=pl.BlockSpec((1, *shape[1:]), lambda i: (i, 0, 0)),
        out_shape=jax.ShapeDtypeStruct(shape, F32),
        compiler_params=limits(16),
    )(packed)


def unpack_kernel(sums_ref, down_ref, up_ref):
    rows = sums_ref.shape[1] // 2
    half = up_ref.shape[1]
    quarter = half // 2
    for which in range(sums_ref.shape[0]):
        down_ref[which * rows : (which + 1) * rows] = sums_ref[which, :rows].astype(F32)
        upper = 2 * which * rows
        for at in range(2):
            columns = slice(at * quarter, (at + 1) * quarter)
            folded = sums_ref[which, rows:, at * half : (at + 1) * half].astype(F32)
            up_ref[upper : upper + rows, columns] = folded[:, :quarter]
            up_ref[upper + rows : upper + 2 * rows, columns] = folded[:, quarter:]


def unpack(sums, planes):
    pieces, both, width = sums.shape
    rows = both // 2
    half = width // 2
    return pl.pallas_call(
        unpack_kernel,
        grid=(pieces // 2,),
        in_specs=[pl.BlockSpec((2, both, width), lambda i: (i, 0, 0))],
        out_specs=[
            pl.BlockSpec((2 * rows, width), lambda i: (i, 0)),
            pl.BlockSpec((4 * rows, half), lambda i: (i % (planes // 2), i // (planes // 2))),
        ],
        out_shape=[
            jax.ShapeDtypeStruct((pieces * rows, width), F32),
            jax.ShapeDtypeStruct((planes * 2 * rows, half * pieces // planes), F32),
        ],
        compiler_params=limits(16),
    )(sums)


def swap(values, axis_name, bit):
    size = lax.axis_size(axis_name)
    return lax.ppermute(values, axis_name, [(at, at ^ (1 << bit)) for at in range(size)])


def bit_of(axis_name, bit):
    return (lax.axis_index(axis_name) >> bit) & 1


def after(values, *others):
    return lax.optimization_barrier((values, others))[0]


def exchange(values, axis_name, bit, dim):
    own = bit_of(axis_name, bit)
    kept = lax.dynamic_index_in_dim(values, own, dim, keepdims=False)
    sent = lax.dynamic_index_in_dim(values, 1 - own, dim, keepdims=False)
    return (kept, swap(sent, axis_name, bit))


def total(kept, got):
    return (kept.astype(F32) + got.astype(F32)).astype(BF16)


def double(values, axis_name, bit, dim):
    own = bit_of(axis_name, bit) == 0
    got = swap(values, axis_name, bit)
    return jnp.stack([jnp.where(own, values, got), jnp.where(own, got, values)], axis=dim)


class PlaneScatter:
    def __init__(self, arrays, orders, dim):
        bits = len(orders[0])
        self.dim = dim
        self.arrays = [
            each.reshape(each.shape[:dim] + (2,) * bits + each.shape[dim + 1 :]) for each in arrays
        ]
        self.orders = [list(order) for order in orders]
        self.left = [list(range(bits - 1, -1, -1)) for _ in orders]

    @classmethod
    def started(cls, kept, sent, orders, dim):
        self = cls.__new__(cls)
        bits = len(orders[0])
        self.dim = dim
        self.orders = [list(order[1:]) for order in orders]
        self.left = [[bit for bit in range(bits - 1, -1, -1) if bit != order[0]] for order in orders]
        self.kept = [
            each.reshape(each.shape[:dim] + (2,) * (bits - 1) + each.shape[dim + 1 :]) for each in kept
        ]
        self.got = [
            swap(each, "plane", order[0]).reshape(like.shape)
            for each, like, order in zip(sent, self.kept, orders)
        ]
        return self

    def send(self):
        self.kept, self.got = [], []
        for values, order, left in zip(self.arrays, self.orders, self.left):
            bit = order.pop(0)
            kept, got = exchange(values, "plane", bit, self.dim + left.index(bit))
            left.remove(bit)
            self.kept.append(kept)
            self.got.append(got)

    def meet(self, *others):
        self.got, others = lax.optimization_barrier((self.got, others))
        return others

    def add(self):
        self.arrays = [total(kept, got) for kept, got in zip(self.kept, self.got)]

    def finish(self):
        while self.orders[0]:
            self.send()
            self.add()
        return self.arrays


def plane_gather(values, order, dim):
    bits = len(order)
    left = []
    for bit in reversed(order):
        left = sorted(left + [bit], reverse=True)
        values = double(values, "plane", bit, dim + left.index(bit))
    shape = values.shape
    return values.reshape(shape[:dim] + (1 << bits,) + shape[dim + bits :])


def ring_gather(shard, meanwhile=None):
    size = lax.axis_size("tensor")
    half = shard.shape[0] // 2
    right, left = [shard[:half]], [shard[half:]]
    for step in range(1, size):
        others = () if meanwhile is None else meanwhile(step, right, left)
        right.append(lax.ppermute(right[-1], "tensor", [(at, (at + 1) % size) for at in range(size)]))
        left.append(lax.ppermute(left[-1], "tensor", [(at, (at - 1) % size) for at in range(size)]))
        right[-1], left[-1], others = lax.optimization_barrier((right[-1], left[-1], others))
        if meanwhile is not None:
            meanwhile(-step, others, None)
    return [(right[(size - at) % size], left[at]) for at in range(size)]


def ring_scatter(chunks, *gates):
    size = len(chunks)
    half = chunks[0].shape[0] // 2
    right = chunks[size - 1][:half]
    left = chunks[1 % size][half:]
    for step in range(1, size):
        right = lax.ppermute(right, "tensor", [(at, (at + 1) % size) for at in range(size)])
        left = lax.ppermute(left, "tensor", [(at, (at - 1) % size) for at in range(size)])
        right, left = after((right, left), *(gates[step - 1] if step <= len(gates) else ()))
        right = right.astype(F32) + chunks[size - 1 - step][:half].astype(F32)
        left = left.astype(F32) + chunks[(step + 1) % size][half:].astype(F32)
        if step < size - 1:
            right, left = right.astype(BF16), left.astype(BF16)
    return (right, left)


def own_first(values, dim):
    size = lax.axis_size("tensor")
    stretch = values.shape[dim] // size
    doubled = jnp.concatenate([values, values], axis=dim)
    return lax.dynamic_slice_in_dim(
        doubled, lax.axis_index("tensor") * stretch, values.shape[dim], dim
    )


def tensor_sum(values):
    size = lax.axis_size("tensor")
    for bit in range(size.bit_length() - 1):
        values = (values.astype(F32) + swap(values, "tensor", bit).astype(F32)).astype(BF16)
    return values


def local(
    tokens,
    time_embed,
    segment_ids,
    positions,
    first_gain,
    first_bias,
    second_gain,
    second_bias,
    time_weight,
    time_bias,
    qkv_weight,
    out_weight,
    up_weight,
    down_weight,
    cotangent,
):
    local_rows, width = tokens.shape
    embed_width = time_embed.shape[1]
    local_width = qkv_weight.shape[2]
    hidden_local = up_weight.shape[1]
    half_hidden = hidden_local // 2
    planes = lax.axis_size("plane")
    groups = lax.axis_size("tensor")
    plane_at = lax.axis_index("plane")
    core_at = lax.axis_index("core")
    place = plane_at.astype(jnp.int32).reshape(1)
    arrival = sorted(range(groups), key=lambda at: max(at, groups - at) if at else 0)
    rising = list(range(planes.bit_length() - 1))
    falling = rising[::-1]

    up_rows = width // planes
    up_piece = lax.dynamic_slice(
        up_weight, (plane_at * up_rows, core_at * half_hidden), (up_rows, half_hidden)
    )
    down_rows = half_hidden // planes
    down_piece = lax.dynamic_slice(
        down_weight, (core_at * half_hidden + plane_at * down_rows, 0), (down_rows, width)
    )
    piece = jnp.concatenate([up_piece, down_piece[:, :half_hidden], down_piece[:, half_hidden:]], axis=0)
    chosen = lax.all_gather(piece, "tensor", axis=0)
    up_half = lax.dynamic_slice_in_dim(up_weight, core_at * half_hidden, half_hidden, 1)
    down_half = lax.dynamic_slice_in_dim(down_weight, core_at * half_hidden, half_hidden, 0)
    down_half = down_half.reshape(planes, down_rows, width)
    own_pieces = jnp.concatenate(
        [
            up_half.reshape(planes, up_rows, half_hidden),
            down_half[..., :half_hidden],
            down_half[..., half_hidden:],
        ],
        axis=1,
    )

    held = {
        "time": time_weight.reshape(embed_width, 4 * width),
        "tables": rotary_tables(own_first(positions, 1).reshape(-1), 2 * HEAD),
        "pieces": own_pieces,
        "cotangent": swap(cotangent, "core", 0),
    }
    bias_flat = time_bias.reshape(1, 4 * width)
    first_gain, first_bias = first_gain.reshape(1, width), first_bias.reshape(1, width)
    second_gain, second_bias = second_gain.reshape(1, width), second_bias.reshape(1, width)
    qkv_planes = jnp.transpose(qkv_weight, (1, 0, 2))
    segments = own_first(segment_ids, 1)
    columns = segments.reshape(-1, 1)

    def enter(places, halves, row):
        return entry(
            halves, held["tables"], held["time"], bias_flat, first_gain, first_bias, qkv_planes, places, groups, row
        )

    def meanwhile(step, right, left):
        if step == 1:
            return held
        if step == -1:
            held.update(right)
        elif step == 2:
            return enter([0], (right[0], left[0]), ())
        elif step > 2 and 2 * (step - 1) == groups:
            return enter([step - 1], (right[step - 1], left[step - 1]), held["row"])
        elif step > 0:
            return held["row"]
        else:
            held["row"] = right
        return None

    gathered = ring_gather(jnp.concatenate([tokens, time_embed], axis=1), meanwhile)
    chosen = after(chosen, gathered[arrival[-1]])
    tensor_at = lax.axis_index("tensor")
    chosen = jnp.stack(
        [
            lax.dynamic_index_in_dim(chosen, (tensor_at + at) % groups, 0, keepdims=False)
            for at in range(1, groups)
        ]
    )
    pieces = lax.all_gather(chosen, "plane", axis=1)
    pieces = pieces.reshape((groups - 1) * planes, up_rows * 2, half_hidden)
    row = held["row"]
    for first in range(2, len(arrival), 2):
        places = arrival[first : first + 2]
        row = enter(places, [half for at in places for half in gathered[at]], row)
    tables, time_flat = held["tables"], held["time"]
    tokens_all, first_all, queries, keys, values = row
    keys, chosen = lax.optimization_barrier((keys, chosen))
    mixed, logsums, parts = {}, {}, {}
    for at in list(range(groups - 1, -1, -1)):
        mixed[at], logsums[at], parts[at] = attend(
            queries, keys, values, segments, columns, out_weight, at, local_rows
        )
    attended = ring_scatter([parts[at] for at in range(groups)])

    residual, second_normed = middle(
        tokens, *attended, time_embed, time_flat, bias_flat, second_gain, second_bias
    )
    branch_own, branch_other, second_own, second_other, *grad_parts = feed_forward(
        place,
        second_normed,
        swap(second_normed, "core", 0),
        cotangent,
        held["cotangent"],
        held["pieces"],
        pieces,
        groups,
    )
    second_other = swap(second_other, "core", 0)

    weight_sums = PlaneScatter.started(
        grad_parts[::2], grad_parts[1::2], [rising, falling], 0
    )
    branch = branch_own + swap(branch_other, "core", 0)
    result = (residual + branch).astype(BF16)

    residual_grad, attended_own, scale_two_grad, shift_two_grad, small_two = middle_back(
        second_own,
        second_other,
        cotangent,
        residual,
        time_embed,
        time_flat,
        bias_flat,
        second_gain,
        second_bias,
    )
    def turn(places, halves):
        return attend_back(
            halves,
            queries,
            keys,
            values,
            [logsums[at] for at in places],
            segments,
            columns,
            out_weight,
            tables,
            places,
        )

    back = {}

    def meanwhile_back(step, right, left):
        if step == 2:
            return turn([0], (right[0], left[0]))
        if step == -2:
            back[(0,)] = right
        elif step == groups - 1:
            done = ()
            if 2 * (step - 1) == groups:
                done = turn([step - 1], (right[step - 1], left[step - 1]))
            return (done, weight_sums.got)
        elif step == 1 - groups:
            done, weight_sums.got = right
            if done:
                back[(groups // 2,)] = done
        return ()

    attended_halves = ring_gather(attended_own, meanwhile_back)
    weight_sums.add()
    attended_halves[arrival[2]], weight_sums.arrays = lax.optimization_barrier(
        (attended_halves[arrival[2]], weight_sums.arrays)
    )
    if weight_sums.orders[0]:
        weight_sums.send()
    rest = [at for at in arrival if (at,) not in back]
    for first in range(0, len(rest), 2):
        places = tuple(rest[first : first + 2])
        back[places] = turn(places, [half for at in places for half in attended_halves[at]])
    query_shards = {at: (parts[0], which) for places, parts in back.items() for which, at in enumerate(places)}
    received = [
        lax.ppermute(parts[hop], "tensor", [(at, (at + hop) % groups) for at in range(groups)])
        for hop in range(1, groups)
    ]
    left = leave(
        core_at.astype(jnp.int32).reshape(1),
        [query_shards[at] for at in range(groups)],
        [parts[1] for parts in back.values()],
        [parts[2] for parts in back.values()],
        [mixed[at] for at in range(groups)],
        attended_halves,
        tables,
        tokens_all,
        first_all,
        (scale_two_grad, shift_two_grad, small_two),
        time_embed,
        time_flat,
        bias_flat,
        first_gain,
        first_bias,
        qkv_planes,
        local_rows,
    )
    (left,) = weight_sums.meet(left)
    weight_sums.add()
    by_link = weight_sums.finish()
    parts = [jnp.concatenate([each[at] for each in by_link], axis=-1) for at in range(groups)]
    received = [
        lax.ppermute(parts[hop], "tensor", [(at, (at + hop) % groups) for at in range(groups)])
        for hop in range(1, groups)
    ]
    first_half, time_kept, time_sent, weight_kept, weight_sent = left

    time_got, weight_got = swap(time_sent, "core", 0), swap(weight_sent, "core", 0)

    def by_plane(pack):
        return pack.reshape(planes, embed_width // (2 * planes), -1)

    pack_sums = PlaneScatter(
        [by_plane(total(time_kept, time_got)), by_plane(total(weight_kept, weight_got))], [rising, falling], 0
    )
    for _ in rising:
        pack_sums.send()
        if len(pack_sums.orders[0]) == 0:
            (received,) = pack_sums.meet(received)
        pack_sums.add()
    time_own, weight_own = pack_sums.arrays
    sums = sum(each.astype(F32) for each in [parts[0], *received]).astype(BF16)
    sums = lax.all_gather(sums, ("core", "plane"), axis=0)
    first_half, time_own = lax.optimization_barrier((first_half, time_own))
    time_sum = tensor_sum(time_own)
    time_halves = plane_gather(time_sum, rising, 0)
    weight_halves = plane_gather(weight_own, falling, 0)
    time_pack = double(time_halves.reshape(embed_width // 2, -1), "core", 0, 0)
    weight_pack = double(weight_halves.reshape(embed_width // 2, -1), "core", 0, 0)
    time_pack = time_pack.reshape(embed_width, -1)
    weight_pack = weight_pack.reshape(embed_width, -1)
    (sums,) = kept_out(sums)
    down_summed, up_summed = unpack(sums, planes)
    first_grad = ring_scatter(
        [first_half[at * local_rows : (at + 1) * local_rows] for at in range(groups)],
        (time_sum,),
        (time_halves, weight_halves),
        (time_pack, weight_pack, down_summed),
    )
    time_weight_grad = spread(time_pack, (embed_width, 4, width), min(64, embed_width))
    small = time_pack[: width // 16, 4 * width :].astype(F32)
    small = jnp.transpose(small.reshape(width // 128, 8, 128), (1, 0, 2)).reshape(8, width)
    qkv_lanes = 3 * local_width * width // embed_width
    qkv_summed = jnp.transpose(
        unfold(weight_pack, (3, width, local_width)), (1, 0, 2)
    )
    out_summed = weight_pack[:, qkv_lanes:].astype(F32)

    own_normed, own_scale = norm_parts(tokens.astype(F32))
    mod_own = product(time_embed, time_flat[:, :width]) + bias_flat[:, :width]
    first_grad = jnp.concatenate(first_grad, axis=0)
    input_grad = residual_grad + norm_input_back(first_grad, own_normed, own_scale, first_gain, mod_own)
    return (
        result,
        input_grad,
        small[0],
        small[1],
        small[4],
        small[5],
        time_weight_grad,
        jnp.concatenate([small[2:4], small[6:]], axis=0),
        qkv_summed,
        out_summed,
        up_summed,
        down_summed,
    )


def solution(mesh):
    whole, tensor = mesh.devices.shape
    finer = Mesh(mesh.devices.reshape(whole // 2, 2, tensor), ("plane", "core", "tensor"))
    rows = P(("plane", "core", "tensor"), None)
    group = P(("plane", "core"), None)
    return jax.shard_map(
        local,
        mesh=finer,
        in_specs=(
            rows,
            rows,
            group,
            group,
            P(),
            P(),
            P(),
            P(),
            P(),
            P(),
            P(None, None, "tensor"),
            P("tensor", None),
            P(None, "tensor"),
            P("tensor", None),
            rows,
        ),
        out_specs=(
            rows,
            rows,
            P(),
            P(),
            P(),
            P(),
            P(),
            P(),
            P(None, None, "tensor"),
            P("tensor", None),
            P(None, "tensor"),
            P("tensor", None),
        ),
        check_vma=False,
    )
```

time: 574 us -> 427 us (0.74)
  Pallas kernels: 0 us -> 107 us
  matrix products: 91 us -> 1.75 us
  local copies, waits for them, and re-layouts: 78.3 us -> 16.8 us
  waiting for transfers between devices: 239 us -> 200 us
  other arithmetic: 61.4 us -> 27.4 us
  starting transfers between devices: 77.7 us -> 51.1 us
    pallas_call x0 -> x17, Pallas kernels: none -> 107 us  [the longest x3 25 us: attend_back(): pl.pallas_call(functools.partial(attend_back_kernel, count=count), grid=(...]
    dot_general x42 -> x1, matrix products: 63.6 us -> 1.75 us  [product(): return lax.dot_general(left, right, dims, preferred_element_type=F32)]
    unnamed x222 -> x81, local copies, waits for them, and re-layouts: 44.3 us -> 6.68 us
    ppermute x6 -> x3, waiting for transfers between devices: 43.7 us -> 14.8 us  [local(): lax.ppermute(parts[hop], 'tensor', [(at, (at + hop) % groups) for at in r...]
    dot_general x24 -> x0, matrix products: 27.4 us -> none  [the longest x4 6.54 us: attend_back_block(): jnp.einsum('qhd,khd->hqk', grad_block, value_rows, preferred_element_type...]
    ppermute x6, waiting for transfers between devices: 33.9 us -> 6.93 us  [ring_scatter(): lax.ppermute(right, 'tensor', [(at, (at + 1) % size) for at in range(size)])]
    convert_element_type x20 -> x13, other arithmetic: 28.3 us -> 12.5 us  [the longest x10 9.26 us: total(): return (kept.astype(F32) + got.astype(F32)).astype(BF16)]
    ppermute x22, starting transfers between devices: 36 us -> 22.2 us  [swap(): lax.ppermute(values, axis_name, [(at, at ^ 1 << bit) for at in range(size)])]
  transfers between devices with their start and end apart: 54 -> 52, of which waited for: 32 -> 27; matrix products, arithmetic and copies ran while one was open for 27% -> 6% of each run, Pallas kernels for 0% -> 21%
where the time goes in v3:
time: 427 us; the launch traced here: 419 us
  waiting for transfers between devices  200 us (47%)
  Pallas kernels  107 us (25%)
  starting transfers between devices  51.1 us (12%)
  other arithmetic  27.4 us (6%)
  local copies, waits for them, and re-layouts  16.8 us (4%)
  between operations  15 us (4%)
    ppermute x22, waiting for transfers between devices, swap(): lax.ppermute(values, axis_name, [(at, at ^ 1 << bit) for at in range(size)])  74.3 us
    ppermute x6, waiting for transfers between devices, ring_gather(): lax.ppermute(left[-1], 'tensor', [(at, (at - 1) % size) for at in range(s...  40.3 us
    ppermute x6, waiting for transfers between devices, ring_gather(): lax.ppermute(right[-1], 'tensor', [(at, (at + 1) % size) for at in range(...  36 us
    pallas_call x3, Pallas kernels, attend_back(): pl.pallas_call(functools.partial(attend_back_kernel, count=count), grid=(...  25 us
    ppermute x22, starting transfers between devices, swap(): lax.ppermute(values, axis_name, [(at, at ^ 1 << bit) for at in range(size)])  22.2 us
    pallas_call x1, Pallas kernels, feed_forward(): pl.pallas_call(functools.partial(forward_kernel, planes=planes), grid_spe...  20.3 us
    ppermute x6, waiting for transfers between devices, ring_scatter(): lax.ppermute(left, 'tensor', [(at, (at - 1) % size) for at in range(size)])  17.8 us
    pallas_call x1, Pallas kernels, leave(): pl.pallas_call(functools.partial(exit_kernel, groups=groups, calls=len(ke...  15.7 us
  transfers between devices with their start and end apart: 52, of which 27 were waited for; matrix products, arithmetic and copies ran while one was open for 6% of the time, Pallas kernels for 21%

profile of v3, /device:TPU:21, one launch (start us, length us, event | category | flops | bytes accessed | tf_op | source)
XLA Modules:
  0.0 419.0 jit_solution(1028715928204386102)
XLA Ops:
  19.0 3.1 fusion.18
  22.0 14.3 %collective-permute-done.1.refs_1_ = bf16[128,1280]{1,0:T(8,128)(2,1)S(1)} collective-permute-done((bf16[128,1280]{1,0:T(8,128)(2,1)S(1)}, bf16[128,1280]{1,0:T(8,128)(2,1)S(1)}, u32[]{:S(2)}, u32[]{:S(2)}) %collective-permute-start.1) | collective-permute-done | bytes 327712 | tf_op jit(solution)/shard_map/ppermute | solution.py:799
  36.3 2.7 collective-permute-start.4
  39.7 3.8 shard_map.238
  43.5 22.7 %collective-permute-done.3.refs_0_ = bf16[128,1280]{1,0:T(8,128)(2,1)S(1)} collective-permute-done((bf16[128,1280]{1,0:T(8,128)(2,1)S(1)}, bf16[128,1280]{1,0:T(8,128)(2,1)S(1)}, u32[]{:S(2)}, u32[]{:S(2)}) %collective-permute-start.3) | collective-permute-done | bytes 327712 | tf_op jit(solution)/shard_map/ppermute | solution.py:798
  67.2 3.0 collective-permute-start.5
  70.3 3.8 shard_map.239
  74.1 7.1 %collective-permute-done.5.refs_0_ = bf16[128,1280]{1,0:T(8,128)(2,1)S(1)} collective-permute-done((bf16[128,1280]{1,0:T(8,128)(2,1)S(1)}, bf16[128,1280]{1,0:T(8,128)(2,1)S(1)}, u32[]{:S(2)}, u32[]{:S(2)}) %collective-permute-start.5) | collective-permute-done | bytes 327712 | tf_op jit(solution)/shard_map/ppermute | solution.py:798
  81.3 7.2 %collective-permute-done.6.refs_3_ = bf16[128,1280]{1,0:T(8,128)(2,1)S(1)} collective-permute-done((bf16[128,1280]{1,0:T(8,128)(2,1)S(1)}, bf16[128,1280]{1,0:T(8,128)(2,1)S(1)}, u32[]{:S(2)}, u32[]{:S(2)}) %collective-permute-start.6) | collective-permute-done | bytes 327712 | tf_op jit(solution)/shard_map/ppermute | solution.py:799
  91.6 5.7 %shard_map.240 = (bf16[1024,1280]{1,0:T(8,128)(2,1)}, bf16[1024,1024]{1,0:T(8,128)(2,1)}, bf16[1024,256]{1,0:T(8,128)(2,1)}, bf16[1024,256]{1,0:T(8,128)(2,1)}, bf16[1024,256]{1,0:T(8,128)(2,1)}) custom-call(bf16[128,1280]{1,0:T(8,128)(2,1)S(1)} %collective-permute-done.5.refs_0_, ...), custom_call_target="tpu_custom_call", output_to_operand_aliasing={{0}: (11, {}), {1}: (12, {}), {2}: (13, {}), {3}: (14, {}),... | custom-call | flops 805306368 | bytes 3670016 | tf_op jit(solution)/shard_map/pallas_call | solution.py:114
  100.5 3.6 shard_map.241
  105.2 3.6 shard_map.242
  109.6 3.6 shard_map.243
  113.2 4.3 %collective-permute-done.8 = bf16[128,1024]{1,0:T(8,128)(2,1)S(1)} collective-permute-done((bf16[128,1024]{1,0:T(8,128)(2,1)S(1)}, bf16[128,1024]{1,0:T(8,128)(2,1)S(1)}, u32[]{:S(2)}, u32[]{:S(2)}) %collective-permute-start.8) | collective-permute-done | bytes 262176 | tf_op jit(solution)/shard_map/ppermute | solution.py:813
  120.1 5.1 %collective-permute-done.9 = bf16[128,1024]{1,0:T(8,128)(2,1)S(1)} collective-permute-done((bf16[128,1024]{1,0:T(8,128)(2,1)S(1)}, bf16[128,1024]{1,0:T(8,128)(2,1)S(1)}, u32[]{:S(2)}, u32[]{:S(2)}) %collective-permute-start.9) | collective-permute-done | bytes 262176 | tf_op jit(solution)/shard_map/ppermute | solution.py:812
  125.2 8.4 %collective-permute-done.10 = bf16[128,1024]{1,0:T(8,128)(2,1)S(1)} collective-permute-done((bf16[128,1024]{1,0:T(8,128)(2,1)S(1)}, bf16[128,1024]{1,0:T(8,128)(2,1)S(1)}, u32[]{:S(2)}, u32[]{:S(2)}) %collective-permute-start.10) | collective-permute-done | bytes 262176 | tf_op jit(solution)/shard_map/ppermute | solution.py:813
  135.7 3.6 shard_map.244
  141.1 5.1 %collective-permute-done.12 = bf16[128,1024]{1,0:T(8,128)(2,1)S(1)} collective-permute-done((bf16[128,1024]{1,0:T(8,128)(2,1)S(1)}, bf16[128,1024]{1,0:T(8,128)(2,1)S(1)}, u32[]{:S(2)}, u32[]{:S(2)}) %collective-permute-start.12) | collective-permute-done | bytes 262176 | tf_op jit(solution)/shard_map/ppermute | solution.py:813
  146.4 3.0 shard_map.245
  152.9 9.9 %all-gather.9.cloned.1.call-done = bf16[3,2048,512]{2,1,0:T(8,128)(2,1)} async-done(((bf16[3,512,512]{2,1,0:T(8,128)(2,1)}), bf16[3,2048,512]{2,1,0:T(8,128)(2,1)}) %all-gather.9.cloned.1.call-update) | async-done | bytes 6291472 | tf_op jit(solution)/shard_map/all_gather | solution.py:933
  162.8 20.3 %shard_map.246 = (f32[256,1024]{1,0:T(8,128)S(1)}, f32[256,1024]{1,0:T(8,128)S(1)}, f32[256,1024]{1,0:T(8,128)S(1)}, f32[256,1024]{1,0:T(8,128)S(1)}, bf16[2,4,2...) custom-call(s32[1]{0:T(128)} %bitcast.10.place_ref, ...), custom_call_target="tpu_custom_call" | custom-call | flops 12884901888 | bytes 16777216 | tf_op jit(solution)/shard_map/pallas_call | solution.py:604
  188.2 4.0 shard_map.247
  193.8 6.2 %collective-permute-done.16.refs_2_.refs_17_ = bf16[128,1024]{1,0:T(8,128)(2,1)S(1)} collective-permute-done((bf16[128,1024]{1,0:T(8,128)(2,1)S(1)}, bf16[128,1024]{1,0:T(8,128)(2,1)S(1)}, u32[]{:S(2)}, u32[]{:S(2)}) %collective-permute-start.16) | collective-permute-done | bytes 262176 | tf_op jit(solution)/shard_map/ppermute | solution.py:798
  199.9 5.6 %collective-permute-done.17.refs_1_.refs_19_ = bf16[128,1024]{1,0:T(8,128)(2,1)S(1)} collective-permute-done((bf16[128,1024]{1,0:T(8,128)(2,1)S(1)}, bf16[128,1024]{1,0:T(8,128)(2,1)S(1)}, u32[]{:S(2)}, u32[]{:S(2)}) %collective-permute-start.17) | collective-permute-done | bytes 262176 | tf_op jit(solution)/shard_map/ppermute | solution.py:799
  207.6 6.7 %shard_map.248 = (bf16[256,256]{1,0:T(8,128)(2,1)}, f32[1024,256]{1,0:T(8,128)}, f32[1024,256]{1,0:T(8,128)}) custom-call(bf16[1024,256]{1,0:T(8,128)(2,1)S(1)} %copy-done.1, bf16[1024,256]{1,0:T(8,128)(2,1)S(1)} %copy-done.3, bf16[1024,256]{1,0:T(8,128)(2,1)S(1)} %copy-done.5, s32[1,1024]{1,0:T(1,128)} %copy-done.18, s32[1024,1]{1,0:T(8,128)} %copy-done.6, ...), custom_call_target="tpu_custom_call" | custom-call | flops 805306368 | bytes 4194304 | tf_op jit(solution)/shard_map/pallas_call | solution.py:262
  214.2 5.2 %collective-permute-done.19.refs_1_.refs_20_ = bf16[128,1024]{1,0:T(8,128)(2,1)S(1)} collective-permute-done((bf16[128,1024]{1,0:T(8,128)(2,1)S(1)}, bf16[128,1024]{1,0:T(8,128)(2,1)S(1)}, u32[]{:S(2)}, u32[]{:S(2)}) %collective-permute-start.19) | collective-permute-done | bytes 262176 | tf_op jit(solution)/shard_map/ppermute | solution.py:799
  221.4 6.8 %shard_map.249 = (bf16[256,256]{1,0:T(8,128)(2,1)}, f32[1024,256]{1,0:T(8,128)}, f32[1024,256]{1,0:T(8,128)}) custom-call(bf16[1024,256]{1,0:T(8,128)(2,1)S(1)} %copy-done.1, bf16[1024,256]{1,0:T(8,128)(2,1)S(1)} %copy-done.3, bf16[1024,256]{1,0:T(8,128)(2,1)S(1)} %copy-done.5, s32[1,1024]{1,0:T(1,128)} %copy-done.18, s32[1024,1]{1,0:T(8,128)} %copy-done.6, ...), custom_call_target="tpu_custom_call" | custom-call | flops 805306368 | bytes 4194304 | tf_op jit(solution)/shard_map/pallas_call | solution.py:262
  228.2 6.9 %collective-permute-done.21.refs_3_.refs_21_ = bf16[128,1024]{1,0:T(8,128)(2,1)S(1)} collective-permute-done((bf16[128,1024]{1,0:T(8,128)(2,1)S(1)}, bf16[128,1024]{1,0:T(8,128)(2,1)S(1)}, u32[]{:S(2)}, u32[]{:S(2)}) %collective-permute-start.21) | collective-permute-done | bytes 262176 | tf_op jit(solution)/shard_map/ppermute | solution.py:799
  235.2 2.4 add_convert_fusion.1
  237.6 2.9 add_convert_fusion
  247.3 11.6 %shard_map.250 = (bf16[512,256]{1,0:T(8,128)(2,1)}, f32[1024,256]{1,0:T(8,128)}, f32[1024,256]{1,0:T(8,128)}) custom-call(bf16[1024,256]{1,0:T(8,128)(2,1)S(1)} %copy-done.1, bf16[1024,256]{1,0:T(8,128)(2,1)S(1)} %copy-done.3, bf16[1024,256]{1,0:T(8,128)(2,1)S(1)} %copy-done.5, s32[1,1024]{1,0:T(1,128)} %copy-done.18, s32[1024,1]{1,0:T(8,128)} %copy-done.6, ...), custom_call_target="tpu_custom_call" | custom-call | flops 1610612736 | bytes 4194304 | tf_op jit(solution)/shard_map/pallas_call | solution.py:262
  258.9 15.7 %shard_map.251 = (bf16[1024,1024]{1,0:T(8,128)(2,1)}, bf16[128,4224]{1,0:T(8,128)(2,1)S(1)}, bf16[128,4224]{1,0:T(8,128)(2,1)S(1)}, bf16[128,4096]{1,0:T(8,128)(2,1)S(1)}, bf16[128,4096]{1,0:T(8,128)(2,1)S(1)}) custom-call(s32[1]{0:T(128)} %bitcast.14.place_ref, f32[1024,128]{1,0:T(8,128)} %get-tuple-element.139.refs_2_.refs_4_.cosine_ref, ...), custom_call_target="tpu_custom_call" | custom-call | flops 1048576 | bytes 1048576 | tf_op jit(solution)/shard_map/pallas_call | solution.py:415
  282.5 11.9 %collective-permute-done.30 = bf16[2,32,4096]{2,1,0:T(8,128)(2,1)S(1)} collective-permute-done((bf16[2,32,4096]{2,1,0:T(8,128)(2,1)S(1)}, bf16[2,32,4096]{2,1,0:T(8,128)(2,1)S(1)}, u32[]{:S(2)}, u32[]{:S(2)}) %collective-permute-start.30) | collective-permute-done | bytes 524320 | tf_op jit(solution)/shard_map/ppermute | solution.py:705
  294.8 11.5 %collective-permute-done.27 = bf16[2,32,4224]{2,1,0:T(8,128)(2,1)S(1)} collective-permute-done((bf16[2,32,4224]{2,1,0:T(8,128)(2,1)S(1)}, bf16[2,32,4224]{2,1,0:T(8,128)(2,1)S(1)}, u32[]{:S(2)}, u32[]{:S(2)}) %collective-permute-start.27) | collective-permute-done | bytes 540704 | tf_op jit(solution)/shard_map/ppermute | solution.py:705
  309.1 5.5 %collective-permute-done.32 = bf16[256,1024]{1,0:T(8,128)(2,1)S(1)} collective-permute-done((bf16[256,1024]{1,0:T(8,128)(2,1)S(1)}, bf16[256,1024]{1,0:T(8,128)(2,1)S(1)}, u32[]{:S(2)}, u32[]{:S(2)}) %collective-permute-start.32) | collective-permute-done | bytes 524320 | tf_op jit(solution)/shard_map/ppermute | solution.py:1053
  314.6 9.3 %collective-permute-done.34 = bf16[256,1024]{1,0:T(8,128)(2,1)S(1)} collective-permute-done((bf16[256,1024]{1,0:T(8,128)(2,1)S(1)}, bf16[256,1024]{1,0:T(8,128)(2,1)S(1)}, u32[]{:S(2)}, u32[]{:S(2)}) %collective-permute-start.34) | collective-permute-done | bytes 524320 | tf_op jit(solution)/shard_map/ppermute | solution.py:1053
  324.9 3.1 collective-permute-start.35
  331.2 4.8 %collective-permute-done.46 = bf16[32,4096]{1,0:T(8,128)(2,1)} collective-permute-done((bf16[32,4096]{1,0:T(8,128)(2,1)S(1)}, bf16[32,4096]{1,0:T(8,128)(2,1)}, u32[]{:S(2)}, u32[]{:S(2)}) %collective-permute-start.46) | collective-permute-done | bytes 262176 | tf_op jit(solution)/shard_map/ppermute | solution.py:705
  337.0 8.6 %collective-permute-done.37 = bf16[32,4224]{1,0:T(8,128)(2,1)S(1)} collective-permute-done((bf16[32,4224]{1,0:T(8,128)(2,1)S(1)}, bf16[32,4224]{1,0:T(8,128)(2,1)S(1)}, u32[]{:S(2)}, u32[]{:S(2)}) %collective-permute-start.37) | collective-permute-done | bytes 270368 | tf_op jit(solution)/shard_map/ppermute | solution.py:705
  345.6 2.8 collective-permute-start.38
  348.8 10.5 %collective-permute-done.38 = bf16[32,4224]{1,0:T(8,128)(2,1)S(1)} collective-permute-done((bf16[32,4224]{1,0:T(8,128)(2,1)S(1)}, bf16[32,4224]{1,0:T(8,128)(2,1)S(1)}, u32[]{:S(2)}, u32[]{:S(2)}) %collective-permute-start.38) | collective-permute-done | bytes 270368 | tf_op jit(solution)/shard_map/ppermute | solution.py:705
  363.1 3.5 collective-permute-done.47
  366.7 11.5 %collective-permute-done.43 = bf16[32,4224]{1,0:T(8,128)(2,1)S(1)} collective-permute-done((bf16[32,4224]{1,0:T(8,128)(2,1)S(1)}, bf16[32,4224]{1,0:T(8,128)(2,1)S(1)}, u32[]{:S(2)}, u32[]{:S(2)}) %collective-permute-start.43) | collective-permute-done | bytes 270368 | tf_op jit(solution)/shard_map/ppermute | solution.py:705
  378.5 2.3 collective-permute-start.48
  382.5 8.0 %collective-permute-done.44 = bf16[2,32,4224]{2,1,0:T(8,128)(2,1)S(1)} collective-permute-done((bf16[2,32,4224]{2,1,0:T(8,128)(2,1)S(1)}, bf16[2,32,4224]{2,1,0:T(8,128)(2,1)S(1)}, u32[]{:S(2)}, u32[]{:S(2)}) %collective-permute-start.44) | collective-permute-done | bytes 540704 | tf_op jit(solution)/shard_map/ppermute | solution.py:705
  390.8 2.6 collective-permute-start.45
  398.3 2.9 shard_map.253
  401.8 5.9 %shard_map.252 = (f32[1024,1024]{1,0:T(8,128)}, f32[1024,1024]{1,0:T(8,128)}) custom-call(bf16[8,256,1024]{2,1,0:T(8,128)(2,1)} %bitcast.146), custom_call_target="tpu_custom_call" | custom-call | tf_op jit(solution)/shard_map/pallas_call | solution.py:687
  (235 shorter events, 81.4 us)
Async XLA Ops:
  7.2 81.3 %all-gather.7.cloned.1.call-start = ((), (), s32[]{:S(2)}) async-start(), calls=%async_computation | async-start | bytes 2621440 | tf_op jit(solution)/shard_map/all_gather | solution.py:878
  10.1 152.6 %all-gather.9.cloned.1.call-start = ((), (), s32[]{:S(2)}) async-start(), calls=%async_computation.1 | async-start | bytes 7864320 | tf_op jit(solution)/shard_map/all_gather | solution.py:933
  10.3 11.7 %collective-permute-start = (bf16[128,1280]{1,0:T(8,128)(2,1)S(1)}, bf16[128,1280]{1,0:T(8,128)(2,1)S(1)}, u32[]{:S(2)}, u32[]{:S(2)}) collective-permute-start(bf16[128,1280]{1,0:T(8,128)(2,1)S(1)} %get-tuple-element.296.refs_0_), channel_id=1, source_target_pairs={{0,1},{1,2},{2,3},{3,0},{4,5},{5,6},{6,7},{7,4},{8,9},{9,10},{10,1... | collective-permute-start | bytes 983048 | tf_op jit(solution)/shard_map/ppermute | solution.py:798
  11.7 24.6 %collective-permute-start.1 = (bf16[128,1280]{1,0:T(8,128)(2,1)S(1)}, bf16[128,1280]{1,0:T(8,128)(2,1)S(1)}, u32[]{:S(2)}, u32[]{:S(2)}) collective-permute-start(bf16[128,1280]{1,0:T(8,128)(2,1)S(1)} %get-tuple-element.295.refs_1_), channel_id=1, source_target_pairs={{0,3},{1,0},{2,1},{3,2},{4,7},{5,4},{6,5},{7,6},{8,11},{9,8},{10,9... | collective-permute-start | bytes 983048 | tf_op jit(solution)/shard_map/ppermute | solution.py:799
  11.9 24.5 %collective-permute-start.2 = (bf16[256,1024]{1,0:T(8,128)(2,1)}, bf16[256,1024]{1,0:T(8,128)(2,1)}, u32[]{:S(2)}, u32[]{:S(2)}) collective-permute-start(bf16[256,1024]{1,0:T(8,128)(2,1)} %cotangent_ref.1), channel_id=1, source_target_pairs={{0,4},{4,0},{1,5},{5,1},{2,6},{6,2},{3,7},{7,3},{8,12},{12,8},{9,1... | collective-permute-start | bytes 1572872 | tf_op jit(solution)/shard_map/ppermute | solution.py:705
  36.3 29.8 %collective-permute-start.3 = (bf16[128,1280]{1,0:T(8,128)(2,1)S(1)}, bf16[128,1280]{1,0:T(8,128)(2,1)S(1)}, u32[]{:S(2)}, u32[]{:S(2)}) collective-permute-start(bf16[128,1280]{1,0:T(8,128)(2,1)S(1)} %collective-permute-done.refs_2_), channel_id=1, source_target_pairs={{0,1},{1,2},{2,3},{3,0},{4,5},{5,6},{6,7},{7,4},{8,9},{9,10},{10,1... | collective-permute-start | bytes 983048 | tf_op jit(solution)/shard_map/ppermute | solution.py:798
  36.3 30.9 %collective-permute-start.4 = (bf16[128,1280]{1,0:T(8,128)(2,1)S(1)}, bf16[128,1280]{1,0:T(8,128)(2,1)S(1)}, u32[]{:S(2)}, u32[]{:S(2)}) collective-permute-start(bf16[128,1280]{1,0:T(8,128)(2,1)S(1)} %collective-permute-done.1.refs_1_), channel_id=1, source_target_pairs={{0,3},{1,0},{2,1},{3,2},{4,7},{5,4},{6,5},{7,6},{8,11},{9,8},{10,9... | collective-permute-start | bytes 983048 | tf_op jit(solution)/shard_map/ppermute | solution.py:799
  67.2 14.0 %collective-permute-start.5 = (bf16[128,1280]{1,0:T(8,128)(2,1)S(1)}, bf16[128,1280]{1,0:T(8,128)(2,1)S(1)}, u32[]{:S(2)}, u32[]{:S(2)}) collective-permute-start(bf16[128,1280]{1,0:T(8,128)(2,1)S(1)} %collective-permute-done.3.refs_0_), channel_id=1, source_target_pairs={{0,1},{1,2},{2,3},{3,0},{4,5},{5,6},{6,7},{7,4},{8,9},{9,10},{10,1... | collective-permute-start | bytes 983048 | tf_op jit(solution)/shard_map/ppermute | solution.py:798
  70.3 18.2 %collective-permute-start.6 = (bf16[128,1280]{1,0:T(8,128)(2,1)S(1)}, bf16[128,1280]{1,0:T(8,128)(2,1)S(1)}, u32[]{:S(2)}, u32[]{:S(2)}) collective-permute-start(bf16[128,1280]{1,0:T(8,128)(2,1)S(1)} %collective-permute-done.4.refs_1_), channel_id=1, source_target_pairs={{0,3},{1,0},{2,1},{3,2},{4,7},{5,4},{6,5},{7,6},{8,11},{9,8},{10,9... | collective-permute-start | bytes 983048 | tf_op jit(solution)/shard_map/ppermute | solution.py:799
  91.3 310.5 %all-gather.11.cloned.1.call-start = ((), (), s32[]{:S(2)}) async-start(), calls=%async_computation.2 | async-start | bytes 4718592 | tf_op jit(solution)/shard_map/all_gather | solution.py:1073
  104.1 9.0 %collective-permute-start.7 = (bf16[128,1024]{1,0:T(8,128)(2,1)S(1)}, bf16[128,1024]{1,0:T(8,128)(2,1)S(1)}, u32[]{:S(2)}, u32[]{:S(2)}) collective-permute-start(bf16[128,1024]{1,0:T(8,128)(2,1)S(1)} %slice.154), channel_id=1, source_target_pairs={{0,1},{1,2},{2,3},{3,0},{4,5},{5,6},{6,7},{7,4},{8,9},{9,10},{10,1... | collective-permute-start | bytes 786440 | tf_op jit(solution)/shard_map/ppermute | solution.py:812
  108.9 8.6 %collective-permute-start.8 = (bf16[128,1024]{1,0:T(8,128)(2,1)S(1)}, bf16[128,1024]{1,0:T(8,128)(2,1)S(1)}, u32[]{:S(2)}, u32[]{:S(2)}) collective-permute-start(bf16[128,1024]{1,0:T(8,128)(2,1)S(1)} %slice.155), channel_id=1, source_target_pairs={{0,3},{1,0},{2,1},{3,2},{4,7},{5,4},{6,5},{7,6},{8,11},{9,8},{10,9... | collective-permute-start | bytes 786440 | tf_op jit(solution)/shard_map/ppermute | solution.py:813
  117.7 7.5 %collective-permute-start.9 = (bf16[128,1024]{1,0:T(8,128)(2,1)S(1)}, bf16[128,1024]{1,0:T(8,128)(2,1)S(1)}, u32[]{:S(2)}, u32[]{:S(2)}) collective-permute-start(bf16[128,1024]{1,0:T(8,128)(2,1)S(1)} %get-tuple-element.306), channel_id=1, source_target_pairs={{0,1},{1,2},{2,3},{3,0},{4,5},{5,6},{6,7},{7,4},{8,9},{9,10},{10,1... | collective-permute-start | bytes 786440 | tf_op jit(solution)/shard_map/ppermute | solution.py:812
  118.6 14.9 %collective-permute-start.10 = (bf16[128,1024]{1,0:T(8,128)(2,1)S(1)}, bf16[128,1024]{1,0:T(8,128)(2,1)S(1)}, u32[]{:S(2)}, u32[]{:S(2)}) collective-permute-start(bf16[128,1024]{1,0:T(8,128)(2,1)S(1)} %get-tuple-element.305), channel_id=1, source_target_pairs={{0,3},{1,0},{2,1},{3,2},{4,7},{5,4},{6,5},{7,6},{8,11},{9,8},{10,9... | collective-permute-start | bytes 786440 | tf_op jit(solution)/shard_map/ppermute | solution.py:813
  133.6 7.5 %collective-permute-start.11 = (bf16[128,1024]{1,0:T(8,128)(2,1)S(1)}, bf16[128,1024]{1,0:T(8,128)(2,1)S(1)}, u32[]{:S(2)}, u32[]{:S(2)}) collective-permute-start(bf16[128,1024]{1,0:T(8,128)(2,1)S(1)} %add_convert_fusion.13), channel_id=1, source_target_pairs={{0,1},{1,2},{2,3},{3,0},{4,5},{5,6},{6,7},{7,4},{8,9},{9,10},{10,1... | collective-permute-start | bytes 786440 | tf_op jit(solution)/shard_map/ppermute | solution.py:812
  133.8 12.5 %collective-permute-start.12 = (bf16[128,1024]{1,0:T(8,128)(2,1)S(1)}, bf16[128,1024]{1,0:T(8,128)(2,1)S(1)}, u32[]{:S(2)}, u32[]{:S(2)}) collective-permute-start(bf16[128,1024]{1,0:T(8,128)(2,1)S(1)} %add_convert_fusion.12), channel_id=1, source_target_pairs={{0,3},{1,0},{2,1},{3,2},{4,7},{5,4},{6,5},{7,6},{8,11},{9,8},{10,9... | collective-permute-start | bytes 786440 | tf_op jit(solution)/shard_map/ppermute | solution.py:813
  183.1 52.0 %collective-permute-start.22 = (bf16[2,4,256,512]{3,2,1,0:T(8,128)(2,1)}, bf16[2,4,256,512]{3,2,1,0:T(8,128)(2,1)}, u32[]{:S(2)}, u32[]{:S(2)}) collective-permute-start(bf16[2,4,256,512]{3,2,1,0:T(8,128)(2,1)} %get-tuple-element.203), channel_id=1, source_target_pairs={{0,8},{8,0},{16,24},{24,16},{1,9},{9,1},{17,25},{25,17},{2,10},{10... | collective-permute-start | bytes 6291464 | tf_op jit(solution)/shard_map/ppermute | solution.py:705
  183.5 51.7 %collective-permute-start.23 = (bf16[2,4,256,512]{3,2,1,0:T(8,128)(2,1)}, bf16[2,4,256,512]{3,2,1,0:T(8,128)(2,1)}, u32[]{:S(2)}, u32[]{:S(2)}) collective-permute-start(bf16[2,4,256,512]{3,2,1,0:T(8,128)(2,1)} %get-tuple-element.204), channel_id=1, source_target_pairs={{0,16},{8,24},{16,0},{24,8},{1,17},{9,25},{17,1},{25,9},{2,18},{10... | collective-permute-start | bytes 6291464 | tf_op jit(solution)/shard_map/ppermute | solution.py:705
  192.2 7.7 %collective-permute-start.16 = (bf16[128,1024]{1,0:T(8,128)(2,1)S(1)}, bf16[128,1024]{1,0:T(8,128)(2,1)S(1)}, u32[]{:S(2)}, u32[]{:S(2)}) collective-permute-start(bf16[128,1024]{1,0:T(8,128)(2,1)S(1)} %get-tuple-element.302.refs_0_.refs_14_), channel_id=1, source_target_pairs={{0,1},{1,2},{2,3},{3,0},{4,5},{5,6},{6,7},{7,4},{8,9},{9,10},{10,1... | collective-permute-start | bytes 786440 | tf_op jit(solution)/shard_map/ppermute | solution.py:798
  193.5 12.0 %collective-permute-start.17 = (bf16[128,1024]{1,0:T(8,128)(2,1)S(1)}, bf16[128,1024]{1,0:T(8,128)(2,1)S(1)}, u32[]{:S(2)}, u32[]{:S(2)}) collective-permute-start(bf16[128,1024]{1,0:T(8,128)(2,1)S(1)} %get-tuple-element.301.refs_1_.refs_18_), channel_id=1, source_target_pairs={{0,3},{1,0},{2,1},{3,2},{4,7},{5,4},{6,5},{7,6},{8,11},{9,8},{10,9... | collective-permute-start | bytes 786440 | tf_op jit(solution)/shard_map/ppermute | solution.py:799
  205.5 8.7 %collective-permute-start.18 = (bf16[128,1024]{1,0:T(8,128)(2,1)S(1)}, bf16[128,1024]{1,0:T(8,128)(2,1)S(1)}, u32[]{:S(2)}, u32[]{:S(2)}) collective-permute-start(bf16[128,1024]{1,0:T(8,128)(2,1)S(1)} %collective-permute-done.16.refs_2_.refs_17_), channel_id=1, source_target_pairs={{0,1},{1,2},{2,3},{3,0},{4,5},{5,6},{6,7},{7,4},{8,9},{9,10},{10,1... | collective-permute-start | bytes 786440 | tf_op jit(solution)/shard_map/ppermute | solution.py:798
  206.6 12.8 %collective-permute-start.19 = (bf16[128,1024]{1,0:T(8,128)(2,1)S(1)}, bf16[128,1024]{1,0:T(8,128)(2,1)S(1)}, u32[]{:S(2)}, u32[]{:S(2)}) collective-permute-start(bf16[128,1024]{1,0:T(8,128)(2,1)S(1)} %collective-permute-done.17.refs_1_.refs_19_), channel_id=1, source_target_pairs={{0,3},{1,0},{2,1},{3,2},{4,7},{5,4},{6,5},{7,6},{8,11},{9,8},{10,9... | collective-permute-start | bytes 786440 | tf_op jit(solution)/shard_map/ppermute | solution.py:799
  219.4 8.8 %collective-permute-start.20 = (bf16[128,1024]{1,0:T(8,128)(2,1)S(1)}, bf16[128,1024]{1,0:T(8,128)(2,1)S(1)}, u32[]{:S(2)}, u32[]{:S(2)}) collective-permute-start(bf16[128,1024]{1,0:T(8,128)(2,1)S(1)} %collective-permute-done.18.refs_0_.refs_16_), channel_id=1, source_target_pairs={{0,1},{1,2},{2,3},{3,0},{4,5},{5,6},{6,7},{7,4},{8,9},{9,10},{10,1... | collective-permute-start | bytes 786440 | tf_op jit(solution)/shard_map/ppermute | solution.py:798
  221.4 13.7 %collective-permute-start.21 = (bf16[128,1024]{1,0:T(8,128)(2,1)S(1)}, bf16[128,1024]{1,0:T(8,128)(2,1)S(1)}, u32[]{:S(2)}, u32[]{:S(2)}) collective-permute-start(bf16[128,1024]{1,0:T(8,128)(2,1)S(1)} %collective-permute-done.19.refs_1_.refs_20_), channel_id=1, source_target_pairs={{0,3},{1,0},{2,1},{3,2},{4,7},{5,4},{6,5},{7,6},{8,11},{9,8},{10,9... | collective-permute-start | bytes 786440 | tf_op jit(solution)/shard_map/ppermute | solution.py:799
  241.7 33.0 %collective-permute-start.24 = (bf16[4,256,512]{2,1,0:T(8,128)(2,1)}, bf16[4,256,512]{2,1,0:T(8,128)(2,1)}, u32[]{:S(2)}, u32[]{:S(2)}) collective-permute-start(bf16[4,256,512]{2,1,0:T(8,128)(2,1)} %dynamic-slice_bitcast_fusion.1), channel_id=1, source_target_pairs={{0,16},{8,24},{16,0},{24,8},{1,17},{9,25},{17,1},{25,9},{2,18},{10... | collective-permute-start | bytes 3145736 | tf_op jit(solution)/shard_map/ppermute | solution.py:705
  242.9 31.8 %collective-permute-start.25 = (bf16[4,256,512]{2,1,0:T(8,128)(2,1)}, bf16[4,256,512]{2,1,0:T(8,128)(2,1)}, u32[]{:S(2)}, u32[]{:S(2)}) collective-permute-start(bf16[4,256,512]{2,1,0:T(8,128)(2,1)} %dynamic-slice_bitcast_fusion), channel_id=1, source_target_pairs={{0,8},{8,0},{16,24},{24,16},{1,9},{9,1},{17,25},{25,17},{2,10},{10... | collective-permute-start | bytes 3145736 | tf_op jit(solution)/shard_map/ppermute | solution.py:705
  245.3 61.5 %collective-permute-start.14 = (f32[256,1024]{1,0:T(8,128)}, f32[256,1024]{1,0:T(8,128)S(1)}, u32[]{:S(2)}, u32[]{:S(2)}) collective-permute-start(f32[256,1024]{1,0:T(8,128)} %copy-done.19), channel_id=1, source_target_pairs={{0,4},{4,0},{1,5},{5,1},{2,6},{6,2},{3,7},{7,3},{8,12},{12,8},{9,1... | collective-permute-start | bytes 3145736 | tf_op jit(solution)/shard_map/ppermute | solution.py:705
  274.7 7.1 %collective-permute-start.26 = (bf16[128,4224]{1,0:T(8,128)(2,1)S(1)}, bf16[128,4224]{1,0:T(8,128)(2,1)S(1)}, u32[]{:S(2)}, u32[]{:S(2)}) collective-permute-start(bf16[128,4224]{1,0:T(8,128)(2,1)S(1)} %get-tuple-element.242), channel_id=1, source_target_pairs={{0,4},{4,0},{1,5},{5,1},{2,6},{6,2},{3,7},{7,3},{8,12},{12,8},{9,1... | collective-permute-start | bytes 3244040 | tf_op jit(solution)/shard_map/ppermute | solution.py:705
  278.6 36.0 %collective-permute-start.32 = (bf16[256,1024]{1,0:T(8,128)(2,1)S(1)}, bf16[256,1024]{1,0:T(8,128)(2,1)S(1)}, u32[]{:S(2)}, u32[]{:S(2)}) collective-permute-start(bf16[256,1024]{1,0:T(8,128)(2,1)S(1)} %pad_maximum_fusion.8), channel_id=1, source_target_pairs={{0,1},{1,2},{2,3},{3,0},{4,5},{5,6},{6,7},{7,4},{8,9},{9,10},{10,1... | collective-permute-start | bytes 1572872 | tf_op jit(solution)/shard_map/ppermute | solution.py:1053
  278.7 35.9 %collective-permute-start.33 = (bf16[256,1024]{1,0:T(8,128)(2,1)S(1)}, bf16[256,1024]{1,0:T(8,128)(2,1)S(1)}, u32[]{:S(2)}, u32[]{:S(2)}) collective-permute-start(bf16[256,1024]{1,0:T(8,128)(2,1)S(1)} %pad_maximum_fusion.9), channel_id=1, source_target_pairs={{0,2},{1,3},{2,0},{3,1},{4,6},{5,7},{6,4},{7,5},{8,10},{9,11},{10,... | collective-permute-start | bytes 1572872 | tf_op jit(solution)/shard_map/ppermute | solution.py:1053
  279.2 44.7 %collective-permute-start.34 = (bf16[256,1024]{1,0:T(8,128)(2,1)S(1)}, bf16[256,1024]{1,0:T(8,128)(2,1)S(1)}, u32[]{:S(2)}, u32[]{:S(2)}) collective-permute-start(bf16[256,1024]{1,0:T(8,128)(2,1)S(1)} %pad_maximum_fusion.10), channel_id=1, source_target_pairs={{0,3},{1,0},{2,1},{3,2},{4,7},{5,4},{6,5},{7,6},{8,11},{9,8},{10,9... | collective-permute-start | bytes 1572872 | tf_op jit(solution)/shard_map/ppermute | solution.py:1053
  281.8 12.6 %collective-permute-start.30 = (bf16[2,32,4096]{2,1,0:T(8,128)(2,1)S(1)}, bf16[2,32,4096]{2,1,0:T(8,128)(2,1)S(1)}, u32[]{:S(2)}, u32[]{:S(2)}) collective-permute-start(bf16[2,32,4096]{2,1,0:T(8,128)(2,1)S(1)} %dynamic-slice_bitcast_fusion.3), channel_id=1, source_target_pairs={{0,16},{8,24},{16,0},{24,8},{1,17},{9,25},{17,1},{25,9},{2,18},{10... | collective-permute-start | bytes 1572872 | tf_op jit(solution)/shard_map/ppermute | solution.py:705
  294.4 12.0 %collective-permute-start.27 = (bf16[2,32,4224]{2,1,0:T(8,128)(2,1)S(1)}, bf16[2,32,4224]{2,1,0:T(8,128)(2,1)S(1)}, u32[]{:S(2)}, u32[]{:S(2)}) collective-permute-start(bf16[2,32,4224]{2,1,0:T(8,128)(2,1)S(1)} %dynamic-slice_bitcast_fusion.2), channel_id=1, source_target_pairs={{0,8},{8,0},{16,24},{24,16},{1,9},{9,1},{17,25},{25,17},{2,10},{10... | collective-permute-start | bytes 1622024 | tf_op jit(solution)/shard_map/ppermute | solution.py:705
  306.4 17.6 %collective-permute-start.31 = (bf16[32,4096]{1,0:T(8,128)(2,1)S(1)}, bf16[32,4096]{1,0:T(8,128)(2,1)S(1)}, u32[]{:S(2)}, u32[]{:S(2)}) collective-permute-start(bf16[32,4096]{1,0:T(8,128)(2,1)S(1)} %dynamic-slice_bitcast_fusion.5), channel_id=1, source_target_pairs={{0,8},{8,0},{16,24},{24,16},{1,9},{9,1},{17,25},{25,17},{2,10},{10... | collective-permute-start | bytes 786440 | tf_op jit(solution)/shard_map/ppermute | solution.py:705
  306.8 17.1 %collective-permute-start.28 = (bf16[32,4224]{1,0:T(8,128)(2,1)S(1)}, bf16[32,4224]{1,0:T(8,128)(2,1)S(1)}, u32[]{:S(2)}, u32[]{:S(2)}) collective-permute-start(bf16[32,4224]{1,0:T(8,128)(2,1)S(1)} %dynamic-slice_bitcast_fusion.4), channel_id=1, source_target_pairs={{0,16},{8,24},{16,0},{24,8},{1,17},{9,25},{17,1},{25,9},{2,18},{10... | collective-permute-start | bytes 811016 | tf_op jit(solution)/shard_map/ppermute | solution.py:705
  324.9 34.8 %collective-permute-start.35 = (bf16[128,1024]{1,0:T(8,128)(2,1)}, bf16[128,1024]{1,0:T(8,128)(2,1)}, u32[]{:S(2)}, u32[]{:S(2)}) collective-permute-start(bf16[128,1024]{1,0:T(8,128)(2,1)} %get-tuple-element.275), channel_id=1, source_target_pairs={{0,1},{1,2},{2,3},{3,0},{4,5},{5,6},{6,7},{7,4},{8,9},{9,10},{10,1... | collective-permute-start | bytes 786440 | tf_op jit(solution)/shard_map/ppermute | solution.py:812
  327.9 31.7 %collective-permute-start.36 = (bf16[128,1024]{1,0:T(8,128)(2,1)}, bf16[128,1024]{1,0:T(8,128)(2,1)}, u32[]{:S(2)}, u32[]{:S(2)}) collective-permute-start(bf16[128,1024]{1,0:T(8,128)(2,1)} %get-tuple-element.274), channel_id=1, source_target_pairs={{0,3},{1,0},{2,1},{3,2},{4,7},{5,4},{6,5},{7,6},{8,11},{9,8},{10,9... | collective-permute-start | bytes 786440 | tf_op jit(solution)/shard_map/ppermute | solution.py:813
  328.2 17.4 %collective-permute-start.37 = (bf16[32,4224]{1,0:T(8,128)(2,1)S(1)}, bf16[32,4224]{1,0:T(8,128)(2,1)S(1)}, u32[]{:S(2)}, u32[]{:S(2)}) collective-permute-start(bf16[32,4224]{1,0:T(8,128)(2,1)S(1)} %fusion.17), channel_id=1, source_target_pairs={{0,1},{1,0},{2,3},{3,2},{4,5},{5,4},{6,7},{7,6},{8,9},{9,8},{10,11... | collective-permute-start | bytes 811016 | tf_op jit(solution)/shard_map/ppermute | solution.py:705
  345.6 13.7 %collective-permute-start.38 = (bf16[32,4224]{1,0:T(8,128)(2,1)S(1)}, bf16[32,4224]{1,0:T(8,128)(2,1)S(1)}, u32[]{:S(2)}, u32[]{:S(2)}) collective-permute-start(bf16[32,4224]{1,0:T(8,128)(2,1)S(1)} %add_convert_fusion.7), channel_id=1, source_target_pairs={{0,2},{1,3},{2,0},{3,1},{4,6},{5,7},{6,4},{7,5},{8,10},{9,11},{10,... | collective-permute-start | bytes 811016 | tf_op jit(solution)/shard_map/ppermute | solution.py:705
  348.5 18.1 %collective-permute-start.47 = (bf16[2,32,4096]{2,1,0:T(8,128)(2,1)S(1)}, bf16[2,32,4096]{2,1,0:T(8,128)(2,1)S(1)}, u32[]{:S(2)}, u32[]{:S(2)}) collective-permute-start(bf16[2,32,4096]{2,1,0:T(8,128)(2,1)S(1)} %pad_maximum_fusion.11), channel_id=1, source_target_pairs={{0,16},{8,24},{16,0},{24,8},{1,17},{9,25},{17,1},{25,9},{2,18},{10... | collective-permute-start | bytes 1572872 | tf_op jit(solution)/shard_map/ppermute | solution.py:705
  359.4 18.8 %collective-permute-start.43 = (bf16[32,4224]{1,0:T(8,128)(2,1)S(1)}, bf16[32,4224]{1,0:T(8,128)(2,1)S(1)}, u32[]{:S(2)}, u32[]{:S(2)}) collective-permute-start(bf16[32,4224]{1,0:T(8,128)(2,1)S(1)} %add_convert_fusion.6), channel_id=1, source_target_pairs={{0,16},{8,24},{16,0},{24,8},{1,17},{9,25},{17,1},{25,9},{2,18},{10... | collective-permute-start | bytes 811016 | tf_op jit(solution)/shard_map/ppermute | solution.py:705
  360.9 19.9 %collective-permute-start.39 = (bf16[128,1024]{1,0:T(8,128)(2,1)S(1)}, bf16[128,1024]{1,0:T(8,128)(2,1)S(1)}, u32[]{:S(2)}, u32[]{:S(2)}) collective-permute-start(bf16[128,1024]{1,0:T(8,128)(2,1)S(1)} %get-tuple-element.273), channel_id=1, source_target_pairs={{0,1},{1,2},{2,3},{3,0},{4,5},{5,6},{6,7},{7,4},{8,9},{9,10},{10,1... | collective-permute-start | bytes 786440 | tf_op jit(solution)/shard_map/ppermute | solution.py:812
  363.1 17.7 %collective-permute-start.40 = (bf16[128,1024]{1,0:T(8,128)(2,1)S(1)}, bf16[128,1024]{1,0:T(8,128)(2,1)S(1)}, u32[]{:S(2)}, u32[]{:S(2)}) collective-permute-start(bf16[128,1024]{1,0:T(8,128)(2,1)S(1)} %get-tuple-element.272), channel_id=1, source_target_pairs={{0,3},{1,0},{2,1},{3,2},{4,7},{5,4},{6,5},{7,6},{8,11},{9,8},{10,9... | collective-permute-start | bytes 786440 | tf_op jit(solution)/shard_map/ppermute | solution.py:813
  378.3 12.2 %collective-permute-start.44 = (bf16[2,32,4224]{2,1,0:T(8,128)(2,1)S(1)}, bf16[2,32,4224]{2,1,0:T(8,128)(2,1)S(1)}, u32[]{:S(2)}, u32[]{:S(2)}) collective-permute-start(bf16[2,32,4224]{2,1,0:T(8,128)(2,1)S(1)} %pad_maximum_fusion.6), channel_id=1, source_target_pairs={{0,8},{8,0},{16,24},{24,16},{1,9},{9,1},{17,25},{25,17},{2,10},{10... | collective-permute-start | bytes 1622024 | tf_op jit(solution)/shard_map/ppermute | solution.py:705
  378.5 15.0 %collective-permute-start.48 = (bf16[128,4096]{1,0:T(8,128)(2,1)S(1)}, bf16[128,4096]{1,0:T(8,128)(2,1)S(1)}, u32[]{:S(2)}, u32[]{:S(2)}) collective-permute-start(bf16[128,4096]{1,0:T(8,128)(2,1)S(1)} %bitcast.142), channel_id=1, source_target_pairs={{0,4},{4,0},{1,5},{5,1},{2,6},{6,2},{3,7},{7,3},{8,12},{12,8},{9,1... | collective-permute-start | bytes 3145736 | tf_op jit(solution)/shard_map/ppermute | solution.py:705
  381.0 26.7 %collective-permute-start.41 = (bf16[128,1024]{1,0:T(8,128)(2,1)S(1)}, bf16[128,1024]{1,0:T(8,128)(2,1)S(1)}, u32[]{:S(2)}, u32[]{:S(2)}) collective-permute-start(bf16[128,1024]{1,0:T(8,128)(2,1)S(1)} %get-tuple-element.271), channel_id=1, source_target_pairs={{0,1},{1,2},{2,3},{3,0},{4,5},{5,6},{6,7},{7,4},{8,9},{9,10},{10,1... | collective-permute-start | bytes 786440 | tf_op jit(solution)/shard_map/ppermute | solution.py:812
  381.1 26.7 %collective-permute-start.42 = (bf16[128,1024]{1,0:T(8,128)(2,1)S(1)}, bf16[128,1024]{1,0:T(8,128)(2,1)}, u32[]{:S(2)}, u32[]{:S(2)}) collective-permute-start(bf16[128,1024]{1,0:T(8,128)(2,1)S(1)} %get-tuple-element.270), channel_id=1, source_target_pairs={{0,3},{1,0},{2,1},{3,2},{4,7},{5,4},{6,5},{7,6},{8,11},{9,8},{10,9... | collective-permute-start | bytes 786440 | tf_op jit(solution)/shard_map/ppermute | solution.py:813
  390.8 6.3 %collective-permute-start.45 = (bf16[128,4224]{1,0:T(8,128)(2,1)S(1)}, bf16[128,4224]{1,0:T(8,128)(2,1)S(1)}, u32[]{:S(2)}, u32[]{:S(2)}) collective-permute-start(bf16[128,4224]{1,0:T(8,128)(2,1)S(1)} %bitcast.141), channel_id=1, source_target_pairs={{0,4},{4,0},{1,5},{5,1},{2,6},{6,2},{3,7},{7,3},{8,12},{12,8},{9,1... | collective-permute-start | bytes 3244040 | tf_op jit(solution)/shard_map/ppermute | solution.py:705
  (43 other events, 608.2 us)
Sparse Core Ops, SparseCore 0:
  10.3 70.9 all-gather.6
  91.4 71.3 all-gather.8
  331.4 48.7 all-gather.10
